TPU v7x, 128 devices: a whole 4x4x4 slice. The times are simulated.
128 devices in a mesh: site: 128 (over x, z, y, core).
Axes of the slice: x: 4, y: 4, z: 4, core: 2. Of those that a mesh axis runs over, the one named last changes fastest.
Arguments:
- site_tensors: bfloat16 [128, 256, 8, 256], P('site'), may hold values from -1.5 to 1.5
- first_gates: bfloat16 [128, 64, 64], P('site'), may hold values from -0.75 to 0.75
- second_gates: bfloat16 [128, 64, 64], P('site'), may hold values from -0.75 to 0.75
- first_sketch: int32 [128, 2048, 256], P('site'), may hold values from -1 to 1
- second_sketch: int32 [128, 2048, 256], P('site'), may hold values from -1 to 1
Outputs:
- evolved: bfloat16 [128, 256, 8, 256], P('site')
All inputs are finite; a program needn't handle non-finite values.
Results may differ from a plain program's by a relative error of at most 0.018.
Values may be sent and summed in bfloat16 or wider, within the bound.
No kernel may reach another device: no remote copies, remote signals or barrier semaphores. Data moves between devices by JAX's collectives and lax.ppermute only.
A program may use at most 64 MiB of HBM per device.

v0:
```python
import jax
import jax.numpy as jnp
from jax import lax
from jax.sharding import PartitionSpec as P


def from_behind(array, axis, by):
    size = lax.axis_size(axis)
    pairs = [(i, i + by) for i in range(size) if 0 <= i + by < size]
    return lax.ppermute(array, axis, pairs)


def contract(row_block, partner, gate_matrix):
    bond_dim = partner.shape[0]
    levels = partner.shape[1]
    rows_count = row_block.shape[0]
    two_site = jnp.dot(
        row_block.reshape(rows_count * levels, bond_dim),
        partner.reshape(bond_dim, levels * bond_dim),
        preferred_element_type=jnp.float32,
    ).astype(jnp.bfloat16)
    two_site = two_site.reshape(rows_count, levels * levels, bond_dim)
    gated_pair = jnp.einsum(
        "xy,ayc->axc", gate_matrix, two_site, preferred_element_type=jnp.float32
    ).astype(jnp.bfloat16)
    return gated_pair.reshape(rows_count * levels, levels * bond_dim)


def basis_from(sampled, gram_matrix, left_scale):
    factor_lower = jnp.linalg.cholesky(gram_matrix)
    basis_rows = jax.scipy.linalg.solve_triangular(factor_lower, sampled.T, lower=True)
    return (basis_rows.T * left_scale).astype(jnp.bfloat16)


def apply_layer(tensor, gate_matrix, sketch_whole, parity):
    bond_dim = tensor.shape[0]
    levels = tensor.shape[1]
    left_scale = levels**0.5 * bond_dim**0.25
    right_scale = (levels * bond_dim) ** (-0.5)
    devices = lax.axis_size("site")
    position = lax.axis_index("site")
    is_left = ((position - parity) % 2 == 0) & (position + 1 < devices)
    is_right = ((position - 1 - parity) % 2 == 0) & (position >= 1)
    sketch_values = sketch_whole.astype(jnp.bfloat16)
    partner = from_behind(tensor, "site", -1)
    half_rows = bond_dim // 2
    lower_block, gate_there, sketch_there = from_behind(
        (tensor[half_rows:], gate_matrix, sketch_values), "site", 1
    )
    row_block = jnp.where(is_left, tensor[:half_rows], lower_block)
    partner_used = jnp.where(is_left, partner, tensor)
    gate_used = jnp.where(is_left, gate_matrix, gate_there)
    sketch_used = jnp.where(is_left, sketch_values, sketch_there)
    matrix = contract(row_block, partner_used, gate_used)
    sampled = jnp.dot(matrix, sketch_used, preferred_element_type=jnp.float32)
    gram_part = jnp.dot(sampled.T, sampled)
    from_right = from_behind(gram_part.astype(jnp.bfloat16), "site", -1).astype(gram_part.dtype)
    from_left = from_behind(gram_part.astype(jnp.bfloat16), "site", 1).astype(gram_part.dtype)
    gram_matrix = gram_part + jnp.where(is_left, from_right, from_left)
    left_rows = basis_from(sampled, gram_matrix, left_scale)
    partial_value = lax.dot_general(
        left_rows, matrix, (((0,), (0,)), ((), ())), preferred_element_type=jnp.float32
    )
    upper_rows = from_behind(left_rows, "site", -1)
    new_left = jnp.concatenate([left_rows, upper_rows], axis=0).reshape(bond_dim, levels, bond_dim)
    arrived = from_behind(partial_value.astype(jnp.bfloat16), "site", 1).astype(partial_value.dtype)
    new_right = (
        ((partial_value + arrived) * right_scale)
        .astype(jnp.bfloat16)
        .reshape(bond_dim, levels, bond_dim)
    )
    return jnp.where(is_left, new_left, jnp.where(is_right, new_right, tensor))


def per_device(site_tensors, first_gates, second_gates, first_sketch, second_sketch):
    tensor = site_tensors[0]
    tensor = apply_layer(tensor, first_gates[0], first_sketch[0], 0)
    tensor = apply_layer(tensor, second_gates[0], second_sketch[0], 1)
    return tensor[None]


def solution(mesh):
    in_specs = (
        P("site", None, None, None),
        P("site", None, None),
        P("site", None, None),
        P("site", None, None),
        P("site", None, None),
    )
    out_specs = P("site", None, None, None)
    return jax.shard_map(
        per_device, mesh=mesh, in_specs=in_specs, out_specs=out_specs, check_vma=False
    )
```

profile of v0, /device:TPU:6, one launch (start us, length us, event | category | flops | bytes accessed | tf_op | source)
XLA Modules:
  0.0 324.8 jit_solution(3431451716770381790)
XLA Ops:
  0.0 8.2 %collective-permute-start.1 = (bf16[256,8,256]{2,1,0:T(8,128)(2,1)}, bf16[256,8,256]{2,1,0:T(8,128)(2,1)}, u32[]{:S(2)}, u32[]{:S(2)}) collective-permute-start(bf16[256,8,256]{2,1,0:T(8,128)(2,1)} %bitcast.149), channel_id=1, source_target_pairs={{1,0},{2,1},{3,2},{4,3},{5,4},{6,5},{7,6},{8,7},{9,8},{10,9},{11,1... | collective-permute-start | bytes 3145736 | tf_op jit(solution)/shard_map/ppermute | solution.py:10
  9.3 1.9 collective-permute-start
  11.3 1.9 collective-permute-start.2
  14.9 1.9 collective-permute-start.3
  16.9 4.0 %collective-permute-done.1 = bf16[256,8,256]{2,1,0:T(8,128)(2,1)} collective-permute-done((bf16[256,8,256]{2,1,0:T(8,128)(2,1)}, bf16[256,8,256]{2,1,0:T(8,128)(2,1)}, u32[]{:S(2)}, u32[]{:S(2)}) %collective-permute-start.1) | collective-permute-done | bytes 1048608 | tf_op jit(solution)/shard_map/ppermute | solution.py:10
  24.0 3.3 %convolution_convert_fusion.1 = bf16[1024,2048]{1,0:T(8,128)(2,1)} fusion(bf16[256,2048]{1,0:T(8,128)(2,1)S(1)} %bitcast.156, bf16[128,8,256]{2,1,0:T(8,128)(2,1)S(1)} %collective-permute-done, bf16[1,256,8,256]{3,2,1,0:T(8,128)(2,1)S(1)} %copy-done, pred[]{:T(512)S(6)} %and.30), kind=kOutput, calls=%fused_computation.7 | convolution fusion | flops 1076101120 | bytes 6291457 | tf_op jit(solution)/shard_map/dot_general | solution.py:17
  27.3 7.4 %reshape.65 = bf16[128,64,256]{2,1,0:T(8,128)(2,1)} reshape(bf16[1024,2048]{1,0:T(8,128)(2,1)} %convolution_convert_fusion.1) | data formatting | bytes 8388608 | tf_op jit(solution)/shard_map/reshape | solution.py:22
  34.7 5.4 %convert_bitcast_fusion.1 = bf16[128,64,256]{2,1,0:T(8,128)(2,1)} fusion(bf16[128,64,256]{2,1,0:T(8,128)(2,1)} %reshape.65, bf16[64,64]{1,0:T(8,128)(2,1)S(1)} %collective-permute-done.2, pred[]{:T(512)S(6)} %and.30, bf16[1,64,64]{2,1,0:T(8,128)(2,1)S(1)} %copy-done.9), kind=kOutput, calls=%fused_computation.5 | convolution fusion | flops 270536704 | bytes 8404993 | tf_op jit(solution)/shard_map/xy,ayc->axc/dot_general | solution.py:23
  40.2 7.4 %reshape.66 = bf16[1024,2048]{1,0:T(8,128)(2,1)} reshape(bf16[128,64,256]{2,1,0:T(8,128)(2,1)} %convert_bitcast_fusion.1) | data formatting | bytes 8388608 | tf_op jit(solution)/shard_map/reshape | solution.py:26
  47.6 3.4 %fusion.8 = f32[1024,256]{1,0:T(8,128)S(1)} fusion(bf16[1024,2048]{1,0:T(8,128)(2,1)} %reshape.66, bf16[2048,256]{1,0:T(8,128)(2,1)S(1)} %convert_bitcast_fusion.3, bf16[2048,256]{1,0:T(8,128)(2,1)} %collective-permute-done.3, pred[]{:T(512)S(6)} %and.30), kind=kOutput, calls=%fused_computation.27 | convolution fusion | flops 1074266112 | bytes 7340033 | tf_op jit(solution)/shard_map/dot_general | solution.py:55
  51.4 5.6 %collective-permute-start.4 = (bf16[256,256]{0,1:T(8,128)(2,1)S(1)}, bf16[256,256]{0,1:T(8,128)(2,1)S(1)}, u32[]{:S(2)}, u32[]{:S(2)}) collective-permute-start(bf16[256,256]{0,1:T(8,128)(2,1)S(1)} %get-tuple-element.51), channel_id=1, source_target_pairs={{1,0},{2,1},{3,2},{4,3},{5,4},{6,5},{7,6},{8,7},{9,8},{10,9},{11,1... | collective-permute-start | bytes 393224 | tf_op jit(solution)/shard_map/ppermute | solution.py:10
  57.0 2.1 collective-permute-start.5
  59.5 8.0 %collective-permute-done.5 = bf16[256,256]{0,1:T(8,128)(2,1)S(1)} collective-permute-done((bf16[256,256]{0,1:T(8,128)(2,1)S(1)}, bf16[256,256]{0,1:T(8,128)(2,1)S(1)}, u32[]{:S(2)}, u32[]{:S(2)}) %collective-permute-start.5) | collective-permute-done | bytes 131104 | tf_op jit(solution)/shard_map/ppermute | solution.py:10
  67.7 11.7 %cholesky.130 = f32[128,128]{1,0:T(8,128)S(1)} custom-call(f32[128,128]{1,0:T(8,128)S(1)} %cholesky.194), custom_call_target="Cholesky" | custom-call | tf_op jit(solution)/shard_map/jit(cholesky)/cholesky | solution.py:30
  79.5 9.8 %custom-call.13 = f32[1,128,128]{1,2,0:T(8,128)S(1)} custom-call(f32[1,128,128]{2,1,0:T(8,128)S(1)} %get-tuple-element.50), custom_call_target="InvertDiagBlocksLowerTriangular" | custom-call | tf_op jit(solution)/shard_map/jit(cholesky)/cholesky | solution.py:30
  89.8 11.7 %cholesky.147 = f32[128,128]{1,0:T(8,128)S(1)} custom-call(f32[128,128]{1,0:T(8,128)S(1)} %convolution_subtract_fusion.1), custom_call_target="Cholesky" | custom-call | tf_op jit(solution)/shard_map/jit(cholesky)/cholesky | solution.py:30
  103.6 4.2 %while.4 = (s32[]{:T(128)}, f32[256,256]{1,0:T(8,128)S(1)}, s32[2,2]{1,0:T(2,128)S(1)}, f32[2,128,128]{2,1,0:T(8,128)S(1)}, s32[]{:T(128)}) while((s32[]{:T(128)}, f32[256,256]{1,0:T(8,128)S(1)}, s32[2,2]{1,0:T(2,128)S(1)}, f32[2,128,128]{2,1,0:T(8,128)S(1)}, s32[]{:T(128)}) %tuple.47), condition=%wide.while_cond, body=%wide.while_body.sunk | while | flops 2 | bytes 131181 | solution.py:31
  107.8 19.7 %custom-call.14 = f32[2,128,128]{1,2,0:T(8,128)S(1)} custom-call(f32[2,128,128]{2,1,0:T(8,128)S(1)} %get-tuple-element.21), custom_call_target="InvertDiagBlocksLowerTriangular" | custom-call | tf_op jit(solution)/shard_map/jit(_solve_triangular)/triangular_solve | solution.py:31
  129.8 5.1 %fusion.61 = (bf16[256,2048]{1,0:T(8,128)(2,1)}, f32[256,2048]{1,0:T(8,128)}) fusion(bf16[1024,2048]{1,0:T(8,128)(2,1)} %reshape.66, f32[128,1024]{1,0:T(8,128)S(1)} %fusion.17, f32[128,1024]{1,0:T(8,128)S(1)} %fusion.18), kind=kOutput, calls=%fused_computation.111 | convolution fusion | flops 1075052544 | bytes 8388608 | tf_op jit(solution)/shard_map/dot_general | solution.py:61
  134.9 1.9 collective-permute-start.7
  136.9 7.9 %collective-permute-start.6 = (bf16[1024,256]{0,1:T(8,128)(2,1)S(1)}, bf16[1024,256]{0,1:T(8,128)(2,1)S(1)}, u32[]{:S(2)}, u32[]{:S(2)}) collective-permute-start(bf16[1024,256]{0,1:T(8,128)(2,1)S(1)} %fusion.51), channel_id=1, source_target_pairs={{1,0},{2,1},{3,2},{4,3},{5,4},{6,5},{7,6},{8,7},{9,8},{10,9},{11,1... | collective-permute-start | bytes 1572872 | tf_op jit(solution)/shard_map/ppermute | solution.py:10
  144.8 6.7 %collective-permute-done.6 = bf16[1024,256]{0,1:T(8,128)(2,1)S(1)} collective-permute-done((bf16[1024,256]{0,1:T(8,128)(2,1)S(1)}, bf16[1024,256]{0,1:T(8,128)(2,1)S(1)}, u32[]{:S(2)}, u32[]{:S(2)}) %collective-permute-start.6) | collective-permute-done | bytes 524320 | tf_op jit(solution)/shard_map/ppermute | solution.py:10
  152.1 3.5 %collective-permute-done.7 = bf16[256,2048]{1,0:T(8,128)(2,1)} collective-permute-done((bf16[256,2048]{1,0:T(8,128)(2,1)}, bf16[256,2048]{1,0:T(8,128)(2,1)}, u32[]{:S(2)}, u32[]{:S(2)}) %collective-permute-start.7) | collective-permute-done | bytes 1048608 | tf_op jit(solution)/shard_map/ppermute | solution.py:10
  155.5 2.2 multiply_convert_fusion.1
  158.2 4.7 %collective-permute-start.9 = (bf16[256,8,256]{2,1,0:T(8,128)(2,1)S(1)}, bf16[256,8,256]{2,1,0:T(8,128)(2,1)}, u32[]{:S(2)}, u32[]{:S(2)}) collective-permute-start(bf16[256,8,256]{2,1,0:T(8,128)(2,1)S(1)} %fusion.3), channel_id=1, source_target_pairs={{1,0},{2,1},{3,2},{4,3},{5,4},{6,5},{7,6},{8,7},{9,8},{10,9},{11,1... | collective-permute-start | bytes 3145736 | tf_op jit(solution)/shard_map/ppermute | solution.py:10
  163.0 1.9 collective-permute-start.10
  165.7 1.9 collective-permute-start.8
  168.9 1.9 collective-permute-start.11
  170.8 4.5 %collective-permute-done.9 = bf16[256,8,256]{2,1,0:T(8,128)(2,1)} collective-permute-done((bf16[256,8,256]{2,1,0:T(8,128)(2,1)S(1)}, bf16[256,8,256]{2,1,0:T(8,128)(2,1)}, u32[]{:S(2)}, u32[]{:S(2)}) %collective-permute-start.9) | collective-permute-done | bytes 1048608 | tf_op jit(solution)/shard_map/ppermute | solution.py:10
  175.7 5.1 %collective-permute-done.8 = bf16[128,8,256]{2,1,0:T(8,128)(2,1)} collective-permute-done((bf16[128,8,256]{2,1,0:T(8,128)(2,1)}, bf16[128,8,256]{2,1,0:T(8,128)(2,1)}, u32[]{:S(2)}, u32[]{:S(2)}) %collective-permute-start.8) | collective-permute-done | bytes 524320 | tf_op jit(solution)/shard_map/ppermute | solution.py:10
  180.8 4.4 %convolution_convert_fusion = bf16[1024,2048]{1,0:T(8,128)(2,1)} fusion(bf16[256,2048]{1,0:T(8,128)(2,1)S(1)} %bitcast.155, bf16[128,8,256]{2,1,0:T(8,128)(2,1)} %collective-permute-done.8, bf16[256,8,256]{2,1,0:T(8,128)(2,1)S(1)} %fusion.3, pred[]{:T(512)S(6)} %and.28), kind=kOutput, calls=%fused_computation.6 | convolution fusion | flops 1076101120 | bytes 6291457 | tf_op jit(solution)/shard_map/dot_general | solution.py:17
  185.1 7.4 %reshape.71 = bf16[128,64,256]{2,1,0:T(8,128)(2,1)} reshape(bf16[1024,2048]{1,0:T(8,128)(2,1)} %convolution_convert_fusion) | data formatting | bytes 8388608 | tf_op jit(solution)/shard_map/reshape | solution.py:22
  192.5 5.5 %convert_bitcast_fusion = bf16[128,64,256]{2,1,0:T(8,128)(2,1)} fusion(bf16[128,64,256]{2,1,0:T(8,128)(2,1)} %reshape.71, bf16[64,64]{1,0:T(8,128)(2,1)S(1)} %collective-permute-done.10, pred[]{:T(512)S(6)} %and.28, bf16[1,64,64]{2,1,0:T(8,128)(2,1)S(1)} %copy-done.10), kind=kOutput, calls=%fused_computation.4 | convolution fusion | flops 270536704 | bytes 8404993 | tf_op jit(solution)/shard_map/xy,ayc->axc/dot_general | solution.py:23
  198.0 7.4 %reshape.72 = bf16[1024,2048]{1,0:T(8,128)(2,1)} reshape(bf16[128,64,256]{2,1,0:T(8,128)(2,1)} %convert_bitcast_fusion) | data formatting | bytes 8388608 | tf_op jit(solution)/shard_map/reshape | solution.py:26
  205.4 3.7 %fusion.6 = f32[1024,256]{1,0:T(8,128)S(1)} fusion(bf16[1024,2048]{1,0:T(8,128)(2,1)} %reshape.72, bf16[2048,256]{1,0:T(8,128)(2,1)} %convert_bitcast_fusion.2, bf16[2048,256]{1,0:T(8,128)(2,1)} %collective-permute-done.11, pred[]{:T(512)S(6)} %and.28), kind=kOutput, calls=%fused_computation.24 | convolution fusion | flops 1074266112 | bytes 7340033 | tf_op jit(solution)/shard_map/dot_general | solution.py:55
  210.2 3.2 %collective-permute-start.12 = (bf16[256,256]{0,1:T(8,128)(2,1)S(1)}, bf16[256,256]{0,1:T(8,128)(2,1)S(1)}, u32[]{:S(2)}, u32[]{:S(2)}) collective-permute-start(bf16[256,256]{0,1:T(8,128)(2,1)S(1)} %get-tuple-element.57), channel_id=1, source_target_pairs={{1,0},{2,1},{3,2},{4,3},{5,4},{6,5},{7,6},{8,7},{9,8},{10,9},{11,1... | collective-permute-start | bytes 393224 | tf_op jit(solution)/shard_map/ppermute | solution.py:10
  213.4 2.3 collective-permute-start.13
  215.9 8.0 %collective-permute-done.13 = bf16[256,256]{0,1:T(8,128)(2,1)S(1)} collective-permute-done((bf16[256,256]{0,1:T(8,128)(2,1)S(1)}, bf16[256,256]{0,1:T(8,128)(2,1)S(1)}, u32[]{:S(2)}, u32[]{:S(2)}) %collective-permute-start.13) | collective-permute-done | bytes 131104 | tf_op jit(solution)/shard_map/ppermute | solution.py:10
  228.2 11.7 %cholesky.164 = f32[128,128]{1,0:T(8,128)S(1)} custom-call(f32[128,128]{1,0:T(8,128)S(1)} %cholesky.197), custom_call_target="Cholesky" | custom-call | tf_op jit(solution)/shard_map/jit(cholesky)/cholesky | solution.py:30
  239.9 9.8 %custom-call.15 = f32[1,128,128]{1,2,0:T(8,128)S(1)} custom-call(f32[1,128,128]{2,1,0:T(8,128)S(1)} %get-tuple-element.46), custom_call_target="InvertDiagBlocksLowerTriangular" | custom-call | tf_op jit(solution)/shard_map/jit(cholesky)/cholesky | solution.py:30
  251.9 11.7 %cholesky.181 = f32[128,128]{1,0:T(8,128)S(1)} custom-call(f32[128,128]{1,0:T(8,128)S(1)} %convolution_subtract_fusion), custom_call_target="Cholesky" | custom-call | tf_op jit(solution)/shard_map/jit(cholesky)/cholesky | solution.py:30
  267.3 4.3 %while.5 = (s32[]{:T(128)}, f32[256,256]{1,0:T(8,128)S(1)}, s32[2,2]{1,0:T(2,128)S(1)}, f32[2,128,128]{2,1,0:T(8,128)S(1)}, s32[]{:T(128)}) while((s32[]{:T(128)}, f32[256,256]{1,0:T(8,128)S(1)}, s32[2,2]{1,0:T(2,128)S(1)}, f32[2,128,128]{2,1,0:T(8,128)S(1)}, s32[]{:T(128)}) %tuple.53), condition=%wide.while_cond.clone, body=%wide.while_body.clone.sunk | while | flops 2 | bytes 131181 | solution.py:31
  272.2 20.5 %custom-call.16 = f32[2,128,128]{1,2,0:T(8,128)S(1)} custom-call(f32[2,128,128]{2,1,0:T(8,128)} %copy-done.7), custom_call_target="InvertDiagBlocksLowerTriangular" | custom-call | tf_op jit(solution)/shard_map/jit(_solve_triangular)/triangular_solve | solution.py:31
  295.0 5.1 %fusion.63 = (bf16[256,2048]{1,0:T(8,128)(2,1)}, f32[256,2048]{1,0:T(8,128)}) fusion(bf16[1024,2048]{1,0:T(8,128)(2,1)} %reshape.72, f32[128,1024]{1,0:T(8,128)S(1)} %fusion.12, f32[128,1024]{1,0:T(8,128)S(1)} %fusion.13), kind=kOutput, calls=%fused_computation.113 | convolution fusion | flops 1075052544 | bytes 8388608 | tf_op jit(solution)/shard_map/dot_general | solution.py:61
  302.2 7.9 %collective-permute-start.14 = (bf16[1024,256]{0,1:T(8,128)(2,1)S(1)}, bf16[1024,256]{0,1:T(8,128)(2,1)S(1)}, u32[]{:S(2)}, u32[]{:S(2)}) collective-permute-start(bf16[1024,256]{0,1:T(8,128)(2,1)S(1)} %fusion.48), channel_id=1, source_target_pairs={{1,0},{2,1},{3,2},{4,3},{5,4},{6,5},{7,6},{8,7},{9,8},{10,9},{11,1... | collective-permute-start | bytes 1572872 | tf_op jit(solution)/shard_map/ppermute | solution.py:10
  310.1 6.7 %collective-permute-done.14 = bf16[1024,256]{0,1:T(8,128)(2,1)S(1)} collective-permute-done((bf16[1024,256]{0,1:T(8,128)(2,1)S(1)}, bf16[1024,256]{0,1:T(8,128)(2,1)S(1)}, u32[]{:S(2)}, u32[]{:S(2)}) %collective-permute-start.14) | collective-permute-done | bytes 524320 | tf_op jit(solution)/shard_map/ppermute | solution.py:10
  317.8 2.4 copy.22
  320.8 2.2 multiply_convert_fusion
  (95 shorter events, 40.5 us)
Async XLA Ops:
  0.0 20.8 %copy-start = (bf16[1,256,8,256]{3,2,1,0:T(8,128)(2,1)S(1)}, bf16[1,256,8,256]{3,2,1,0:T(8,128)(2,1)}, u32[]{:S(2)}) copy-start(bf16[1,256,8,256]{3,2,1,0:T(8,128)(2,1)} %param.8) | copy-start | bytes 3145732
  0.0 20.8 %collective-permute-start.1 = (bf16[256,8,256]{2,1,0:T(8,128)(2,1)}, bf16[256,8,256]{2,1,0:T(8,128)(2,1)}, u32[]{:S(2)}, u32[]{:S(2)}) collective-permute-start(bf16[256,8,256]{2,1,0:T(8,128)(2,1)} %bitcast.149), channel_id=1, source_target_pairs={{1,0},{2,1},{3,2},{4,3},{5,4},{6,5},{7,6},{8,7},{9,8},{10,9},{11,1... | collective-permute-start | bytes 3145736 | tf_op jit(solution)/shard_map/ppermute | solution.py:10
  9.3 14.7 %collective-permute-start = (bf16[128,8,256]{2,1,0:T(8,128)(2,1)S(1)}, bf16[128,8,256]{2,1,0:T(8,128)(2,1)S(1)}, u32[]{:S(2)}, u32[]{:S(2)}) collective-permute-start(bf16[128,8,256]{2,1,0:T(8,128)(2,1)S(1)} %slice_bitcast_fusion), channel_id=1, source_target_pairs={{0,1},{1,2},{2,3},{3,4},{4,5},{5,6},{6,7},{7,8},{8,9},{9,10},{10,1... | collective-permute-start | bytes 1572872 | tf_op jit(solution)/shard_map/ppermute | solution.py:10
  11.3 23.5 %collective-permute-start.2 = (bf16[64,64]{1,0:T(8,128)(2,1)}, bf16[64,64]{1,0:T(8,128)(2,1)S(1)}, u32[]{:S(2)}, u32[]{:S(2)}) collective-permute-start(bf16[64,64]{1,0:T(8,128)(2,1)} %bitcast.162), channel_id=1, source_target_pairs={{0,1},{1,2},{2,3},{3,4},{4,5},{5,6},{6,7},{7,8},{8,9},{9,10},{10,1... | collective-permute-start | bytes 24584 | tf_op jit(solution)/shard_map/ppermute | solution.py:10
  14.9 32.6 %collective-permute-start.3 = (bf16[2048,256]{1,0:T(8,128)(2,1)S(1)}, bf16[2048,256]{1,0:T(8,128)(2,1)}, u32[]{:S(2)}, u32[]{:S(2)}) collective-permute-start(bf16[2048,256]{1,0:T(8,128)(2,1)S(1)} %convert_bitcast_fusion.3), channel_id=1, source_target_pairs={{0,1},{1,2},{2,3},{3,4},{4,5},{5,6},{6,7},{7,8},{8,9},{9,10},{10,1... | collective-permute-start | bytes 3145736 | tf_op jit(solution)/shard_map/ppermute | solution.py:10
  27.3 7.4 %copy-start.9 = (bf16[1,64,64]{2,1,0:T(8,128)(2,1)S(1)}, bf16[1,64,64]{2,1,0:T(8,128)(2,1)}, u32[]{:S(2)}) copy-start(bf16[1,64,64]{2,1,0:T(8,128)(2,1)} %param.9) | copy-start | bytes 24580
  51.4 8.1 %collective-permute-start.4 = (bf16[256,256]{0,1:T(8,128)(2,1)S(1)}, bf16[256,256]{0,1:T(8,128)(2,1)S(1)}, u32[]{:S(2)}, u32[]{:S(2)}) collective-permute-start(bf16[256,256]{0,1:T(8,128)(2,1)S(1)} %get-tuple-element.51), channel_id=1, source_target_pairs={{1,0},{2,1},{3,2},{4,3},{5,4},{6,5},{7,6},{8,7},{9,8},{10,9},{11,1... | collective-permute-start | bytes 393224 | tf_op jit(solution)/shard_map/ppermute | solution.py:10
  57.0 10.5 %collective-permute-start.5 = (bf16[256,256]{0,1:T(8,128)(2,1)S(1)}, bf16[256,256]{0,1:T(8,128)(2,1)S(1)}, u32[]{:S(2)}, u32[]{:S(2)}) collective-permute-start(bf16[256,256]{0,1:T(8,128)(2,1)S(1)} %get-tuple-element.51), channel_id=1, source_target_pairs={{0,1},{1,2},{2,3},{3,4},{4,5},{5,6},{6,7},{7,8},{8,9},{9,10},{10,1... | collective-permute-start | bytes 393224 | tf_op jit(solution)/shard_map/ppermute | solution.py:10
  134.9 20.6 %collective-permute-start.7 = (bf16[256,2048]{1,0:T(8,128)(2,1)}, bf16[256,2048]{1,0:T(8,128)(2,1)}, u32[]{:S(2)}, u32[]{:S(2)}) collective-permute-start(bf16[256,2048]{1,0:T(8,128)(2,1)} %get-tuple-element.55), channel_id=1, source_target_pairs={{0,1},{1,2},{2,3},{3,4},{4,5},{5,6},{6,7},{7,8},{8,9},{9,10},{10,1... | collective-permute-start | bytes 3145736 | tf_op jit(solution)/shard_map/ppermute | solution.py:10
  136.9 14.5 %collective-permute-start.6 = (bf16[1024,256]{0,1:T(8,128)(2,1)S(1)}, bf16[1024,256]{0,1:T(8,128)(2,1)S(1)}, u32[]{:S(2)}, u32[]{:S(2)}) collective-permute-start(bf16[1024,256]{0,1:T(8,128)(2,1)S(1)} %fusion.51), channel_id=1, source_target_pairs={{1,0},{2,1},{3,2},{4,3},{5,4},{6,5},{7,6},{8,7},{9,8},{10,9},{11,1... | collective-permute-start | bytes 1572872 | tf_op jit(solution)/shard_map/ppermute | solution.py:10
  157.7 5.3 %copy-start.10 = (bf16[1,64,64]{2,1,0:T(8,128)(2,1)S(1)}, bf16[1,64,64]{2,1,0:T(8,128)(2,1)}, u32[]{:S(2)}) copy-start(bf16[1,64,64]{2,1,0:T(8,128)(2,1)} %param.10) | copy-start | bytes 24580
  157.7 10.0 %copy-start.4 = (s32[1,2048,256]{2,1,0:T(8,128)S(1)}, s32[1,2048,256]{2,1,0:T(8,128)}, u32[]{:S(2)}) copy-start(s32[1,2048,256]{2,1,0:T(8,128)} %param.12) | copy-start | bytes 6291460
  158.0 10.8 %copy-start.1 = (bf16[32,8,8,256]{3,2,1,0:T(8,128)(2,1)}, bf16[32,8,8,256]{3,2,1,0:T(8,128)(2,1)S(1)}, u32[]{:S(2)}) copy-start(bf16[32,8,8,256]{3,2,1,0:T(8,128)(2,1)S(1)} %copy.27) | copy-start | bytes 3145732
  158.2 17.0 %collective-permute-start.9 = (bf16[256,8,256]{2,1,0:T(8,128)(2,1)S(1)}, bf16[256,8,256]{2,1,0:T(8,128)(2,1)}, u32[]{:S(2)}, u32[]{:S(2)}) collective-permute-start(bf16[256,8,256]{2,1,0:T(8,128)(2,1)S(1)} %fusion.3), channel_id=1, source_target_pairs={{1,0},{2,1},{3,2},{4,3},{5,4},{6,5},{7,6},{8,7},{9,8},{10,9},{11,1... | collective-permute-start | bytes 3145736 | tf_op jit(solution)/shard_map/ppermute | solution.py:10
  163.0 29.5 %collective-permute-start.10 = (bf16[64,64]{1,0:T(8,128)(2,1)S(1)}, bf16[64,64]{1,0:T(8,128)(2,1)S(1)}, u32[]{:S(2)}, u32[]{:S(2)}) collective-permute-start(bf16[64,64]{1,0:T(8,128)(2,1)S(1)} %bitcast.163), channel_id=1, source_target_pairs={{0,1},{1,2},{2,3},{3,4},{4,5},{5,6},{6,7},{7,8},{8,9},{9,10},{10,1... | collective-permute-start | bytes 24584 | tf_op jit(solution)/shard_map/ppermute | solution.py:10
  165.7 15.0 %collective-permute-start.8 = (bf16[128,8,256]{2,1,0:T(8,128)(2,1)}, bf16[128,8,256]{2,1,0:T(8,128)(2,1)}, u32[]{:S(2)}, u32[]{:S(2)}) collective-permute-start(bf16[128,8,256]{2,1,0:T(8,128)(2,1)} %slice.71), channel_id=1, source_target_pairs={{0,1},{1,2},{2,3},{3,4},{4,5},{5,6},{6,7},{7,8},{8,9},{9,10},{10,1... | collective-permute-start | bytes 1572872 | tf_op jit(solution)/shard_map/ppermute | solution.py:10
  168.9 36.5 %collective-permute-start.11 = (bf16[2048,256]{1,0:T(8,128)(2,1)}, bf16[2048,256]{1,0:T(8,128)(2,1)}, u32[]{:S(2)}, u32[]{:S(2)}) collective-permute-start(bf16[2048,256]{1,0:T(8,128)(2,1)} %convert_bitcast_fusion.2), channel_id=1, source_target_pairs={{0,1},{1,2},{2,3},{3,4},{4,5},{5,6},{6,7},{7,8},{8,9},{9,10},{10,1... | collective-permute-start | bytes 3145736 | tf_op jit(solution)/shard_map/ppermute | solution.py:10
  210.2 5.8 %collective-permute-start.12 = (bf16[256,256]{0,1:T(8,128)(2,1)S(1)}, bf16[256,256]{0,1:T(8,128)(2,1)S(1)}, u32[]{:S(2)}, u32[]{:S(2)}) collective-permute-start(bf16[256,256]{0,1:T(8,128)(2,1)S(1)} %get-tuple-element.57), channel_id=1, source_target_pairs={{1,0},{2,1},{3,2},{4,3},{5,4},{6,5},{7,6},{8,7},{9,8},{10,9},{11,1... | collective-permute-start | bytes 393224 | tf_op jit(solution)/shard_map/ppermute | solution.py:10
  213.4 10.5 %collective-permute-start.13 = (bf16[256,256]{0,1:T(8,128)(2,1)S(1)}, bf16[256,256]{0,1:T(8,128)(2,1)S(1)}, u32[]{:S(2)}, u32[]{:S(2)}) collective-permute-start(bf16[256,256]{0,1:T(8,128)(2,1)S(1)} %get-tuple-element.57), channel_id=1, source_target_pairs={{0,1},{1,2},{2,3},{3,4},{4,5},{5,6},{6,7},{7,8},{8,9},{9,10},{10,1... | collective-permute-start | bytes 393224 | tf_op jit(solution)/shard_map/ppermute | solution.py:10
  224.0 0.7 copy-start.8
  227.5 0.7 copy-start.6
  263.7 2.6 copy-start.5
  271.6 0.7 copy-start.7
  300.2 20.6 %collective-permute-start.15 = (bf16[256,2048]{1,0:T(8,128)(2,1)}, bf16[256,2048]{1,0:T(8,128)(2,1)}, u32[]{:S(2)}, u32[]{:S(2)}) collective-permute-start(bf16[256,2048]{1,0:T(8,128)(2,1)} %get-tuple-element.61), channel_id=1, source_target_pairs={{0,1},{1,2},{2,3},{3,4},{4,5},{5,6},{6,7},{7,8},{8,9},{9,10},{10,1... | collective-permute-start | bytes 3145736 | tf_op jit(solution)/shard_map/ppermute | solution.py:10
  302.2 14.5 %collective-permute-start.14 = (bf16[1024,256]{0,1:T(8,128)(2,1)S(1)}, bf16[1024,256]{0,1:T(8,128)(2,1)S(1)}, u32[]{:S(2)}, u32[]{:S(2)}) collective-permute-start(bf16[1024,256]{0,1:T(8,128)(2,1)S(1)} %fusion.48), channel_id=1, source_target_pairs={{1,0},{2,1},{3,2},{4,3},{5,4},{6,5},{7,6},{8,7},{9,8},{10,9},{11,1... | collective-permute-start | bytes 1572872 | tf_op jit(solution)/shard_map/ppermute | solution.py:10
  317.8 5.5 %copy-start.2 = (bf16[32,8,8,256]{3,2,1,0:T(8,128)(2,1)S(1)}, bf16[32,8,8,256]{3,2,1,0:T(8,128)(2,1)}, u32[]{:S(2)}) copy-start(bf16[32,8,8,256]{3,2,1,0:T(8,128)(2,1)} %copy-done.1) | copy-start | bytes 3145732
  320.2 3.1 copy-start.3
where the time goes:
time: 331 us; the launch traced here: 325 us
  other arithmetic  123 us (37%)
  starting transfers between devices  57.2 us (17%)
  waiting for transfers between devices  49.1 us (15%)
  local copies, waits for them, and re-layouts  46.7 us (14%)
  matrix products  44.6 us (13%)
  between operations  3.33 us (1%)
    another operation x13, other arithmetic, basis_from(): factor_lower = jnp.linalg.cholesky(gram_matrix)  68.6 us
    ppermute x16, starting transfers between devices, from_behind(): return lax.ppermute(array, axis, pairs)  57.2 us
    ppermute x16, waiting for transfers between devices, from_behind(): return lax.ppermute(array, axis, pairs)  49.1 us
    another operation x5, other arithmetic, basis_from(): jax.scipy.linalg.solve_triangular(factor_lower, sampled.T, lower=True)  41.2 us
    reshape x2, local copies, waits for them, and re-layouts, contract(): two_site = two_site.reshape(rows_count, levels * levels, bond_dim)  14.8 us
    reshape x2, local copies, waits for them, and re-layouts, contract(): return gated_pair.reshape(rows_count * levels, levels * bond_dim)  14.8 us
    dot_general x2, matrix products, contract(): jnp.einsum('xy,ayc->axc', gate_matrix, two_site, preferred_element_type=j...  10.9 us
    dot_general x2, matrix products, apply_layer(): lax.dot_general(left_rows, matrix, (((0,), (0,)), ((), ())), preferred_el...  10.3 us
  transfers between devices with their start and end apart: 16, of which 12 were waited for; matrix products, arithmetic and copies ran while one was open for 18% of the time, Pallas kernels for 0%

commit v1 on v0

v1 whole, which is shorter than its diff:
```python
import functools

import jax
import jax.numpy as jnp
from jax import lax
from jax.experimental import pallas as pl
from jax.experimental.pallas import tpu as pltpu
from jax.sharding import PartitionSpec as P

F32 = jnp.float32
BF16 = jnp.bfloat16
ANY = pl.BlockSpec(memory_space=pl.ANY)
VMEM = pl.BlockSpec(memory_space=pltpu.VMEM)
CHI = 256
LEVELS = 8
ROWS = CHI * LEVELS
GATE = LEVELS * LEVELS
BLOCK = 64


def lanes_of(v, k):
    return jnp.broadcast_to(v[:, k : k + 1], (8, 128))


def row_of(v, r):
    return jnp.broadcast_to(v[r : r + 1, :], (8, 128))


def inverse_factor(diag_block):
    nb = BLOCK
    nv = nb // 8
    rows = lax.broadcasted_iota(jnp.int32, (nb, nb), 0)
    cols = lax.broadcasted_iota(jnp.int32, (nb, nb), 1)
    beside = jnp.concatenate([diag_block, jnp.where(rows == cols, 1.0, 0.0).astype(F32)], axis=1)
    v = [beside[8 * q : 8 * q + 8, :] for q in range(nv)]
    sub = lax.broadcasted_iota(jnp.int32, (8, 128), 0)
    scale = [jnp.ones((8, 128), F32)] * nv
    c = [[lanes_of(v[q], i) for q in range(nv)] for i in range(4)]
    for k in range(0, nb, 4):
        p, r = divmod(k, 8)
        last = k + 4 >= nb
        if not last:
            p2, r2 = divmod(k + 4, 8)
            ahead = [[lanes_of(v[q], k + 4 + i) for q in range(p2, nv)] for i in range(4)]
        row = [row_of(v[p], r + i) for i in range(4)]
        g = [[row_of(c[j][0], r + i) if i >= j else None for j in range(4)] for i in range(4)]
        a, b, d = g[0][0], g[1][0], g[1][1]
        det = a * d - b * b
        idet = 1.0 / det
        ia = 1.0 / a
        ad, bd, dd = a * idet, b * idet, d * idet

        def first_pair(x, y):
            return x * dd - y * bd, y * ad - x * bd

        m20, m21 = first_pair(g[2][0], g[2][1])
        m30, m31 = first_pair(g[3][0], g[3][1])
        a2 = g[2][2] - (m20 * g[2][0] + m21 * g[2][1])
        b2 = g[3][2] - (m30 * g[2][0] + m31 * g[2][1])
        d2 = g[3][3] - (m30 * g[3][0] + m31 * g[3][1])
        det2 = a2 * d2 - b2 * b2
        idet2 = 1.0 / det2
        ia2 = 1.0 / a2
        ad2, bd2, dd2 = a2 * idet2, b2 * idet2, d2 * idet2

        def panel_solve(x0, x1, x2, x3):
            y2 = x2 - (m20 * x0 + m21 * x1)
            y3 = x3 - (m30 * x0 + m31 * x1)
            h2 = y2 * dd2 - y3 * bd2
            h3 = y3 * ad2 - y2 * bd2
            u0, u1 = first_pair(x0, x1)
            return (u0 - (m20 * h2 + m30 * h3), u1 - (m21 * h2 + m31 * h3), h2, h3), y2, y3

        if not last:
            c_next = []
            for i in range(4):
                hs, _, _ = panel_solve(*[row_of(c[j][p2 - p], r2 + i) for j in range(4)])
                c_next.append(
                    [
                        ahead[i][q - p2]
                        - (
                            (c[0][q - p] * hs[0] + c[1][q - p] * hs[1])
                            + (c[2][q - p] * hs[2] + c[3][q - p] * hs[3])
                        )
                        for q in range(p2, nv)
                    ]
                )
        h, row2, row3 = panel_solve(*row)
        below = sub > r + 3
        for q in range(p, nv):
            cq = [c[j][q - p] for j in range(4)]
            if q == p:
                cq = [jnp.where(below, x, 0.0) for x in cq]
            v[q] = v[q] - ((cq[0] * h[0] + cq[1] * h[1]) + (cq[2] * h[2] + cq[3] * h[3]))
        row1 = row[1] - (b * ia) * row[0]
        row3 = row3 - (b2 * ia2) * row2
        v[p] = jnp.where(
            sub == r + 1, row1, jnp.where(sub == r + 2, row2, jnp.where(sub == r + 3, row3, v[p]))
        )
        scale[p] = jnp.where(
            sub == r,
            lax.rsqrt(a),
            jnp.where(
                sub == r + 1,
                lax.rsqrt(det * ia),
                jnp.where(sub == r + 2, lax.rsqrt(a2), jnp.where(sub == r + 3, lax.rsqrt(det2 * ia2), scale[p])),
            ),
        )
        if not last:
            c = c_next
    return jnp.concatenate([v[q] * scale[q] for q in range(nv)], axis=0)[:, nb:]


def dot(x, y, dims=((1,), (0,))):
    return lax.dot_general(x, y, (dims, ((), ())), preferred_element_type=F32)


def dot_split(x, y, dims=((1,), (0,))):
    xh = x.astype(BF16)
    xl = (x - xh.astype(F32)).astype(BF16)
    yh = y.astype(BF16)
    yl = (y - yh.astype(F32)).astype(BF16)
    return dot(xh, yh, dims) + (dot(xh, yl, dims) + dot(xl, yh, dims))


def gate_matrix(packed):
    i = lax.broadcasted_iota(jnp.int32, (GATE, GATE), 0)
    j = lax.broadcasted_iota(jnp.int32, (GATE, GATE), 1)
    swap = jnp.where(j == (i & 7) * 8 + (i >> 3), 1.0, 0.0).astype(BF16)
    g = dot(dot(swap, packed[:, :GATE]).astype(BF16), swap, ((1,), (1,))).astype(BF16)
    wide = jnp.concatenate([jnp.concatenate([g] * 4, axis=1)] * 4, axis=0)
    big_i = lax.broadcasted_iota(jnp.int32, (4 * GATE, 4 * GATE), 0)
    big_j = lax.broadcasted_iota(jnp.int32, (4 * GATE, 4 * GATE), 1)
    return jnp.where((big_i >> 6) == (big_j >> 6), wide, jnp.zeros_like(wide))


def every_level(wide, t):
    return jnp.concatenate([wide[h, pl.ds(t, CHI, stride=LEVELS), :] for h in range(2)], axis=1)


def put_level(wide, t, value):
    for h in range(2):
        wide[h, pl.ds(t, CHI, stride=LEVELS), :] = value[:, h * 128 : (h + 1) * 128]


def pair_kernel(own, recv, sk_own, sk_recv, out, left, right, raw, sk, gate, y, m, s, wide, q, ab, sems, *, layer):
    me = lax.axis_index("site")
    devices = lax.axis_size("site")
    is_left = lax.rem(me, 2) == layer
    idle = (layer == 1) & ((me == 0) | (me == devices - 1))
    right_in = raw if layer == 0 else right

    @pl.when(is_left)
    def _():
        pltpu.make_async_copy(recv, right_in, sems.at[1]).start()
        pltpu.make_async_copy(own, left, sems.at[0]).start()
        pltpu.make_async_copy(sk_own, sk, sems.at[2]).start()

    @pl.when(jnp.logical_not(is_left))
    def _():
        pltpu.make_async_copy(own, right_in, sems.at[1]).start()
        pltpu.make_async_copy(recv, left, sems.at[0]).start()
        pltpu.make_async_copy(sk_recv, sk, sems.at[2]).start()

    pltpu.make_async_copy(own, right_in, sems.at[1]).wait()
    if layer == 0:
        for h in range(2):
            wide[h] = raw[:, h * 128 : (h + 1) * 128].astype(F32)
        for t in range(LEVELS):
            right[t * CHI : (t + 1) * CHI, :] = every_level(wide, t).astype(BF16)
    pltpu.make_async_copy(own, left, sems.at[0]).wait()

    step = 1024
    bonds = step // LEVELS

    def two_site(i, _):
        r0 = pl.multiple_of(i * step, step)
        a0 = pl.multiple_of(i * bonds, bonds)
        block = left[pl.ds(r0, step), :]
        for t in range(0, LEVELS, 2):
            parts = [
                dot(block, right[u * CHI : (u + 1) * CHI, :]).reshape(bonds, LEVELS, CHI) for u in (t, t + 1)
            ]
            y[pl.ds(a0, bonds), t * LEVELS : (t + 2) * LEVELS, :] = jnp.concatenate(parts, axis=1).astype(BF16)
        return 0

    lax.fori_loop(0, ROWS // step, two_site, 0)

    pltpu.make_async_copy(sk_own, sk, sems.at[2]).wait()
    gate[...] = gate_matrix(sk[ROWS:, :])

    step_g = 512
    bonds_g = step_g // LEVELS

    def gated(i, _):
        r0 = pl.multiple_of(i * step_g, step_g)
        a0 = pl.multiple_of(i * bonds_g, bonds_g)
        for j in range(bonds_g // 4):
            four = y[pl.ds(a0 + 4 * j, 4)].reshape(4 * GATE, CHI)
            o = dot(gate[...], four).reshape(4, LEVELS, LEVELS, CHI)
            for h in range(2):
                at = pl.multiple_of(r0 + j * 32 + h * 16, 16)
                for t in range(LEVELS):
                    m[pl.ds(at, 16), t * CHI : (t + 1) * CHI] = jnp.concatenate(
                        [o[2 * h, t], o[2 * h + 1, t]], axis=0
                    ).astype(BF16)
        return 0

    lax.fori_loop(0, ROWS // step_g, gated, 0)

    def sample(i, _):
        r0 = pl.multiple_of(i * step, step)
        s[pl.ds(r0, step), :] = dot(m[pl.ds(r0, step), :], sk[:ROWS, :]).astype(BF16)
        return 0

    lax.fori_loop(0, ROWS // step, sample, 0)

    ab[:, :CHI] = dot(s[...], s[...], ((0,), (0,)))
    diag_i = lax.broadcasted_iota(jnp.int32, (CHI, CHI), 0)
    diag_j = lax.broadcasted_iota(jnp.int32, (CHI, CHI), 1)
    ab[:, CHI:] = jnp.where(diag_i == diag_j, 1.0, 0.0).astype(F32)
    for o in range(0, CHI, BLOCK):
        e = o + BLOCK
        w = inverse_factor(ab[o:e, o:e])
        panel = dot_split(w, ab[o:e, :])
        ab[o:e, CHI:] = panel[:, CHI:]
        if e < CHI:
            ab[e:, :] = ab[e:, :] - dot_split(panel[:, e:CHI], panel, ((0,), (0,)))

    left_scale = LEVELS**0.5 * CHI**0.25

    @pl.when(is_left)
    def _():
        inv = (ab[:, CHI:] * left_scale).astype(BF16)
        if layer == 0:
            made = dot(s[...], inv, ((1,), (1,)))
            for h in range(2):
                wide[h] = made[:, h * 128 : (h + 1) * 128]
            for t in range(LEVELS):
                out[t * CHI : (t + 1) * CHI, :] = every_level(wide, t).astype(BF16)
        else:
            out[...] = dot(s[...], inv, ((1,), (1,))).astype(BF16)

            @pl.when(idle)
            def _():
                out[...] = left[...]

    @pl.when(jnp.logical_not(is_left))
    def _():
        inv = (ab[:, CHI:] * (left_scale * ROWS**-0.5)).astype(BF16)
        for t in range(LEVELS):
            q[...] = dot(s[...], m[:, t * CHI : (t + 1) * CHI], ((0,), (0,)))
            put_level(wide, t, dot(inv, q[...].astype(BF16)))
        if layer == 1:

            @pl.when(idle)
            def _():
                for t in range(LEVELS):
                    put_level(wide, t, right[t * CHI : (t + 1) * CHI, :].astype(F32))

        for h in range(2):
            out[:, h * 128 : (h + 1) * 128] = wide[h].astype(BF16)


def pair_step(own, recv, sk_own, sk_recv, layer):
    return pl.pallas_call(
        functools.partial(pair_kernel, layer=layer),
        out_shape=jax.ShapeDtypeStruct((ROWS, CHI), BF16),
        in_specs=[ANY] * 4,
        out_specs=VMEM,
        scratch_shapes=[
            pltpu.VMEM((ROWS, CHI), BF16),
            pltpu.VMEM((ROWS, CHI), BF16),
            pltpu.VMEM((ROWS, CHI), BF16),
            pltpu.VMEM((ROWS + GATE, CHI), BF16),
            pltpu.VMEM((4 * GATE, 4 * GATE), BF16),
            pltpu.VMEM((CHI, GATE, CHI), BF16),
            pltpu.VMEM((ROWS, ROWS), BF16),
            pltpu.VMEM((ROWS, CHI), BF16),
            pltpu.VMEM((2, ROWS, 128), F32),
            pltpu.VMEM((CHI, CHI), F32),
            pltpu.VMEM((CHI, 2 * CHI), F32),
            pltpu.SemaphoreType.DMA((3,)),
        ],
        compiler_params=pltpu.CompilerParams(vmem_limit_bytes=56 << 20),
        name=f"pair{layer}",
    )(own, recv, sk_own, sk_recv)


def pack_kernel(sketch, gate, out):
    out[:ROWS, :] = sketch[...].astype(BF16)
    out[ROWS:, :] = jnp.concatenate([gate[...]] * 4, axis=1)


def pack(sketch, gate, layer):
    return pl.pallas_call(
        pack_kernel,
        out_shape=jax.ShapeDtypeStruct((ROWS + GATE, CHI), BF16),
        in_specs=[VMEM, VMEM],
        out_specs=VMEM,
        name=f"pack{layer}",
    )(sketch, gate)


def per_device(site_tensors, first_gates, second_gates, first_sketch, second_sketch):
    devices = lax.axis_size("site")
    inside = [(i, i ^ 1) for i in range(devices)]
    across = [(i, (i + 1) % devices if i % 2 else (i - 1) % devices) for i in range(devices)]
    own = site_tensors[0].reshape(ROWS, CHI)
    recv = lax.ppermute(own, "site", inside)
    sk0 = pack(first_sketch[0], first_gates[0], 0)
    sk0_recv = lax.ppermute(sk0, "site", inside)
    sk1 = pack(second_sketch[0], second_gates[0], 1)
    sk1_recv = lax.ppermute(sk1, "site", across)
    own = pair_step(own, recv, sk0, sk0_recv, 0)
    recv = lax.ppermute(own, "site", across)
    own = pair_step(own, recv, sk1, sk1_recv, 1)
    return own.reshape(1, CHI, LEVELS, CHI)


def solution(mesh):
    in_specs = (
        P("site", None, None, None),
        P("site", None, None),
        P("site", None, None),
        P("site", None, None),
        P("site", None, None),
    )
    out_specs = P("site", None, None, None)
    return jax.shard_map(
        per_device, mesh=mesh, in_specs=in_specs, out_specs=out_specs, check_vma=False
    )
```

time: 331 us -> 81.9 us (0.25)
  the two profiles are of different devices: /device:TPU:6 before, /device:TPU:0 now
where the time goes in v1:
time: 81.9 us; the launch traced here: 81.8 us
  Pallas kernels  49.8 us (61%)
  starting transfers between devices  15.6 us (19%)
  waiting for transfers between devices  13.2 us (16%)
  local copies, waits for them, and re-layouts  2.92 us (4%)
    pallas_call x2, Pallas kernels, pair_step(): pl.pallas_call(functools.partial(pair_kernel, layer=layer), out_shape=jax...  44.1 us
    ppermute x1, waiting for transfers between devices, per_device(): recv = lax.ppermute(own, 'site', across)  13.2 us
    ppermute x1, starting transfers between devices, per_device(): sk1_recv = lax.ppermute(sk1, 'site', across)  8.4 us
    ppermute x1, starting transfers between devices, per_device(): recv = lax.ppermute(own, 'site', across)  6.72 us
    pallas_call x2, Pallas kernels, pack(): pl.pallas_call(pack_kernel, out_shape=jax.ShapeDtypeStruct((ROWS + GATE,...  5.75 us
    unnamed x10, local copies, waits for them, and re-layouts  2.92 us
  transfers between devices with their start and end apart: 4, of which 1 were waited for; matrix products, arithmetic and copies ran while one was open for 0% of the time, Pallas kernels for 27%

profile of v1, /device:TPU:0, one launch (start us, length us, event | category | flops | bytes accessed | tf_op | source)
XLA Modules:
  0.0 81.8 jit_solution(18252472721653996959)
XLA Ops:
  0.0 0.0 copy-start.2
  0.0 2.9 %pack0.1.sk_own = bf16[2112,256]{1,0:T(8,128)(2,1)} custom-call(s32[2048,256]{1,0:T(8,128)} %bitcast.6, bf16[64,64]{1,0:T(8,128)(2,1)} %bitcast.10), custom_call_target="tpu_custom_call" | custom-call | tf_op jit(solution)/shard_map/pack0/pallas_call | solution.py:296
  2.9 0.0 collective-permute-start.1
  2.9 0.0 copy-done.2
  2.9 0.5 collective-permute-start
  3.5 2.8 %pack1.1.sk_own = bf16[2112,256]{1,0:T(8,128)(2,1)} custom-call(s32[2048,256]{1,0:T(8,128)} %bitcast.7, bf16[64,64]{1,0:T(8,128)(2,1)} %bitcast.11), custom_call_target="tpu_custom_call" | custom-call | tf_op jit(solution)/shard_map/pack1/pallas_call | solution.py:296
  6.3 8.4 %collective-permute-start.3 = (bf16[2112,256]{1,0:T(8,128)(2,1)}, bf16[2112,256]{1,0:T(8,128)(2,1)S(1)}, u32[]{:S(2)}, u32[]{:S(2)}) collective-permute-start(bf16[2112,256]{1,0:T(8,128)(2,1)} %pack1.1.sk_own), channel_id=1, source_target_pairs={{0,127},{1,2},{2,1},{3,4},{4,3},{5,6},{6,5},{7,8},{8,7},{9,10},{10... | collective-permute-start | bytes 3244040 | tf_op jit(solution)/shard_map/ppermute | solution.py:314
  14.7 0.0 collective-permute-done.recv
  14.7 0.0 copy-start.3
  14.7 0.0 collective-permute-done.1.sk_recv
  14.7 1.0 %copy-done.3 = bf16[2048,256]{1,0:T(8,128)(2,1)} copy-done((bf16[2048,256]{1,0:T(8,128)(2,1)}, bf16[2048,256]{1,0:T(8,128)(2,1)S(1)}, u32[]{:S(2)}) %copy-start.3) | copy-done | bytes 1048600
  15.6 0.0 copy-start.1
  15.6 1.0 %copy-done.1 = bf16[2112,256]{1,0:T(8,128)(2,1)} copy-done((bf16[2112,256]{1,0:T(8,128)(2,1)}, bf16[2112,256]{1,0:T(8,128)(2,1)S(1)}, u32[]{:S(2)}) %copy-start.1) | copy-done | bytes 1081368
  16.6 19.3 %pair0.1.own = bf16[2048,256]{1,0:T(8,128)(2,1)} custom-call(bf16[2048,256]{1,0:T(8,128)(2,1)} %bitcast.8, bf16[2048,256]{1,0:T(8,128)(2,1)} %copy-done.3, bf16[2112,256]{1,0:T(8,128)(2,1)} %pack0.1.sk_own, bf16[2112,256]{1,0:T(8,128)(2,1)} %copy-done.1), custom_call_target="tpu_custom_call" | custom-call | tf_op jit(solution)/shard_map/pair0/pallas_call | solution.py:266
  35.9 6.7 %collective-permute-start.2 = (bf16[2048,256]{1,0:T(8,128)(2,1)}, bf16[2048,256]{1,0:T(8,128)(2,1)S(1)}, u32[]{:S(2)}, u32[]{:S(2)}) collective-permute-start(bf16[2048,256]{1,0:T(8,128)(2,1)} %pair0.1.own), channel_id=1, source_target_pairs={{0,127},{1,2},{2,1},{3,4},{4,3},{5,6},{6,5},{7,8},{8,7},{9,10},{10... | collective-permute-start | bytes 3145736 | tf_op jit(solution)/shard_map/ppermute | solution.py:316
  42.6 0.0 collective-permute-done.3.sk_recv
  42.6 0.0 copy-start
  42.6 13.2 %collective-permute-done.2.recv = bf16[2048,256]{1,0:T(8,128)(2,1)S(1)} collective-permute-done((bf16[2048,256]{1,0:T(8,128)(2,1)}, bf16[2048,256]{1,0:T(8,128)(2,1)S(1)}, u32[]{:S(2)}, u32[]{:S(2)}) %collective-permute-start.2) | collective-permute-done | bytes 1048608 | tf_op jit(solution)/shard_map/ppermute | solution.py:316
  55.9 0.0 copy-done
  55.9 0.0 copy-start.4
  55.9 1.0 %copy-done.4 = bf16[2048,256]{1,0:T(8,128)(2,1)} copy-done((bf16[2048,256]{1,0:T(8,128)(2,1)}, bf16[2048,256]{1,0:T(8,128)(2,1)S(1)}, u32[]{:S(2)}) %copy-start.4) | copy-done | bytes 1048600
  56.8 24.8 %pair1.1 = bf16[2048,256]{1,0:T(8,128)(2,1)} custom-call(bf16[2048,256]{1,0:T(8,128)(2,1)} %pair0.1.own, bf16[2048,256]{1,0:T(8,128)(2,1)} %copy-done.4, bf16[2112,256]{1,0:T(8,128)(2,1)} %pack1.1.sk_own, bf16[2112,256]{1,0:T(8,128)(2,1)} %copy-done), custom_call_target="tpu_custom_call" | custom-call | tf_op jit(solution)/shard_map/pair1/pallas_call | solution.py:266
Async XLA Ops:
  0.0 2.9 %copy-start.2 = (bf16[1,256,8,256]{3,2,1,0:T(8,128)(2,1)S(1)}, bf16[1,256,8,256]{3,2,1,0:T(8,128)(2,1)}, u32[]{:S(2)}) copy-start(bf16[1,256,8,256]{3,2,1,0:T(8,128)(2,1)} %param.5) | copy-start | bytes 3145732
  2.9 11.7 %collective-permute-start.1 = (bf16[2112,256]{1,0:T(8,128)(2,1)}, bf16[2112,256]{1,0:T(8,128)(2,1)S(1)}, u32[]{:S(2)}, u32[]{:S(2)}) collective-permute-start(bf16[2112,256]{1,0:T(8,128)(2,1)} %pack0.1.sk_own), channel_id=1, source_target_pairs={{0,1},{1,0},{2,3},{3,2},{4,5},{5,4},{6,7},{7,6},{8,9},{9,8},{10,11... | collective-permute-start | bytes 3244040 | tf_op jit(solution)/shard_map/ppermute | solution.py:312
  2.9 11.7 %collective-permute-start = (bf16[2048,256]{1,0:T(8,128)(2,1)S(1)}, bf16[2048,256]{1,0:T(8,128)(2,1)S(1)}, u32[]{:S(2)}, u32[]{:S(2)}) collective-permute-start(bf16[2048,256]{1,0:T(8,128)(2,1)S(1)} %bitcast.9), channel_id=1, source_target_pairs={{0,1},{1,0},{2,3},{3,2},{4,5},{5,4},{6,7},{7,6},{8,9},{9,8},{10,11... | collective-permute-start | bytes 3145736 | tf_op jit(solution)/shard_map/ppermute | solution.py:310
  6.3 36.4 %collective-permute-start.3 = (bf16[2112,256]{1,0:T(8,128)(2,1)}, bf16[2112,256]{1,0:T(8,128)(2,1)S(1)}, u32[]{:S(2)}, u32[]{:S(2)}) collective-permute-start(bf16[2112,256]{1,0:T(8,128)(2,1)} %pack1.1.sk_own), channel_id=1, source_target_pairs={{0,127},{1,2},{2,1},{3,4},{4,3},{5,6},{6,5},{7,8},{8,7},{9,10},{10... | collective-permute-start | bytes 3244040 | tf_op jit(solution)/shard_map/ppermute | solution.py:314
  14.7 1.0 %copy-start.3 = (bf16[2048,256]{1,0:T(8,128)(2,1)}, bf16[2048,256]{1,0:T(8,128)(2,1)S(1)}, u32[]{:S(2)}) copy-start(bf16[2048,256]{1,0:T(8,128)(2,1)S(1)} %collective-permute-done.recv) | copy-start | bytes 3145732
  15.6 1.0 %copy-start.1 = (bf16[2112,256]{1,0:T(8,128)(2,1)}, bf16[2112,256]{1,0:T(8,128)(2,1)S(1)}, u32[]{:S(2)}) copy-start(bf16[2112,256]{1,0:T(8,128)(2,1)S(1)} %collective-permute-done.1.sk_recv) | copy-start | bytes 3244036
  35.9 19.9 %collective-permute-start.2 = (bf16[2048,256]{1,0:T(8,128)(2,1)}, bf16[2048,256]{1,0:T(8,128)(2,1)S(1)}, u32[]{:S(2)}, u32[]{:S(2)}) collective-permute-start(bf16[2048,256]{1,0:T(8,128)(2,1)} %pair0.1.own), channel_id=1, source_target_pairs={{0,127},{1,2},{2,1},{3,4},{4,3},{5,6},{6,5},{7,8},{8,7},{9,10},{10... | collective-permute-start | bytes 3145736 | tf_op jit(solution)/shard_map/ppermute | solution.py:316
  42.6 13.2 %copy-start = (bf16[2112,256]{1,0:T(8,128)(2,1)}, bf16[2112,256]{1,0:T(8,128)(2,1)S(1)}, u32[]{:S(2)}) copy-start(bf16[2112,256]{1,0:T(8,128)(2,1)S(1)} %collective-permute-done.3.sk_recv) | copy-start | bytes 3244036
  55.9 1.0 %copy-start.4 = (bf16[2048,256]{1,0:T(8,128)(2,1)}, bf16[2048,256]{1,0:T(8,128)(2,1)S(1)}, u32[]{:S(2)}) copy-start(bf16[2048,256]{1,0:T(8,128)(2,1)S(1)} %collective-permute-done.2.recv) | copy-start | bytes 3145732

commit v2 on v1

--- a/solution.py
+++ b/solution.py
@@ -143,7 +143,7 @@
         wide[h, pl.ds(t, CHI, stride=LEVELS), :] = value[:, h * 128 : (h + 1) * 128]
 
 
-def pair_kernel(own, recv, sk_own, sk_recv, out, left, right, raw, sk, gate, y, m, s, wide, q, ab, sems, *, layer):
+def pair_kernel(own, recv, sk_own, sk_recv, out, left, right, raw, sk, gate, y, m, s, st, wide, q, ab, sems, *, layer):
     me = lax.axis_index("site")
     devices = lax.axis_size("site")
     is_left = lax.rem(me, 2) == layer
@@ -215,13 +215,19 @@
 
     lax.fori_loop(0, ROWS // step, sample, 0)
 
-    ab[:, :CHI] = dot(s[...], s[...], ((0,), (0,)))
+    unit = jnp.where(
+        lax.broadcasted_iota(jnp.int32, (CHI, CHI), 0) == lax.broadcasted_iota(jnp.int32, (CHI, CHI), 1), 1.0, 0.0
+    ).astype(BF16)
+    st[...] = dot(unit, s[...], ((1,), (1,))).astype(BF16)
+    ab[:, :CHI] = dot(st[...], s[...])
     diag_i = lax.broadcasted_iota(jnp.int32, (CHI, CHI), 0)
     diag_j = lax.broadcasted_iota(jnp.int32, (CHI, CHI), 1)
     ab[:, CHI:] = jnp.where(diag_i == diag_j, 1.0, 0.0).astype(F32)
     for o in range(0, CHI, BLOCK):
         e = o + BLOCK
         w = inverse_factor(ab[o:e, o:e])
+        for t in range(o // BLOCK * 2, o // BLOCK * 2 + 2):
+            q[:, t * CHI : (t + 1) * CHI] = dot(st[...], m[:, t * CHI : (t + 1) * CHI]).astype(BF16)
         panel = dot_split(w, ab[o:e, :])
         ab[o:e, CHI:] = panel[:, CHI:]
         if e < CHI:
@@ -249,8 +255,7 @@
     def _():
         inv = (ab[:, CHI:] * (left_scale * ROWS**-0.5)).astype(BF16)
         for t in range(LEVELS):
-            q[...] = dot(s[...], m[:, t * CHI : (t + 1) * CHI], ((0,), (0,)))
-            put_level(wide, t, dot(inv, q[...].astype(BF16)))
+            put_level(wide, t, dot(inv, q[:, t * CHI : (t + 1) * CHI]))
         if layer == 1:
 
             @pl.when(idle)
@@ -277,29 +282,19 @@
             pltpu.VMEM((CHI, GATE, CHI), BF16),
             pltpu.VMEM((ROWS, ROWS), BF16),
             pltpu.VMEM((ROWS, CHI), BF16),
+            pltpu.VMEM((CHI, ROWS), BF16),
             pltpu.VMEM((2, ROWS, 128), F32),
-            pltpu.VMEM((CHI, CHI), F32),
+            pltpu.VMEM((CHI, ROWS), BF16),
             pltpu.VMEM((CHI, 2 * CHI), F32),
             pltpu.SemaphoreType.DMA((3,)),
         ],
-        compiler_params=pltpu.CompilerParams(vmem_limit_bytes=56 << 20),
+        compiler_params=pltpu.CompilerParams(vmem_limit_bytes=32 << 20),
         name=f"pair{layer}",
     )(own, recv, sk_own, sk_recv)
 
 
-def pack_kernel(sketch, gate, out):
-    out[:ROWS, :] = sketch[...].astype(BF16)
-    out[ROWS:, :] = jnp.concatenate([gate[...]] * 4, axis=1)
-
-
 def pack(sketch, gate, layer):
-    return pl.pallas_call(
-        pack_kernel,
-        out_shape=jax.ShapeDtypeStruct((ROWS + GATE, CHI), BF16),
-        in_specs=[VMEM, VMEM],
-        out_specs=VMEM,
-        name=f"pack{layer}",
-    )(sketch, gate)
+    return jnp.concatenate([sketch.astype(BF16), jnp.concatenate([gate] * 4, axis=1)], axis=0)
 
 
 def per_device(site_tensors, first_gates, second_gates, first_sketch, second_sketch):

time: 81.9 us -> 67.8 us (0.83)
  Pallas kernels: 49.8 us -> 36.2 us
  waiting for transfers between devices: 13.2 us -> 16.5 us
  starting transfers between devices: 15.6 us -> 12.4 us
  local copies, waits for them, and re-layouts: 2.92 us -> 0.08 us
  other arithmetic: 0 us -> 2.32 us
    pallas_call x2, Pallas kernels: 44.1 us -> 36.2 us  [pair_step(): pl.pallas_call(functools.partial(pair_kernel, layer=layer), out_shape=jax...]
    pallas_call x2 -> x0, Pallas kernels: 5.75 us -> none  [pack(): pl.pallas_call(pack_kernel, out_shape=jax.ShapeDtypeStruct((ROWS + GATE,...]
    ppermute x1, starting transfers between devices: 6.72 us -> 3.27 us  [per_device(): recv = lax.ppermute(own, 'site', across)]
    ppermute x1, waiting for transfers between devices: 13.2 us -> 16.5 us  [per_device(): recv = lax.ppermute(own, 'site', across)]
    unnamed x10 -> x8, local copies, waits for them, and re-layouts: 2.92 us -> 0.08 us
    convert_element_type x0 -> x2, other arithmetic: none -> 2.08 us  [pack(): sketch.astype(BF16)]
  transfers between devices with their start and end apart: 4 -> 4, of which waited for: 1 -> 1; matrix products, arithmetic and copies ran while one was open for 0% -> 0% of each run, Pallas kernels for 27% -> 26%
where the time goes in v2:
time: 67.8 us; the launch traced here: 67.7 us
  Pallas kernels  36.2 us (53%)
  waiting for transfers between devices  16.5 us (24%)
  starting transfers between devices  12.4 us (18%)
  other arithmetic  2.32 us (3%)
    pallas_call x2, Pallas kernels, pair_step(): pl.pallas_call(functools.partial(pair_kernel, layer=layer), out_shape=jax...  36.2 us
    ppermute x1, waiting for transfers between devices, per_device(): recv = lax.ppermute(own, 'site', across)  16.5 us
    ppermute x1, starting transfers between devices, per_device(): sk1_recv = lax.ppermute(sk1, 'site', across)  8.53 us
    ppermute x1, starting transfers between devices, per_device(): recv = lax.ppermute(own, 'site', across)  3.27 us
    convert_element_type x2, other arithmetic, pack(): sketch.astype(BF16)  2.08 us
  transfers between devices with their start and end apart: 4, of which 1 were waited for; matrix products, arithmetic and copies ran while one was open for 0% of the time, Pallas kernels for 26%

profile of v2, /device:TPU:0, one launch (start us, length us, event | category | flops | bytes accessed | tf_op | source)
XLA Modules:
  0.0 67.7 jit_solution(12518412916691315017)
XLA Ops:
  0.0 0.0 copy-start.2
  0.0 0.0 copy-start
  0.0 0.0 copy-start.1
  0.0 1.9 %convert_bitcast_fusion.1 = bf16[2048,256]{1,0:T(8,128)(2,1)S(1)} fusion(s32[1,2048,256]{2,1,0:T(8,128)} %param.8), kind=kLoop, calls=%fused_computation.3 | loop fusion | flops 524288 | bytes 3145728 | tf_op jit(solution)/shard_map/convert_element_type | solution.py:297
  1.9 0.0 copy-done.2
  1.9 0.1 maximum_maximum_fusion.sk_own
  2.1 0.0 copy-start.3
  2.1 0.1 collective-permute-start.1
  2.2 0.0 copy-done
  2.2 0.5 collective-permute-start
  2.7 0.0 copy-done.1
  2.7 0.2 convert_bitcast_fusion
  2.8 0.1 copy-done.3
  2.9 0.1 maximum_maximum_fusion.1.sk_own
  3.0 8.5 %collective-permute-start.3 = (bf16[2112,256]{1,0:T(8,128)(2,1)S(1)}, bf16[2112,256]{1,0:T(8,128)(2,1)S(1)}, u32[]{:S(2)}, u32[]{:S(2)}) collective-permute-start(bf16[2112,256]{1,0:T(8,128)(2,1)S(1)} %maximum_maximum_fusion.1.sk_own), channel_id=1, source_target_pairs={{0,127},{1,2},{2,1},{3,4},{4,3},{5,6},{6,5},{7,8},{8,7},{9,10},{10... | collective-permute-start | bytes 3244040 | tf_op jit(solution)/shard_map/ppermute | solution.py:309
  11.6 0.0 collective-permute-done.recv
  11.6 0.0 collective-permute-done.1.sk_recv
  11.6 17.7 %pair0.1.own = bf16[2048,256]{1,0:T(8,128)(2,1)S(1)} custom-call(bf16[2048,256]{1,0:T(8,128)(2,1)S(1)} %bitcast.9, bf16[2048,256]{1,0:T(8,128)(2,1)S(1)} %collective-permute-done.recv, bf16[2112,256]{1,0:T(8,128)(2,1)S(1)} %maximum_maximum_fusion.sk_own, bf16[2112,256]{1,0:T(8,128)(2,1)S(1)} %collective-permute-done.1.sk_recv), custom_call_target="tpu_custom_call" | custom-call | tf_op jit(solution)/shard_map/pair0/pallas_call | solution.py:271
  29.3 3.3 %collective-permute-start.2 = (bf16[2048,256]{1,0:T(8,128)(2,1)S(1)}, bf16[2048,256]{1,0:T(8,128)(2,1)S(1)}, u32[]{:S(2)}, u32[]{:S(2)}) collective-permute-start(bf16[2048,256]{1,0:T(8,128)(2,1)S(1)} %pair0.1.own), channel_id=1, source_target_pairs={{0,127},{1,2},{2,1},{3,4},{4,3},{5,6},{6,5},{7,8},{8,7},{9,10},{10... | collective-permute-start | bytes 3145736 | tf_op jit(solution)/shard_map/ppermute | solution.py:311
  32.6 0.0 collective-permute-done.3.sk_recv
  32.6 16.5 %collective-permute-done.2.recv = bf16[2048,256]{1,0:T(8,128)(2,1)S(1)} collective-permute-done((bf16[2048,256]{1,0:T(8,128)(2,1)S(1)}, bf16[2048,256]{1,0:T(8,128)(2,1)S(1)}, u32[]{:S(2)}, u32[]{:S(2)}) %collective-permute-start.2) | collective-permute-done | bytes 1048608 | tf_op jit(solution)/shard_map/ppermute | solution.py:311
  49.0 18.5 %pair1.1 = bf16[2048,256]{1,0:T(8,128)(2,1)} custom-call(bf16[2048,256]{1,0:T(8,128)(2,1)S(1)} %pair0.1.own, bf16[2048,256]{1,0:T(8,128)(2,1)S(1)} %collective-permute-done.2.recv, bf16[2112,256]{1,0:T(8,128)(2,1)S(1)} %maximum_maximum_fusion.1.sk_own, bf16[2112,256]{1,0:T(8,128)(2,1)S(1)} %collective-permute-done.3.sk_recv), custom_call_target="tpu_custom_call" | custom-call | tf_op jit(solution)/shard_map/pair1/pallas_call | solution.py:271
Async XLA Ops:
  0.0 1.9 %copy-start.2 = (bf16[1,64,64]{2,1,0:T(8,128)(2,1)S(1)}, bf16[1,64,64]{2,1,0:T(8,128)(2,1)}, u32[]{:S(2)}) copy-start(bf16[1,64,64]{2,1,0:T(8,128)(2,1)} %param.6) | copy-start | bytes 24580
  0.0 2.2 %copy-start = (bf16[1,256,8,256]{3,2,1,0:T(8,128)(2,1)S(1)}, bf16[1,256,8,256]{3,2,1,0:T(8,128)(2,1)}, u32[]{:S(2)}) copy-start(bf16[1,256,8,256]{3,2,1,0:T(8,128)(2,1)} %param.5) | copy-start | bytes 3145732
  0.0 2.7 %copy-start.1 = (s32[1,2048,256]{2,1,0:T(8,128)S(1)}, s32[1,2048,256]{2,1,0:T(8,128)}, u32[]{:S(2)}) copy-start(s32[1,2048,256]{2,1,0:T(8,128)} %param.9) | copy-start | bytes 6291460
  2.1 0.8 %copy-start.3 = (bf16[1,64,64]{2,1,0:T(8,128)(2,1)S(1)}, bf16[1,64,64]{2,1,0:T(8,128)(2,1)}, u32[]{:S(2)}) copy-start(bf16[1,64,64]{2,1,0:T(8,128)(2,1)} %param.7) | copy-start | bytes 24580
  2.1 9.5 %collective-permute-start.1 = (bf16[2112,256]{1,0:T(8,128)(2,1)S(1)}, bf16[2112,256]{1,0:T(8,128)(2,1)S(1)}, u32[]{:S(2)}, u32[]{:S(2)}) collective-permute-start(bf16[2112,256]{1,0:T(8,128)(2,1)S(1)} %maximum_maximum_fusion.sk_own), channel_id=1, source_target_pairs={{0,1},{1,0},{2,3},{3,2},{4,5},{5,4},{6,7},{7,6},{8,9},{9,8},{10,11... | collective-permute-start | bytes 3244040 | tf_op jit(solution)/shard_map/ppermute | solution.py:307
  2.2 9.4 %collective-permute-start = (bf16[2048,256]{1,0:T(8,128)(2,1)S(1)}, bf16[2048,256]{1,0:T(8,128)(2,1)S(1)}, u32[]{:S(2)}, u32[]{:S(2)}) collective-permute-start(bf16[2048,256]{1,0:T(8,128)(2,1)S(1)} %bitcast.8), channel_id=1, source_target_pairs={{0,1},{1,0},{2,3},{3,2},{4,5},{5,4},{6,7},{7,6},{8,9},{9,8},{10,11... | collective-permute-start | bytes 3145736 | tf_op jit(solution)/shard_map/ppermute | solution.py:305
  3.0 29.6 %collective-permute-start.3 = (bf16[2112,256]{1,0:T(8,128)(2,1)S(1)}, bf16[2112,256]{1,0:T(8,128)(2,1)S(1)}, u32[]{:S(2)}, u32[]{:S(2)}) collective-permute-start(bf16[2112,256]{1,0:T(8,128)(2,1)S(1)} %maximum_maximum_fusion.1.sk_own), channel_id=1, source_target_pairs={{0,127},{1,2},{2,1},{3,4},{4,3},{5,6},{6,5},{7,8},{8,7},{9,10},{10... | collective-permute-start | bytes 3244040 | tf_op jit(solution)/shard_map/ppermute | solution.py:309
  29.3 19.7 %collective-permute-start.2 = (bf16[2048,256]{1,0:T(8,128)(2,1)S(1)}, bf16[2048,256]{1,0:T(8,128)(2,1)S(1)}, u32[]{:S(2)}, u32[]{:S(2)}) collective-permute-start(bf16[2048,256]{1,0:T(8,128)(2,1)S(1)} %pair0.1.own), channel_id=1, source_target_pairs={{0,127},{1,2},{2,1},{3,4},{4,3},{5,6},{6,5},{7,8},{8,7},{9,10},{10... | collective-permute-start | bytes 3145736 | tf_op jit(solution)/shard_map/ppermute | solution.py:311

commit v3 on v2

v3 whole, which is shorter than its diff:
```python
import jax
import jax.numpy as jnp
from jax import lax
from jax.experimental import pallas as pl
from jax.experimental.pallas import tpu as pltpu
from jax.sharding import PartitionSpec as P

F32 = jnp.float32
BF16 = jnp.bfloat16
ANY = pl.BlockSpec(memory_space=pl.ANY)
VMEM = pl.BlockSpec(memory_space=pltpu.VMEM)
CHI = 256
LEVELS = 8
ROWS = CHI * LEVELS
GATE = LEVELS * LEVELS
BLOCK = 64


def lanes_of(v, k):
    return jnp.broadcast_to(v[:, k : k + 1], (8, 128))


def row_of(v, r):
    return jnp.broadcast_to(v[r : r + 1, :], (8, 128))


def inverse_factor(diag_block):
    nb = BLOCK
    nv = nb // 8
    rows = lax.broadcasted_iota(jnp.int32, (nb, nb), 0)
    cols = lax.broadcasted_iota(jnp.int32, (nb, nb), 1)
    beside = jnp.concatenate([diag_block, jnp.where(rows == cols, 1.0, 0.0).astype(F32)], axis=1)
    v = [beside[8 * q : 8 * q + 8, :] for q in range(nv)]
    sub = lax.broadcasted_iota(jnp.int32, (8, 128), 0)
    scale = [jnp.ones((8, 128), F32)] * nv
    c = [[lanes_of(v[q], i) for q in range(nv)] for i in range(4)]
    for k in range(0, nb, 4):
        p, r = divmod(k, 8)
        last = k + 4 >= nb
        if not last:
            p2, r2 = divmod(k + 4, 8)
            ahead = [[lanes_of(v[q], k + 4 + i) for q in range(p2, nv)] for i in range(4)]
        row = [row_of(v[p], r + i) for i in range(4)]
        g = [[row_of(c[j][0], r + i) if i >= j else None for j in range(4)] for i in range(4)]
        a, b, d = g[0][0], g[1][0], g[1][1]
        det = a * d - b * b
        idet = 1.0 / det
        ia = 1.0 / a
        ad, bd, dd = a * idet, b * idet, d * idet

        def first_pair(x, y):
            return x * dd - y * bd, y * ad - x * bd

        m20, m21 = first_pair(g[2][0], g[2][1])
        m30, m31 = first_pair(g[3][0], g[3][1])
        a2 = g[2][2] - (m20 * g[2][0] + m21 * g[2][1])
        b2 = g[3][2] - (m30 * g[2][0] + m31 * g[2][1])
        d2 = g[3][3] - (m30 * g[3][0] + m31 * g[3][1])
        det2 = a2 * d2 - b2 * b2
        idet2 = 1.0 / det2
        ia2 = 1.0 / a2
        ad2, bd2, dd2 = a2 * idet2, b2 * idet2, d2 * idet2

        def panel_solve(x0, x1, x2, x3):
            y2 = x2 - (m20 * x0 + m21 * x1)
            y3 = x3 - (m30 * x0 + m31 * x1)
            h2 = y2 * dd2 - y3 * bd2
            h3 = y3 * ad2 - y2 * bd2
            u0, u1 = first_pair(x0, x1)
            return (u0 - (m20 * h2 + m30 * h3), u1 - (m21 * h2 + m31 * h3), h2, h3), y2, y3

        if not last:
            c_next = []
            for i in range(4):
                hs, _, _ = panel_solve(*[row_of(c[j][p2 - p], r2 + i) for j in range(4)])
                c_next.append(
                    [
                        ahead[i][q - p2]
                        - (
                            (c[0][q - p] * hs[0] + c[1][q - p] * hs[1])
                            + (c[2][q - p] * hs[2] + c[3][q - p] * hs[3])
                        )
                        for q in range(p2, nv)
                    ]
                )
        h, row2, row3 = panel_solve(*row)
        below = sub > r + 3
        for q in range(p, nv):
            cq = [c[j][q - p] for j in range(4)]
            if q == p:
                cq = [jnp.where(below, x, 0.0) for x in cq]
            v[q] = v[q] - ((cq[0] * h[0] + cq[1] * h[1]) + (cq[2] * h[2] + cq[3] * h[3]))
        row1 = row[1] - (b * ia) * row[0]
        row3 = row3 - (b2 * ia2) * row2
        v[p] = jnp.where(
            sub == r + 1, row1, jnp.where(sub == r + 2, row2, jnp.where(sub == r + 3, row3, v[p]))
        )
        scale[p] = jnp.where(
            sub == r,
            lax.rsqrt(a),
            jnp.where(
                sub == r + 1,
                lax.rsqrt(det * ia),
                jnp.where(sub == r + 2, lax.rsqrt(a2), jnp.where(sub == r + 3, lax.rsqrt(det2 * ia2), scale[p])),
            ),
        )
        if not last:
            c = c_next
    return jnp.concatenate([v[q] * scale[q] for q in range(nv)], axis=0)[:, nb:]


def dot(x, y, dims=((1,), (0,))):
    return lax.dot_general(x, y, (dims, ((), ())), preferred_element_type=F32)


def dot_split(x, y, dims=((1,), (0,))):
    xh = x.astype(BF16)
    xl = (x - xh.astype(F32)).astype(BF16)
    yh = y.astype(BF16)
    yl = (y - yh.astype(F32)).astype(BF16)
    return dot(xh, yh, dims) + (dot(xh, yl, dims) + dot(xl, yh, dims))


def gate_matrix(packed):
    i = lax.broadcasted_iota(jnp.int32, (GATE, GATE), 0)
    j = lax.broadcasted_iota(jnp.int32, (GATE, GATE), 1)
    swap = jnp.where(j == (i & 7) * 8 + (i >> 3), 1.0, 0.0).astype(BF16)
    g = dot(dot(swap, packed[:, :GATE]).astype(BF16), swap, ((1,), (1,))).astype(BF16)
    wide = jnp.concatenate([jnp.concatenate([g] * 4, axis=1)] * 4, axis=0)
    big_i = lax.broadcasted_iota(jnp.int32, (4 * GATE, 4 * GATE), 0)
    big_j = lax.broadcasted_iota(jnp.int32, (4 * GATE, 4 * GATE), 1)
    return jnp.where((big_i >> 6) == (big_j >> 6), wide, jnp.zeros_like(wide))


HALF = ROWS // 2
BONDS = CHI // 2
STEP = 512


def put_level(wide, t, value):
    for h in range(2):
        wide[h, pl.ds(t, CHI, stride=LEVELS), :] = value[:, h * 128 : (h + 1) * 128]


def take_slabs(wide, put):
    for h in range(2):
        for u in range(LEVELS // 2):
            pair = [wide[h, pl.ds(2 * u + e, CHI, stride=LEVELS), :] for e in range(2)]
            put(h, u, jnp.concatenate(pair, axis=1).astype(BF16))


def identity(dtype):
    i = lax.broadcasted_iota(jnp.int32, (CHI, CHI), 0)
    j = lax.broadcasted_iota(jnp.int32, (CHI, CHI), 1)
    return jnp.where(i == j, 1.0, 0.0).astype(dtype)


def two_site(lhs_of, weights, y, a0):
    for p in range(2):
        block = lhs_of(p)
        for u in range(LEVELS // 2):
            made = dot(block, weights[p, u * CHI : (u + 1) * CHI, :]).reshape(BONDS, LEVELS, CHI)
            both = jnp.concatenate([made[:, :, :128], made[:, :, 128:]], axis=1).astype(BF16)
            y[pl.ds(a0, BONDS), 16 * u : 16 * u + 16, p * 128 : (p + 1) * 128] = both


def gated(y, gate, m, rows):
    bonds = STEP // LEVELS

    def some(i, _):
        r0 = pl.multiple_of(i * STEP, STEP)
        a0 = pl.multiple_of(i * bonds, bonds)
        for j in range(bonds // 4):
            four = y[pl.ds(a0 + 4 * j, 4)].reshape(4 * GATE, CHI)
            o = dot(gate[...], four).reshape(4, LEVELS, LEVELS, CHI)
            for h in range(2):
                at = pl.multiple_of(r0 + j * 32 + h * 16, 16)
                for t in range(LEVELS):
                    m[pl.ds(at, 16), t * CHI : (t + 1) * CHI] = jnp.concatenate(
                        [o[2 * h, t], o[2 * h + 1, t]], axis=0
                    ).astype(BF16)
        return 0

    lax.fori_loop(0, rows // STEP, some, 0)


def factor(ab, alongside):
    ab[:, CHI:] = identity(F32)
    for o in range(0, CHI, BLOCK):
        e = o + BLOCK
        w = inverse_factor(ab[o:e, o:e])
        alongside(o // BLOCK)
        panel = dot_split(w, ab[o:e, :])
        ab[o:e, CHI:] = panel[:, CHI:]
        if e < CHI:
            ab[e:, :] = ab[e:, :] - dot_split(panel[:, e:CHI], panel, ((0,), (0,)))


LEFT_SCALE = LEVELS**0.5 * CHI**0.25
RIGHT_SCALE = LEFT_SCALE * ROWS**-0.5


def first_kernel(own, recv, sk_own, sk_recv, out_a, out_b, lhs, raw, wts, sk, gate, y, m, s, st, wide, q, ab, sems):
    is_left = lax.rem(lax.axis_index("site"), 2) == 0
    outs = (out_a, out_b)

    def fetch(left, right, sketch):
        return (
            pltpu.make_async_copy(right, raw, sems.at[0]),
            pltpu.make_async_copy(left.at[pl.ds(0, HALF)], lhs.at[0], sems.at[1]),
            pltpu.make_async_copy(left.at[pl.ds(HALF, HALF)], lhs.at[1], sems.at[2]),
            pltpu.make_async_copy(sketch, sk, sems.at[3]),
        )

    copies = fetch(own, recv, sk_own)

    @pl.when(is_left)
    def _():
        for copy in copies:
            copy.start()

    @pl.when(jnp.logical_not(is_left))
    def _():
        for copy in fetch(recv, own, sk_recv):
            copy.start()

    copies[0].wait()
    for h in range(2):
        wide[h] = raw[:, h * 128 : (h + 1) * 128].astype(F32)

    def put(h, u, value):
        wts[h, u * CHI : (u + 1) * CHI, :] = value

    take_slabs(wide, put)
    copies[1].wait()
    copies[2].wait()

    def product(x, _):
        two_site(lambda p: lhs[x], wts, y, pl.multiple_of(x * BONDS, BONDS))
        return 0

    lax.fori_loop(0, 2, product, 0)
    copies[3].wait()
    gate[...] = gate_matrix(sk[ROWS:, :])
    gated(y, gate, m, ROWS)

    def sample(i, _):
        r0 = pl.multiple_of(i * HALF, HALF)
        s[pl.ds(r0, HALF), :] = dot(m[pl.ds(r0, HALF), :], sk[:ROWS, :]).astype(BF16)
        return 0

    lax.fori_loop(0, 2, sample, 0)
    st[...] = dot(identity(BF16), s[...], ((1,), (1,))).astype(BF16)
    ab[:, :CHI] = dot(st[...], s[...])

    def alongside(j):
        for t in (2 * j, 2 * j + 1):
            q[:, t * CHI : (t + 1) * CHI] = dot(st[...], m[:, t * CHI : (t + 1) * CHI]).astype(BF16)

    factor(ab, alongside)

    @pl.when(is_left)
    def _():
        made = dot(s[...], (ab[:, CHI:] * LEFT_SCALE).astype(BF16), ((1,), (1,)))
        for h in range(2):
            wide[h] = made[:, h * 128 : (h + 1) * 128]

        def put_out(h, u, value):
            outs[h][u * CHI : (u + 1) * CHI, :] = value

        take_slabs(wide, put_out)

    @pl.when(jnp.logical_not(is_left))
    def _():
        inv = (ab[:, CHI:] * RIGHT_SCALE).astype(BF16)
        for t in range(LEVELS):
            put_level(wide, t, dot(inv, q[:, t * CHI : (t + 1) * CHI]))
        for x in range(2):
            for h in range(2):
                outs[x][:, h * 128 : (h + 1) * 128] = wide[h, x * HALF : (x + 1) * HALF, :].astype(BF16)


def half_pair(own_a, own_b, recv, sk_own, sk_recv, lhs, wts, sk, gate, y, m, sems, is_left):
    def fetch(left_a, left_b, right_a, right_b, sketch):
        return (
            pltpu.make_async_copy(left_a, lhs.at[0], sems.at[0]),
            pltpu.make_async_copy(left_b, lhs.at[1], sems.at[1]),
            pltpu.make_async_copy(right_a, wts.at[0], sems.at[2]),
            pltpu.make_async_copy(right_b, wts.at[1], sems.at[3]),
            pltpu.make_async_copy(sketch, sk, sems.at[4]),
        )

    copies = fetch(own_a, own_b, recv, recv, sk_own)

    @pl.when(is_left)
    def _():
        for copy in copies:
            copy.start()

    @pl.when(jnp.logical_not(is_left))
    def _():
        for copy in fetch(recv, recv, own_a, own_b, sk_recv):
            copy.start()

    for copy in copies[:4]:
        copy.wait()
    two_site(lambda p: lhs[p], wts, y, 0)
    copies[4].wait()
    gate[...] = gate_matrix(sk[ROWS:, :])
    gated(y, gate, m, HALF)


def column_half(sk, sh, h):
    for t in range(LEVELS):
        at = t * CHI + h * 128
        sh[t * 128 : (t + 1) * 128, :] = sk[at : at + 128, :]


def sampled_rows(m, sh, g):
    lanes = [m[:, t * CHI + g * 128 : t * CHI + (g + 1) * 128] for t in range(LEVELS)]
    return dot(jnp.concatenate(lanes, axis=1), sh[...])


def role():
    me = lax.axis_index("site")
    return lax.rem(me, 2) == 1, (me > 0) & (me < lax.axis_size("site") - 1)


def mid_kernel(own_a, own_b, recv, sk_own, sk_recv, acc, s0, lhs, wts, sk, sh, gate, y, m, sems):
    is_left, busy = role()

    @pl.when(busy)
    def _():
        half_pair(own_a, own_b, recv, sk_own, sk_recv, lhs, wts, sk, gate, y, m, sems, is_left)

        @pl.when(is_left)
        def _():
            column_half(sk, sh, 0)
            for g in range(2):
                acc[g * HALF : (g + 1) * HALF, :] = sampled_rows(m, sh, g)
            s0[...] = jnp.zeros_like(s0)

        @pl.when(jnp.logical_not(is_left))
        def _():
            s0[...] = dot(m[...], sk[:ROWS, :]).astype(BF16)
            turned = dot(identity(BF16), s0[...], ((1,), (1,))).astype(BF16)
            for t in range(LEVELS):
                acc[t * CHI : (t + 1) * CHI, :] = dot(turned, m[:, t * CHI : (t + 1) * CHI])


def last_kernel(
    own_a, own_b, recv, sk_own, sk_recv, acc_in, s0_in, out, lhs, wts, sk, sh, gate, y, m, acc, s, st, wide, q, ab, sems, sems_acc
):
    is_left, busy = role()
    owns = (own_a, own_b)

    @pl.when(busy)
    def _():
        get_acc = pltpu.make_async_copy(acc_in, acc, sems_acc.at[0])
        get_s0 = pltpu.make_async_copy(s0_in, s.at[pl.ds(0, HALF)], sems_acc.at[1])
        get_acc.start()
        get_s0.start()
        half_pair(own_a, own_b, recv, sk_own, sk_recv, lhs, wts, sk, gate, y, m, sems, is_left)
        get_acc.wait()
        get_s0.wait()

        @pl.when(is_left)
        def _():
            column_half(sk, sh, 1)
            for g in range(2):
                rows = slice(g * HALF, (g + 1) * HALF)
                s[rows, :] = (acc[rows, :] + sampled_rows(m, sh, g)).astype(BF16)

        @pl.when(jnp.logical_not(is_left))
        def _():
            s[HALF:, :] = dot(m[...], sk[:ROWS, :]).astype(BF16)

        st[...] = dot(identity(BF16), s[...], ((1,), (1,))).astype(BF16)
        ab[:, :CHI] = dot(st[...], s[...])

        def alongside(j):
            for t in (2 * j, 2 * j + 1):
                more = dot(st[:, HALF:], m[:, t * CHI : (t + 1) * CHI])
                q[:, t * CHI : (t + 1) * CHI] = (acc[t * CHI : (t + 1) * CHI, :] + more).astype(BF16)

        factor(ab, alongside)

        @pl.when(is_left)
        def _():
            out[...] = dot(s[...], (ab[:, CHI:] * LEFT_SCALE).astype(BF16), ((1,), (1,))).astype(BF16)

        @pl.when(jnp.logical_not(is_left))
        def _():
            inv = (ab[:, CHI:] * RIGHT_SCALE).astype(BF16)
            for t in range(LEVELS):
                put_level(wide, t, dot(inv, q[:, t * CHI : (t + 1) * CHI]))
            for h in range(2):
                out[:, h * 128 : (h + 1) * 128] = wide[h].astype(BF16)

    @pl.when(jnp.logical_not(busy))
    def _():
        for x in range(2):
            copy = pltpu.make_async_copy(owns[x], lhs.at[x], sems.at[x])
            copy.start()
            copy.wait()

        @pl.when(is_left)
        def _():
            for x in range(2):
                out[x * HALF : (x + 1) * HALF, :] = lhs[x]

        @pl.when(jnp.logical_not(is_left))
        def _():
            for h in range(2):
                for u in range(LEVELS // 2):
                    for e in range(2):
                        slab = lhs[h, u * CHI : (u + 1) * CHI, e * 128 : (e + 1) * 128].astype(F32)
                        wide[h, pl.ds(2 * u + e, CHI, stride=LEVELS), :] = slab
            for h in range(2):
                out[:, h * 128 : (h + 1) * 128] = wide[h].astype(BF16)


HALF_ARRAY = jax.ShapeDtypeStruct((HALF, CHI), BF16)
HALVES = pltpu.VMEM((2, HALF, CHI), BF16)
WHOLE = pltpu.VMEM((ROWS, CHI), BF16)
TURNED = pltpu.VMEM((CHI, ROWS), BF16)
SKETCH = pltpu.VMEM((ROWS + GATE, CHI), BF16)
GATES = pltpu.VMEM((4 * GATE, 4 * GATE), BF16)
WIDE = pltpu.VMEM((2, ROWS, 128), F32)
GRAM = pltpu.VMEM((CHI, 2 * CHI), F32)


def first_layer(own, recv, sk_own, sk_recv):
    return pl.pallas_call(
        first_kernel,
        out_shape=(HALF_ARRAY, HALF_ARRAY),
        in_specs=[ANY] * 4,
        out_specs=(VMEM, VMEM),
        scratch_shapes=[
            HALVES,
            WHOLE,
            HALVES,
            SKETCH,
            GATES,
            pltpu.VMEM((CHI, GATE, CHI), BF16),
            pltpu.VMEM((ROWS, ROWS), BF16),
            WHOLE,
            TURNED,
            WIDE,
            TURNED,
            GRAM,
            pltpu.SemaphoreType.DMA((4,)),
        ],
        compiler_params=pltpu.CompilerParams(vmem_limit_bytes=32 << 20),
        name="first",
    )(own, recv, sk_own, sk_recv)


HALF_SCRATCH = [
    HALVES,
    HALVES,
    SKETCH,
    pltpu.VMEM((HALF, CHI), BF16),
    GATES,
    pltpu.VMEM((BONDS, GATE, CHI), BF16),
    pltpu.VMEM((HALF, ROWS), BF16),
]


def second_start(own_a, own_b, recv, sk_own, sk_recv):
    return pl.pallas_call(
        mid_kernel,
        out_shape=(jax.ShapeDtypeStruct((ROWS, CHI), F32), HALF_ARRAY),
        in_specs=[ANY] * 5,
        out_specs=(VMEM, VMEM),
        scratch_shapes=[*HALF_SCRATCH, pltpu.SemaphoreType.DMA((5,))],
        compiler_params=pltpu.CompilerParams(vmem_limit_bytes=24 << 20),
        cost_estimate=pl.CostEstimate(flops=5 << 30, bytes_accessed=8 << 20, transcendentals=0),
        name="mid",
    )(own_a, own_b, recv, sk_own, sk_recv)


def second_end(own_a, own_b, recv, sk_own, sk_recv, acc, s0):
    return pl.pallas_call(
        last_kernel,
        out_shape=jax.ShapeDtypeStruct((ROWS, CHI), BF16),
        in_specs=[ANY] * 7,
        out_specs=VMEM,
        scratch_shapes=[
            *HALF_SCRATCH,
            pltpu.VMEM((ROWS, CHI), F32),
            WHOLE,
            TURNED,
            WIDE,
            TURNED,
            GRAM,
            pltpu.SemaphoreType.DMA((5,)),
            pltpu.SemaphoreType.DMA((2,)),
        ],
        compiler_params=pltpu.CompilerParams(vmem_limit_bytes=32 << 20),
        name="last",
    )(own_a, own_b, recv, sk_own, sk_recv, acc, s0)


def pack(sketch, gate):
    return jnp.concatenate([sketch.astype(BF16), jnp.concatenate([gate] * 4, axis=1)], axis=0)


def per_device(site_tensors, first_gates, second_gates, first_sketch, second_sketch):
    devices = lax.axis_size("site")
    inside = [(i, i ^ 1) for i in range(devices)]
    across = [(i, (i + 1) % devices if i % 2 else (i - 1) % devices) for i in range(devices)]
    own = site_tensors[0].reshape(ROWS, CHI)
    recv = lax.ppermute(own, "site", inside)
    sk0 = pack(first_sketch[0], first_gates[0])
    sk0_recv = lax.ppermute(sk0, "site", inside)
    sk1 = pack(second_sketch[0], second_gates[0])
    sk1_recv = lax.ppermute(sk1, "site", across)
    own_a, own_b = first_layer(own, recv, sk0, sk0_recv)
    recv_a = lax.ppermute(own_a, "site", across)
    recv_b = lax.ppermute(own_b, "site", across)
    acc, s0 = second_start(own_a, own_b, recv_a, sk1, sk1_recv)
    made = second_end(own_a, own_b, recv_b, sk1, sk1_recv, acc, s0)
    return made.reshape(1, CHI, LEVELS, CHI)


def solution(mesh):
    in_specs = (
        P("site", None, None, None),
        P("site", None, None),
        P("site", None, None),
        P("site", None, None),
        P("site", None, None),
    )
    out_specs = P("site", None, None, None)
    return jax.shard_map(
        per_device, mesh=mesh, in_specs=in_specs, out_specs=out_specs, check_vma=False
    )
```

time: 67.8 us -> 62.1 us (0.916)
  the two profiles are of different devices: /device:TPU:0 before, /device:TPU:6 now
where the time goes in v3:
time: 62.1 us; the launch traced here: 61.9 us
  Pallas kernels  39.1 us (63%)
  starting transfers between devices  13.2 us (21%)
  waiting for transfers between devices  6.87 us (11%)
  other arithmetic  2.32 us (4%)
    pallas_call x1, Pallas kernels, first_layer(): pl.pallas_call(first_kernel, out_shape=(HALF_ARRAY, HALF_ARRAY), in_specs...  17.6 us
    pallas_call x1, Pallas kernels, second_end(): pl.pallas_call(last_kernel, out_shape=jax.ShapeDtypeStruct((ROWS, CHI), B...  13.9 us
    pallas_call x1, Pallas kernels, second_start(): pl.pallas_call(mid_kernel, out_shape=(jax.ShapeDtypeStruct((ROWS, CHI), F...  7.61 us
    ppermute x1, waiting for transfers between devices, per_device(): recv_a = lax.ppermute(own_a, 'site', across)  6.86 us
    ppermute x1, starting transfers between devices, per_device(): sk1_recv = lax.ppermute(sk1, 'site', across)  6.74 us
    ppermute x1, starting transfers between devices, per_device(): recv_b = lax.ppermute(own_b, 'site', across)  4.24 us
    convert_element_type x2, other arithmetic, pack(): sketch.astype(BF16)  2.08 us
    ppermute x1, starting transfers between devices, per_device(): recv_a = lax.ppermute(own_a, 'site', across)  1.81 us
  transfers between devices with their start and end apart: 5, of which 1 were waited for; matrix products, arithmetic and copies ran while one was open for 4% of the time, Pallas kernels for 41%

profile of v3, /device:TPU:6, one launch (start us, length us, event | category | flops | bytes accessed | tf_op | source)
XLA Modules:
  0.0 61.9 jit_solution(6458989704173247714)
XLA Ops:
  0.0 0.0 copy-start.2
  0.0 0.0 copy-start.1
  0.0 0.0 collective-permute-start
  0.0 1.9 %convert_bitcast_fusion.1 = bf16[2048,256]{1,0:T(8,128)(2,1)S(1)} fusion(s32[1,2048,256]{2,1,0:T(8,128)} %param.8), kind=kLoop, calls=%fused_computation.3 | loop fusion | flops 524288 | bytes 3145728 | tf_op jit(solution)/shard_map/convert_element_type | solution.py:506
  1.9 0.0 copy-done.2
  1.9 0.1 maximum_maximum_fusion.sk_own
  2.1 0.0 copy-start.3
  2.1 0.0 copy-start
  2.1 0.4 collective-permute-start.1
  2.5 0.0 copy-done.1
  2.5 0.2 convert_bitcast_fusion
  2.7 0.1 copy-done.3
  2.8 0.1 maximum_maximum_fusion.1.sk_own
  3.0 6.7 %collective-permute-start.3 = (bf16[2112,256]{1,0:T(8,128)(2,1)S(1)}, bf16[2112,256]{1,0:T(8,128)(2,1)S(1)}, u32[]{:S(2)}, u32[]{:S(2)}) collective-permute-start(bf16[2112,256]{1,0:T(8,128)(2,1)S(1)} %maximum_maximum_fusion.1.sk_own), channel_id=1, source_target_pairs={{0,127},{1,2},{2,1},{3,4},{4,3},{5,6},{6,5},{7,8},{8,7},{9,10},{10... | collective-permute-start | bytes 3244040 | tf_op jit(solution)/shard_map/ppermute | solution.py:518
  9.7 0.0 collective-permute-done.recv
  9.7 0.0 collective-permute-done.1.sk_recv
  9.7 0.0 copy-done
  9.7 17.6 %first.1 = (bf16[1024,256]{1,0:T(8,128)(2,1)S(1)}, bf16[1024,256]{1,0:T(8,128)(2,1)S(1)}) custom-call(bf16[2048,256]{1,0:T(8,128)(2,1)S(1)} %bitcast.9, bf16[2048,256]{1,0:T(8,128)(2,1)S(1)} %collective-permute-done.recv, bf16[2112,256]{1,0:T(8,128)(2,1)S(1)} %maximum_maximum_fusion.sk_own, bf16[2112,256]{1,0:T(8,128)(2,1)S(1)} %collective-permute-done.1.sk_recv), custom_call_target="tpu_custom_call" | custom-call | tf_op jit(solution)/shard_map/first/pallas_call | solution.py:434
  27.3 1.8 %collective-permute-start.4 = (bf16[1024,256]{1,0:T(8,128)(2,1)S(1)}, bf16[1024,256]{1,0:T(8,128)(2,1)S(1)}, u32[]{:S(2)}, u32[]{:S(2)}) collective-permute-start(bf16[1024,256]{1,0:T(8,128)(2,1)S(1)} %get-tuple-element.9.own_a), channel_id=1, source_target_pairs={{0,127},{1,2},{2,1},{3,4},{4,3},{5,6},{6,5},{7,8},{8,7},{9,10},{10... | collective-permute-start | bytes 1572872 | tf_op jit(solution)/shard_map/ppermute | solution.py:520
  29.1 4.2 %collective-permute-start.2 = (bf16[1024,256]{1,0:T(8,128)(2,1)S(1)}, bf16[1024,256]{1,0:T(8,128)(2,1)S(1)}, u32[]{:S(2)}, u32[]{:S(2)}) collective-permute-start(bf16[1024,256]{1,0:T(8,128)(2,1)S(1)} %get-tuple-element.10.own_b), channel_id=1, source_target_pairs={{0,127},{1,2},{2,1},{3,4},{4,3},{5,6},{6,5},{7,8},{8,7},{9,10},{10... | collective-permute-start | bytes 1572872 | tf_op jit(solution)/shard_map/ppermute | solution.py:521
  33.4 0.0 collective-permute-done.3.sk_recv
  33.4 6.9 %collective-permute-done.4.recv = bf16[1024,256]{1,0:T(8,128)(2,1)S(1)} collective-permute-done((bf16[1024,256]{1,0:T(8,128)(2,1)S(1)}, bf16[1024,256]{1,0:T(8,128)(2,1)S(1)}, u32[]{:S(2)}, u32[]{:S(2)}) %collective-permute-start.4) | collective-permute-done | bytes 524320 | tf_op jit(solution)/shard_map/ppermute | solution.py:520
  40.2 7.6 %mid.1 = (f32[2048,256]{1,0:T(8,128)S(1)}, bf16[1024,256]{1,0:T(8,128)(2,1)S(1)}) custom-call(bf16[1024,256]{1,0:T(8,128)(2,1)S(1)} %get-tuple-element.9.own_a, bf16[1024,256]{1,0:T(8,128)(2,1)S(1)} %get-tuple-element.10.own_b, bf16[1024,256]{1,0:T(8,128)(2,1)S(1)} %collective-permute-done.4.recv, bf16[2112,256]{1,0:T(8,128)(2,1)S(1)} %maximum_maximum_fusion.1.sk_own, ...), custom_call_target="tpu_custom_call" | custom-call | flops 5368709120 | bytes 8388608 | tf_op jit(solution)/shard_map/mid/pallas_call | solution.py:471
  47.8 0.0 collective-permute-done.2.recv
  47.9 13.9 %last.1 = bf16[2048,256]{1,0:T(8,128)(2,1)} custom-call(bf16[1024,256]{1,0:T(8,128)(2,1)S(1)} %get-tuple-element.9.own_a, bf16[1024,256]{1,0:T(8,128)(2,1)S(1)} %get-tuple-element.10.own_b, bf16[1024,256]{1,0:T(8,128)(2,1)S(1)} %collective-permute-done.2.recv, bf16[2112,256]{1,0:T(8,128)(2,1)S(1)} %maximum_maximum_fusion.1.sk_own, ...), custom_call_target="tpu_custom_call" | custom-call | tf_op jit(solution)/shard_map/last/pallas_call | solution.py:484
Async XLA Ops:
  0.0 1.9 %copy-start.2 = (bf16[1,64,64]{2,1,0:T(8,128)(2,1)S(1)}, bf16[1,64,64]{2,1,0:T(8,128)(2,1)}, u32[]{:S(2)}) copy-start(bf16[1,64,64]{2,1,0:T(8,128)(2,1)} %param.6) | copy-start | bytes 24580
  0.0 2.5 %copy-start.1 = (s32[1,2048,256]{2,1,0:T(8,128)S(1)}, s32[1,2048,256]{2,1,0:T(8,128)}, u32[]{:S(2)}) copy-start(s32[1,2048,256]{2,1,0:T(8,128)} %param.9) | copy-start | bytes 6291460
  0.0 9.7 %collective-permute-start = (bf16[2048,256]{1,0:T(8,128)(2,1)}, bf16[2048,256]{1,0:T(8,128)(2,1)S(1)}, u32[]{:S(2)}, u32[]{:S(2)}) collective-permute-start(bf16[2048,256]{1,0:T(8,128)(2,1)} %bitcast.8), channel_id=1, source_target_pairs={{0,1},{1,0},{2,3},{3,2},{4,5},{5,4},{6,7},{7,6},{8,9},{9,8},{10,11... | collective-permute-start | bytes 3145736 | tf_op jit(solution)/shard_map/ppermute | solution.py:514
  2.1 0.8 %copy-start.3 = (bf16[1,64,64]{2,1,0:T(8,128)(2,1)S(1)}, bf16[1,64,64]{2,1,0:T(8,128)(2,1)}, u32[]{:S(2)}) copy-start(bf16[1,64,64]{2,1,0:T(8,128)(2,1)} %param.7) | copy-start | bytes 24580
  2.1 7.6 %copy-start = (bf16[1,256,8,256]{3,2,1,0:T(8,128)(2,1)S(1)}, bf16[1,256,8,256]{3,2,1,0:T(8,128)(2,1)}, u32[]{:S(2)}) copy-start(bf16[1,256,8,256]{3,2,1,0:T(8,128)(2,1)} %param.5) | copy-start | bytes 3145732
  2.1 7.6 %collective-permute-start.1 = (bf16[2112,256]{1,0:T(8,128)(2,1)S(1)}, bf16[2112,256]{1,0:T(8,128)(2,1)S(1)}, u32[]{:S(2)}, u32[]{:S(2)}) collective-permute-start(bf16[2112,256]{1,0:T(8,128)(2,1)S(1)} %maximum_maximum_fusion.sk_own), channel_id=1, source_target_pairs={{0,1},{1,0},{2,3},{3,2},{4,5},{5,4},{6,7},{7,6},{8,9},{9,8},{10,11... | collective-permute-start | bytes 3244040 | tf_op jit(solution)/shard_map/ppermute | solution.py:516
  3.0 30.4 %collective-permute-start.3 = (bf16[2112,256]{1,0:T(8,128)(2,1)S(1)}, bf16[2112,256]{1,0:T(8,128)(2,1)S(1)}, u32[]{:S(2)}, u32[]{:S(2)}) collective-permute-start(bf16[2112,256]{1,0:T(8,128)(2,1)S(1)} %maximum_maximum_fusion.1.sk_own), channel_id=1, source_target_pairs={{0,127},{1,2},{2,1},{3,4},{4,3},{5,6},{6,5},{7,8},{8,7},{9,10},{10... | collective-permute-start | bytes 3244040 | tf_op jit(solution)/shard_map/ppermute | solution.py:518
  27.3 12.9 %collective-permute-start.4 = (bf16[1024,256]{1,0:T(8,128)(2,1)S(1)}, bf16[1024,256]{1,0:T(8,128)(2,1)S(1)}, u32[]{:S(2)}, u32[]{:S(2)}) collective-permute-start(bf16[1024,256]{1,0:T(8,128)(2,1)S(1)} %get-tuple-element.9.own_a), channel_id=1, source_target_pairs={{0,127},{1,2},{2,1},{3,4},{4,3},{5,6},{6,5},{7,8},{8,7},{9,10},{10... | collective-permute-start | bytes 1572872 | tf_op jit(solution)/shard_map/ppermute | solution.py:520
  29.1 18.7 %collective-permute-start.2 = (bf16[1024,256]{1,0:T(8,128)(2,1)S(1)}, bf16[1024,256]{1,0:T(8,128)(2,1)S(1)}, u32[]{:S(2)}, u32[]{:S(2)}) collective-permute-start(bf16[1024,256]{1,0:T(8,128)(2,1)S(1)} %get-tuple-element.10.own_b), channel_id=1, source_target_pairs={{0,127},{1,2},{2,1},{3,4},{4,3},{5,6},{6,5},{7,8},{8,7},{9,10},{10... | collective-permute-start | bytes 1572872 | tf_op jit(solution)/shard_map/ppermute | solution.py:521

commit v4 on v3

--- a/solution.py
+++ b/solution.py
@@ -45,51 +45,55 @@
         a, b, d = g[0][0], g[1][0], g[1][1]
         det = a * d - b * b
         idet = 1.0 / det
-        ia = 1.0 / a
-        ad, bd, dd = a * idet, b * idet, d * idet
-
-        def first_pair(x, y):
-            return x * dd - y * bd, y * ad - x * bd
-
-        m20, m21 = first_pair(g[2][0], g[2][1])
-        m30, m31 = first_pair(g[3][0], g[3][1])
-        a2 = g[2][2] - (m20 * g[2][0] + m21 * g[2][1])
-        b2 = g[3][2] - (m30 * g[2][0] + m31 * g[2][1])
-        d2 = g[3][3] - (m30 * g[3][0] + m31 * g[3][1])
+
+        def adjugate(x, y):
+            return x * d - y * b, y * a - x * b
+
+        n20, n21 = adjugate(g[2][0], g[2][1])
+        n30, n31 = adjugate(g[3][0], g[3][1])
+        a2 = g[2][2] - (g[2][0] * n20 + g[2][1] * n21) * idet
+        b2 = g[3][2] - (g[3][0] * n20 + g[3][1] * n21) * idet
+        d2 = g[3][3] - (g[3][0] * n30 + g[3][1] * n31) * idet
         det2 = a2 * d2 - b2 * b2
         idet2 = 1.0 / det2
-        ia2 = 1.0 / a2
-        ad2, bd2, dd2 = a2 * idet2, b2 * idet2, d2 * idet2
+        m20, m21, m30, m31 = n20 * idet, n21 * idet, n30 * idet, n31 * idet
 
         def panel_solve(x0, x1, x2, x3):
+            u0, u1 = adjugate(x0, x1)
             y2 = x2 - (m20 * x0 + m21 * x1)
             y3 = x3 - (m30 * x0 + m31 * x1)
-            h2 = y2 * dd2 - y3 * bd2
-            h3 = y3 * ad2 - y2 * bd2
-            u0, u1 = first_pair(x0, x1)
-            return (u0 - (m20 * h2 + m30 * h3), u1 - (m21 * h2 + m31 * h3), h2, h3), y2, y3
-
+            return u0 * idet, u1 * idet, (y2 * d2 - y3 * b2) * idet2, (y3 * a2 - y2 * b2) * idet2, y2, y3
+
+        ce = [
+            (
+                c[0][q - p],
+                c[1][q - p],
+                c[2][q - p] - (m20 * c[0][q - p] + m21 * c[1][q - p]),
+                c[3][q - p] - (m30 * c[0][q - p] + m31 * c[1][q - p]),
+            )
+            for q in range(p, nv)
+        ]
         if not last:
+            across = panel_solve(*[c[j][p2 - p] for j in range(4)])[:4]
             c_next = []
             for i in range(4):
-                hs, _, _ = panel_solve(*[row_of(c[j][p2 - p], r2 + i) for j in range(4)])
+                hs = [row_of(x, r2 + i) for x in across]
                 c_next.append(
                     [
-                        ahead[i][q - p2]
-                        - (
-                            (c[0][q - p] * hs[0] + c[1][q - p] * hs[1])
-                            + (c[2][q - p] * hs[2] + c[3][q - p] * hs[3])
-                        )
+                        (ahead[i][q - p2] - (ce[q - p][0] * hs[0] + ce[q - p][1] * hs[1]))
+                        - (ce[q - p][2] * hs[2] + ce[q - p][3] * hs[3])
                         for q in range(p2, nv)
                     ]
                 )
-        h, row2, row3 = panel_solve(*row)
+        u0, u1, h2, h3, row2, row3 = panel_solve(*row)
         below = sub > r + 3
         for q in range(p, nv):
-            cq = [c[j][q - p] for j in range(4)]
+            cq = ce[q - p]
             if q == p:
                 cq = [jnp.where(below, x, 0.0) for x in cq]
-            v[q] = v[q] - ((cq[0] * h[0] + cq[1] * h[1]) + (cq[2] * h[2] + cq[3] * h[3]))
+            v[q] = (v[q] - (cq[0] * u0 + cq[1] * u1)) - (cq[2] * h2 + cq[3] * h3)
+        ia = 1.0 / a
+        ia2 = 1.0 / a2
         row1 = row[1] - (b * ia) * row[0]
         row3 = row3 - (b2 * ia2) * row2
         v[p] = jnp.where(
@@ -106,7 +110,7 @@
         )
         if not last:
             c = c_next
-    return jnp.concatenate([v[q] * scale[q] for q in range(nv)], axis=0)[:, nb:]
+    return jnp.concatenate([v[q] * scale[q] for q in range(nv)], axis=0)
 
 
 def dot(x, y, dims=((1,), (0,))):
@@ -185,15 +189,33 @@
 
 
 def factor(ab, alongside):
-    ab[:, CHI:] = identity(F32)
+    unit = identity(F32)
+    gram = ab[:, :CHI]
+    largest = jnp.max(gram * unit, keepdims=True)
+    ab[:, :CHI] = gram * (1.0 / largest)
+    ab[:, CHI:] = unit
+    lane = lax.broadcasted_iota(jnp.int32, (BLOCK, 128), 1)
+    none = jnp.zeros((BLOCK, 2 * CHI), F32)
+    block = ab[:BLOCK, :BLOCK]
     for o in range(0, CHI, BLOCK):
         e = o + BLOCK
-        w = inverse_factor(ab[o:e, o:e])
+        uw = inverse_factor(block)
         alongside(o // BLOCK)
-        panel = dot_split(w, ab[o:e, :])
+        panel = dot_split(uw, jnp.concatenate([none, ab[o:e, :]], axis=0))
         ab[o:e, CHI:] = panel[:, CHI:]
         if e < CHI:
-            ab[e:, :] = ab[e:, :] - dot_split(panel[:, e:CHI], panel, ((0,), (0,)))
+            tile = o // 128 * 128
+            if o == tile:
+                w = jnp.concatenate([uw[:, BLOCK:], jnp.zeros((BLOCK, BLOCK), F32)], axis=1)
+            else:
+                w = jnp.where(lane >= BLOCK, uw, 0.0)
+            turned = dot_split(ab[e:, tile : tile + 128], w, ((1,), (1,)))
+            top = ab[e : e + BLOCK, :] - dot_split(turned[:BLOCK], panel)
+            block = top[:, e : e + BLOCK]
+            ab[e : e + BLOCK, :] = top
+            if e + BLOCK < CHI:
+                ab[e + BLOCK :, :] = ab[e + BLOCK :, :] - dot_split(turned[BLOCK:], panel)
+    return lax.rsqrt(largest)
 
 
 LEFT_SCALE = LEVELS**0.5 * CHI**0.25
@@ -257,11 +279,11 @@
         for t in (2 * j, 2 * j + 1):
             q[:, t * CHI : (t + 1) * CHI] = dot(st[...], m[:, t * CHI : (t + 1) * CHI]).astype(BF16)
 
-    factor(ab, alongside)
+    unscale = factor(ab, alongside)
 
     @pl.when(is_left)
     def _():
-        made = dot(s[...], (ab[:, CHI:] * LEFT_SCALE).astype(BF16), ((1,), (1,)))
+        made = dot(s[...], (ab[:, CHI:] * (unscale * LEFT_SCALE)).astype(BF16), ((1,), (1,)))
         for h in range(2):
             wide[h] = made[:, h * 128 : (h + 1) * 128]
 
@@ -272,7 +294,7 @@
 
     @pl.when(jnp.logical_not(is_left))
     def _():
-        inv = (ab[:, CHI:] * RIGHT_SCALE).astype(BF16)
+        inv = (ab[:, CHI:] * (unscale * RIGHT_SCALE)).astype(BF16)
         for t in range(LEVELS):
             put_level(wide, t, dot(inv, q[:, t * CHI : (t + 1) * CHI]))
         for x in range(2):
@@ -326,7 +348,7 @@
     return lax.rem(me, 2) == 1, (me > 0) & (me < lax.axis_size("site") - 1)
 
 
-def mid_kernel(own_a, own_b, recv, sk_own, sk_recv, acc, s0, lhs, wts, sk, sh, gate, y, m, sems):
+def mid_kernel(own_a, own_b, recv, sk_own, sk_recv, acc, s0, m, lhs, wts, sk, sh, gate, y, sems):
     is_left, busy = role()
 
     @pl.when(busy)
@@ -343,26 +365,17 @@
         @pl.when(jnp.logical_not(is_left))
         def _():
             s0[...] = dot(m[...], sk[:ROWS, :]).astype(BF16)
-            turned = dot(identity(BF16), s0[...], ((1,), (1,))).astype(BF16)
-            for t in range(LEVELS):
-                acc[t * CHI : (t + 1) * CHI, :] = dot(turned, m[:, t * CHI : (t + 1) * CHI])
 
 
 def last_kernel(
-    own_a, own_b, recv, sk_own, sk_recv, acc_in, s0_in, out, lhs, wts, sk, sh, gate, y, m, acc, s, st, wide, q, ab, sems, sems_acc
+    own_a, own_b, recv, sk_own, sk_recv, acc, s0, m0, out, lhs, wts, sk, sh, gate, y, m, s, st, wide, q, ab, sems
 ):
     is_left, busy = role()
     owns = (own_a, own_b)
 
     @pl.when(busy)
     def _():
-        get_acc = pltpu.make_async_copy(acc_in, acc, sems_acc.at[0])
-        get_s0 = pltpu.make_async_copy(s0_in, s.at[pl.ds(0, HALF)], sems_acc.at[1])
-        get_acc.start()
-        get_s0.start()
         half_pair(own_a, own_b, recv, sk_own, sk_recv, lhs, wts, sk, gate, y, m, sems, is_left)
-        get_acc.wait()
-        get_s0.wait()
 
         @pl.when(is_left)
         def _():
@@ -373,6 +386,7 @@
 
         @pl.when(jnp.logical_not(is_left))
         def _():
+            s[:HALF, :] = s0[...]
             s[HALF:, :] = dot(m[...], sk[:ROWS, :]).astype(BF16)
 
         st[...] = dot(identity(BF16), s[...], ((1,), (1,))).astype(BF16)
@@ -380,18 +394,19 @@
 
         def alongside(j):
             for t in (2 * j, 2 * j + 1):
-                more = dot(st[:, HALF:], m[:, t * CHI : (t + 1) * CHI])
-                q[:, t * CHI : (t + 1) * CHI] = (acc[t * CHI : (t + 1) * CHI, :] + more).astype(BF16)
-
-        factor(ab, alongside)
+                columns = slice(t * CHI, (t + 1) * CHI)
+                made = dot(st[:, :HALF], m0[:, columns]) + dot(st[:, HALF:], m[:, columns])
+                q[:, columns] = made.astype(BF16)
+
+        unscale = factor(ab, alongside)
 
         @pl.when(is_left)
         def _():
-            out[...] = dot(s[...], (ab[:, CHI:] * LEFT_SCALE).astype(BF16), ((1,), (1,))).astype(BF16)
+            out[...] = dot(s[...], (ab[:, CHI:] * (unscale * LEFT_SCALE)).astype(BF16), ((1,), (1,))).astype(BF16)
 
         @pl.when(jnp.logical_not(is_left))
         def _():
-            inv = (ab[:, CHI:] * RIGHT_SCALE).astype(BF16)
+            inv = (ab[:, CHI:] * (unscale * RIGHT_SCALE)).astype(BF16)
             for t in range(LEVELS):
                 put_level(wide, t, dot(inv, q[:, t * CHI : (t + 1) * CHI]))
             for h in range(2):
@@ -463,16 +478,19 @@
     pltpu.VMEM((HALF, CHI), BF16),
     GATES,
     pltpu.VMEM((BONDS, GATE, CHI), BF16),
-    pltpu.VMEM((HALF, ROWS), BF16),
 ]
 
 
 def second_start(own_a, own_b, recv, sk_own, sk_recv):
     return pl.pallas_call(
         mid_kernel,
-        out_shape=(jax.ShapeDtypeStruct((ROWS, CHI), F32), HALF_ARRAY),
+        out_shape=(
+            jax.ShapeDtypeStruct((ROWS, CHI), F32),
+            HALF_ARRAY,
+            jax.ShapeDtypeStruct((HALF, ROWS), BF16),
+        ),
         in_specs=[ANY] * 5,
-        out_specs=(VMEM, VMEM),
+        out_specs=(VMEM, VMEM, VMEM),
         scratch_shapes=[*HALF_SCRATCH, pltpu.SemaphoreType.DMA((5,))],
         compiler_params=pltpu.CompilerParams(vmem_limit_bytes=24 << 20),
         cost_estimate=pl.CostEstimate(flops=5 << 30, bytes_accessed=8 << 20, transcendentals=0),
@@ -480,26 +498,25 @@
     )(own_a, own_b, recv, sk_own, sk_recv)
 
 
-def second_end(own_a, own_b, recv, sk_own, sk_recv, acc, s0):
+def second_end(own_a, own_b, recv, sk_own, sk_recv, acc, s0, m0):
     return pl.pallas_call(
         last_kernel,
         out_shape=jax.ShapeDtypeStruct((ROWS, CHI), BF16),
-        in_specs=[ANY] * 7,
+        in_specs=[*[ANY] * 5, VMEM, VMEM, VMEM],
         out_specs=VMEM,
         scratch_shapes=[
             *HALF_SCRATCH,
-            pltpu.VMEM((ROWS, CHI), F32),
+            pltpu.VMEM((HALF, ROWS), BF16),
             WHOLE,
             TURNED,
             WIDE,
             TURNED,
             GRAM,
             pltpu.SemaphoreType.DMA((5,)),
-            pltpu.SemaphoreType.DMA((2,)),
         ],
         compiler_params=pltpu.CompilerParams(vmem_limit_bytes=32 << 20),
         name="last",
-    )(own_a, own_b, recv, sk_own, sk_recv, acc, s0)
+    )(own_a, own_b, recv, sk_own, sk_recv, acc, s0, m0)
 
 
 def pack(sketch, gate):
@@ -519,8 +536,8 @@
     own_a, own_b = first_layer(own, recv, sk0, sk0_recv)
     recv_a = lax.ppermute(own_a, "site", across)
     recv_b = lax.ppermute(own_b, "site", across)
-    acc, s0 = second_start(own_a, own_b, recv_a, sk1, sk1_recv)
-    made = second_end(own_a, own_b, recv_b, sk1, sk1_recv, acc, s0)
+    acc, s0, m0 = second_start(own_a, own_b, recv_a, sk1, sk1_recv)
+    made = second_end(own_a, own_b, recv_b, sk1, sk1_recv, acc, s0, m0)
     return made.reshape(1, CHI, LEVELS, CHI)
 
 

time: 62.1 us -> 58.5 us (0.942)
  Pallas kernels: 39.1 us -> 34.6 us
  waiting for transfers between devices: 6.87 us -> 7.88 us
    pallas_call x1, Pallas kernels: 7.61 us -> 4.59 us  [second_start(): pl.pallas_call(mid_kernel, out_shape=(jax.ShapeDtypeStruct((ROWS, CHI), F...]
    ppermute x1, waiting for transfers between devices: 0.01 us -> 1.02 us  [per_device(): recv_b = lax.ppermute(own_b, 'site', across)]
    pallas_call x1, Pallas kernels: 17.6 us -> 16.8 us  [first_layer(): pl.pallas_call(first_kernel, out_shape=(HALF_ARRAY, HALF_ARRAY), in_specs...]
    pallas_call x1, Pallas kernels: 13.9 us -> 13.2 us  [second_end(): pl.pallas_call(last_kernel, out_shape=jax.ShapeDtypeStruct((ROWS, CHI), B...]
  transfers between devices with their start and end apart: 5 -> 5, of which waited for: 1 -> 2; matrix products, arithmetic and copies ran while one was open for 4% -> 4% of each run, Pallas kernels for 41% -> 37%
where the time goes in v4:
time: 58.5 us; the launch traced here: 58.4 us
  Pallas kernels  34.6 us (59%)
  starting transfers between devices  13.2 us (23%)
  waiting for transfers between devices  7.88 us (13%)
  other arithmetic  2.36 us (4%)
    pallas_call x1, Pallas kernels, first_layer(): pl.pallas_call(first_kernel, out_shape=(HALF_ARRAY, HALF_ARRAY), in_specs...  16.8 us
    pallas_call x1, Pallas kernels, second_end(): pl.pallas_call(last_kernel, out_shape=jax.ShapeDtypeStruct((ROWS, CHI), B...  13.2 us
    ppermute x1, waiting for transfers between devices, per_device(): recv_a = lax.ppermute(own_a, 'site', across)  6.86 us
    ppermute x1, starting transfers between devices, per_device(): sk1_recv = lax.ppermute(sk1, 'site', across)  6.74 us
    pallas_call x1, Pallas kernels, second_start(): pl.pallas_call(mid_kernel, out_shape=(jax.ShapeDtypeStruct((ROWS, CHI), F...  4.59 us
    ppermute x1, starting transfers between devices, per_device(): recv_b = lax.ppermute(own_b, 'site', across)  4.14 us
    convert_element_type x2, other arithmetic, pack(): sketch.astype(BF16)  2.12 us
    ppermute x1, starting transfers between devices, per_device(): recv_a = lax.ppermute(own_a, 'site', across)  1.9 us
  transfers between devices with their start and end apart: 5, of which 2 were waited for; matrix products, arithmetic and copies ran while one was open for 4% of the time, Pallas kernels for 37%

profile of v4, /device:TPU:6, one launch (start us, length us, event | category | flops | bytes accessed | tf_op | source)
XLA Modules:
  0.0 58.4 jit_solution(5374663812019483074)
XLA Ops:
  0.0 0.0 copy-start.2
  0.0 0.0 copy-start.1
  0.0 0.0 collective-permute-start
  0.0 1.9 %convert_bitcast_fusion.1 = bf16[2048,256]{1,0:T(8,128)(2,1)S(1)} fusion(s32[1,2048,256]{2,1,0:T(8,128)} %param.8), kind=kLoop, calls=%fused_computation.3 | loop fusion | flops 524288 | bytes 3145728 | tf_op jit(solution)/shard_map/convert_element_type | solution.py:523
  1.9 0.0 copy-done.2
  1.9 0.1 maximum_maximum_fusion.sk_own
  2.1 0.0 copy-start.3
  2.1 0.0 copy-start
  2.1 0.4 collective-permute-start.1
  2.5 0.0 copy-done.1
  2.5 0.2 convert_bitcast_fusion
  2.7 0.1 copy-done.3
  2.8 0.1 maximum_maximum_fusion.1.sk_own
  3.0 6.7 %collective-permute-start.3 = (bf16[2112,256]{1,0:T(8,128)(2,1)S(1)}, bf16[2112,256]{1,0:T(8,128)(2,1)S(1)}, u32[]{:S(2)}, u32[]{:S(2)}) collective-permute-start(bf16[2112,256]{1,0:T(8,128)(2,1)S(1)} %maximum_maximum_fusion.1.sk_own), channel_id=1, source_target_pairs={{0,127},{1,2},{2,1},{3,4},{4,3},{5,6},{6,5},{7,8},{8,7},{9,10},{10... | collective-permute-start | bytes 3244040 | tf_op jit(solution)/shard_map/ppermute | solution.py:535
  9.7 0.0 collective-permute-done.recv
  9.7 0.0 collective-permute-done.1.sk_recv
  9.7 0.0 copy-done
  9.7 16.8 %first.1 = (bf16[1024,256]{1,0:T(8,128)(2,1)S(1)}, bf16[1024,256]{1,0:T(8,128)(2,1)S(1)}) custom-call(bf16[2048,256]{1,0:T(8,128)(2,1)S(1)} %bitcast.9, bf16[2048,256]{1,0:T(8,128)(2,1)S(1)} %collective-permute-done.recv, bf16[2112,256]{1,0:T(8,128)(2,1)S(1)} %maximum_maximum_fusion.sk_own, bf16[2112,256]{1,0:T(8,128)(2,1)S(1)} %collective-permute-done.1.sk_recv), custom_call_target="tpu_custom_call" | custom-call | tf_op jit(solution)/shard_map/first/pallas_call | solution.py:449
  26.5 1.9 %collective-permute-start.4 = (bf16[1024,256]{1,0:T(8,128)(2,1)S(1)}, bf16[1024,256]{1,0:T(8,128)(2,1)S(1)}, u32[]{:S(2)}, u32[]{:S(2)}) collective-permute-start(bf16[1024,256]{1,0:T(8,128)(2,1)S(1)} %get-tuple-element.10.own_a), channel_id=1, source_target_pairs={{0,127},{1,2},{2,1},{3,4},{4,3},{5,6},{6,5},{7,8},{8,7},{9,10},{10... | collective-permute-start | bytes 1572872 | tf_op jit(solution)/shard_map/ppermute | solution.py:537
  28.4 4.1 %collective-permute-start.2 = (bf16[1024,256]{1,0:T(8,128)(2,1)S(1)}, bf16[1024,256]{1,0:T(8,128)(2,1)S(1)}, u32[]{:S(2)}, u32[]{:S(2)}) collective-permute-start(bf16[1024,256]{1,0:T(8,128)(2,1)S(1)} %get-tuple-element.11.own_b), channel_id=1, source_target_pairs={{0,127},{1,2},{2,1},{3,4},{4,3},{5,6},{6,5},{7,8},{8,7},{9,10},{10... | collective-permute-start | bytes 1572872 | tf_op jit(solution)/shard_map/ppermute | solution.py:538
  32.6 0.0 collective-permute-done.3.sk_recv
  32.6 6.9 %collective-permute-done.4.recv = bf16[1024,256]{1,0:T(8,128)(2,1)S(1)} collective-permute-done((bf16[1024,256]{1,0:T(8,128)(2,1)S(1)}, bf16[1024,256]{1,0:T(8,128)(2,1)S(1)}, u32[]{:S(2)}, u32[]{:S(2)}) %collective-permute-start.4) | collective-permute-done | bytes 524320 | tf_op jit(solution)/shard_map/ppermute | solution.py:537
  39.4 4.6 %mid.1 = (f32[2048,256]{1,0:T(8,128)S(1)}, bf16[1024,256]{1,0:T(8,128)(2,1)S(1)}, bf16[1024,2048]{1,0:T(8,128)(2,1)S(1)}) custom-call(bf16[1024,256]{1,0:T(8,128)(2,1)S(1)} %get-tuple-element.10.own_a, bf16[1024,256]{1,0:T(8,128)(2,1)S(1)} %get-tuple-element.11.own_b, bf16[1024,256]{1,0:T(8,128)(2,1)S(1)} %collective-permute-done.4.recv, ...), custom_call_target="tpu_custom_call" | custom-call | flops 5368709120 | bytes 8388608 | tf_op jit(solution)/shard_map/mid/pallas_call | solution.py:485
  44.0 1.0 %collective-permute-done.2.recv = bf16[1024,256]{1,0:T(8,128)(2,1)S(1)} collective-permute-done((bf16[1024,256]{1,0:T(8,128)(2,1)S(1)}, bf16[1024,256]{1,0:T(8,128)(2,1)S(1)}, u32[]{:S(2)}, u32[]{:S(2)}) %collective-permute-start.2) | collective-permute-done | bytes 524320 | tf_op jit(solution)/shard_map/ppermute | solution.py:538
  45.0 13.2 %last.1 = bf16[2048,256]{1,0:T(8,128)(2,1)} custom-call(bf16[1024,256]{1,0:T(8,128)(2,1)S(1)} %get-tuple-element.10.own_a, bf16[1024,256]{1,0:T(8,128)(2,1)S(1)} %get-tuple-element.11.own_b, bf16[1024,256]{1,0:T(8,128)(2,1)S(1)} %collective-permute-done.2.recv, bf16[2112,256]{1,0:T(8,128)(2,1)S(1)} %maximum_maximum_fusion.1.sk_own, ...), custom_call_target="tpu_custom_call" | custom-call | tf_op jit(solution)/shard_map/last/pallas_call | solution.py:502
Async XLA Ops:
  0.0 1.9 %copy-start.2 = (bf16[1,64,64]{2,1,0:T(8,128)(2,1)S(1)}, bf16[1,64,64]{2,1,0:T(8,128)(2,1)}, u32[]{:S(2)}) copy-start(bf16[1,64,64]{2,1,0:T(8,128)(2,1)} %param.6) | copy-start | bytes 24580
  0.0 2.5 %copy-start.1 = (s32[1,2048,256]{2,1,0:T(8,128)S(1)}, s32[1,2048,256]{2,1,0:T(8,128)}, u32[]{:S(2)}) copy-start(s32[1,2048,256]{2,1,0:T(8,128)} %param.9) | copy-start | bytes 6291460
  0.0 9.7 %collective-permute-start = (bf16[2048,256]{1,0:T(8,128)(2,1)}, bf16[2048,256]{1,0:T(8,128)(2,1)S(1)}, u32[]{:S(2)}, u32[]{:S(2)}) collective-permute-start(bf16[2048,256]{1,0:T(8,128)(2,1)} %bitcast.8), channel_id=1, source_target_pairs={{0,1},{1,0},{2,3},{3,2},{4,5},{5,4},{6,7},{7,6},{8,9},{9,8},{10,11... | collective-permute-start | bytes 3145736 | tf_op jit(solution)/shard_map/ppermute | solution.py:531
  2.1 0.8 %copy-start.3 = (bf16[1,64,64]{2,1,0:T(8,128)(2,1)S(1)}, bf16[1,64,64]{2,1,0:T(8,128)(2,1)}, u32[]{:S(2)}) copy-start(bf16[1,64,64]{2,1,0:T(8,128)(2,1)} %param.7) | copy-start | bytes 24580
  2.1 7.6 %copy-start = (bf16[1,256,8,256]{3,2,1,0:T(8,128)(2,1)S(1)}, bf16[1,256,8,256]{3,2,1,0:T(8,128)(2,1)}, u32[]{:S(2)}) copy-start(bf16[1,256,8,256]{3,2,1,0:T(8,128)(2,1)} %param.5) | copy-start | bytes 3145732
  2.1 7.6 %collective-permute-start.1 = (bf16[2112,256]{1,0:T(8,128)(2,1)S(1)}, bf16[2112,256]{1,0:T(8,128)(2,1)S(1)}, u32[]{:S(2)}, u32[]{:S(2)}) collective-permute-start(bf16[2112,256]{1,0:T(8,128)(2,1)S(1)} %maximum_maximum_fusion.sk_own), channel_id=1, source_target_pairs={{0,1},{1,0},{2,3},{3,2},{4,5},{5,4},{6,7},{7,6},{8,9},{9,8},{10,11... | collective-permute-start | bytes 3244040 | tf_op jit(solution)/shard_map/ppermute | solution.py:533
  3.0 29.6 %collective-permute-start.3 = (bf16[2112,256]{1,0:T(8,128)(2,1)S(1)}, bf16[2112,256]{1,0:T(8,128)(2,1)S(1)}, u32[]{:S(2)}, u32[]{:S(2)}) collective-permute-start(bf16[2112,256]{1,0:T(8,128)(2,1)S(1)} %maximum_maximum_fusion.1.sk_own), channel_id=1, source_target_pairs={{0,127},{1,2},{2,1},{3,4},{4,3},{5,6},{6,5},{7,8},{8,7},{9,10},{10... | collective-permute-start | bytes 3244040 | tf_op jit(solution)/shard_map/ppermute | solution.py:535
  26.5 12.9 %collective-permute-start.4 = (bf16[1024,256]{1,0:T(8,128)(2,1)S(1)}, bf16[1024,256]{1,0:T(8,128)(2,1)S(1)}, u32[]{:S(2)}, u32[]{:S(2)}) collective-permute-start(bf16[1024,256]{1,0:T(8,128)(2,1)S(1)} %get-tuple-element.10.own_a), channel_id=1, source_target_pairs={{0,127},{1,2},{2,1},{3,4},{4,3},{5,6},{6,5},{7,8},{8,7},{9,10},{10... | collective-permute-start | bytes 1572872 | tf_op jit(solution)/shard_map/ppermute | solution.py:537
  28.4 16.6 %collective-permute-start.2 = (bf16[1024,256]{1,0:T(8,128)(2,1)S(1)}, bf16[1024,256]{1,0:T(8,128)(2,1)S(1)}, u32[]{:S(2)}, u32[]{:S(2)}) collective-permute-start(bf16[1024,256]{1,0:T(8,128)(2,1)S(1)} %get-tuple-element.11.own_b), channel_id=1, source_target_pairs={{0,127},{1,2},{2,1},{3,4},{4,3},{5,6},{6,5},{7,8},{8,7},{9,10},{10... | collective-permute-start | bytes 1572872 | tf_op jit(solution)/shard_map/ppermute | solution.py:538

commit v5 on v4

--- a/solution.py
+++ b/solution.py
@@ -7,7 +7,6 @@
 
 F32 = jnp.float32
 BF16 = jnp.bfloat16
-ANY = pl.BlockSpec(memory_space=pl.ANY)
 VMEM = pl.BlockSpec(memory_space=pltpu.VMEM)
 CHI = 256
 LEVELS = 8
@@ -159,11 +158,11 @@
     return jnp.where(i == j, 1.0, 0.0).astype(dtype)
 
 
-def two_site(lhs_of, weights, y, a0):
+def two_site(lhs_of, weights_of, y, a0):
     for p in range(2):
-        block = lhs_of(p)
+        block, weights = lhs_of(p), weights_of(p)
         for u in range(LEVELS // 2):
-            made = dot(block, weights[p, u * CHI : (u + 1) * CHI, :]).reshape(BONDS, LEVELS, CHI)
+            made = dot(block, weights[u * CHI : (u + 1) * CHI, :]).reshape(BONDS, LEVELS, CHI)
             both = jnp.concatenate([made[:, :, :128], made[:, :, 128:]], axis=1).astype(BF16)
             y[pl.ds(a0, BONDS), 16 * u : 16 * u + 16, p * 128 : (p + 1) * 128] = both
 
@@ -222,56 +221,57 @@
 RIGHT_SCALE = LEFT_SCALE * ROWS**-0.5
 
 
-def first_kernel(own, recv, sk_own, sk_recv, out_a, out_b, lhs, raw, wts, sk, gate, y, m, s, st, wide, q, ab, sems):
+def product_kernel(own, recv, gate_own, gate_recv, m, wts, gate, y, wide):
+    is_left = lax.rem(lax.axis_index("site"), 2) == 0
+
+    def product(left, right, small):
+        gate[...] = gate_matrix(small[...])
+        for h in range(2):
+            wide[h] = right[:, h * 128 : (h + 1) * 128].astype(F32)
+
+        def put(h, u, value):
+            wts[h, u * CHI : (u + 1) * CHI, :] = value
+
+        take_slabs(wide, put)
+
+        def some(x, _):
+            block = left[pl.ds(pl.multiple_of(x * HALF, HALF), HALF), :]
+            two_site(lambda p: block, lambda p: wts.at[p], y, pl.multiple_of(x * BONDS, BONDS))
+            return 0
+
+        lax.fori_loop(0, 2, some, 0)
+
+    @pl.when(is_left)
+    def _():
+        product(own, recv, gate_own)
+
+    @pl.when(jnp.logical_not(is_left))
+    def _():
+        product(recv, own, gate_recv)
+
+    gated(y, gate, m, ROWS)
+
+
+def first_kernel(m, sk_own, sk_recv, out_a, out_b, s, st, wide, q, ab):
     is_left = lax.rem(lax.axis_index("site"), 2) == 0
     outs = (out_a, out_b)
 
-    def fetch(left, right, sketch):
-        return (
-            pltpu.make_async_copy(right, raw, sems.at[0]),
-            pltpu.make_async_copy(left.at[pl.ds(0, HALF)], lhs.at[0], sems.at[1]),
-            pltpu.make_async_copy(left.at[pl.ds(HALF, HALF)], lhs.at[1], sems.at[2]),
-            pltpu.make_async_copy(sketch, sk, sems.at[3]),
-        )
-
-    copies = fetch(own, recv, sk_own)
+    def sample(sketch):
+        def some(i, _):
+            rows = pl.ds(pl.multiple_of(i * HALF, HALF), HALF)
+            s[rows, :] = dot(m[rows, :], sketch[:ROWS, :]).astype(BF16)
+            return 0
+
+        lax.fori_loop(0, 2, some, 0)
 
     @pl.when(is_left)
     def _():
-        for copy in copies:
-            copy.start()
+        sample(sk_own)
 
     @pl.when(jnp.logical_not(is_left))
     def _():
-        for copy in fetch(recv, own, sk_recv):
-            copy.start()
-
-    copies[0].wait()
-    for h in range(2):
-        wide[h] = raw[:, h * 128 : (h + 1) * 128].astype(F32)
-
-    def put(h, u, value):
-        wts[h, u * CHI : (u + 1) * CHI, :] = value
-
-    take_slabs(wide, put)
-    copies[1].wait()
-    copies[2].wait()
-
-    def product(x, _):
-        two_site(lambda p: lhs[x], wts, y, pl.multiple_of(x * BONDS, BONDS))
-        return 0
-
-    lax.fori_loop(0, 2, product, 0)
-    copies[3].wait()
-    gate[...] = gate_matrix(sk[ROWS:, :])
-    gated(y, gate, m, ROWS)
-
-    def sample(i, _):
-        r0 = pl.multiple_of(i * HALF, HALF)
-        s[pl.ds(r0, HALF), :] = dot(m[pl.ds(r0, HALF), :], sk[:ROWS, :]).astype(BF16)
-        return 0
-
-    lax.fori_loop(0, 2, sample, 0)
+        sample(sk_recv)
+
     st[...] = dot(identity(BF16), s[...], ((1,), (1,))).astype(BF16)
     ab[:, :CHI] = dot(st[...], s[...])
 
@@ -302,33 +302,34 @@
                 outs[x][:, h * 128 : (h + 1) * 128] = wide[h, x * HALF : (x + 1) * HALF, :].astype(BF16)
 
 
-def half_pair(own_a, own_b, recv, sk_own, sk_recv, lhs, wts, sk, gate, y, m, sems, is_left):
-    def fetch(left_a, left_b, right_a, right_b, sketch):
-        return (
-            pltpu.make_async_copy(left_a, lhs.at[0], sems.at[0]),
-            pltpu.make_async_copy(left_b, lhs.at[1], sems.at[1]),
-            pltpu.make_async_copy(right_a, wts.at[0], sems.at[2]),
-            pltpu.make_async_copy(right_b, wts.at[1], sems.at[3]),
-            pltpu.make_async_copy(sketch, sk, sems.at[4]),
-        )
-
-    copies = fetch(own_a, own_b, recv, recv, sk_own)
+def ready_kernel(sk_own, sk_recv, sk, gate):
+    is_left, _ = role()
+
+    def take(packed):
+        sk[...] = packed[:ROWS, :]
+        gate[...] = gate_matrix(packed[ROWS:, :])
 
     @pl.when(is_left)
     def _():
-        for copy in copies:
-            copy.start()
+        take(sk_own)
 
     @pl.when(jnp.logical_not(is_left))
     def _():
-        for copy in fetch(recv, recv, own_a, own_b, sk_recv):
-            copy.start()
-
-    for copy in copies[:4]:
-        copy.wait()
-    two_site(lambda p: lhs[p], wts, y, 0)
-    copies[4].wait()
-    gate[...] = gate_matrix(sk[ROWS:, :])
+        take(sk_recv)
+
+
+def half_pair(own_a, own_b, recv, gate, y, m, is_left):
+    owns = (own_a, own_b)
+
+    @pl.when(is_left)
+    def _():
+        two_site(lambda p: owns[p][...], lambda p: recv, y, 0)
+
+    @pl.when(jnp.logical_not(is_left))
+    def _():
+        block = recv[...]
+        two_site(lambda p: block, lambda p: owns[p], y, 0)
+
     gated(y, gate, m, HALF)
 
 
@@ -348,12 +349,12 @@
     return lax.rem(me, 2) == 1, (me > 0) & (me < lax.axis_size("site") - 1)
 
 
-def mid_kernel(own_a, own_b, recv, sk_own, sk_recv, acc, s0, m, lhs, wts, sk, sh, gate, y, sems):
+def mid_kernel(own_a, own_b, recv, sk, gate, acc, s0, m, sh, y):
     is_left, busy = role()
 
     @pl.when(busy)
     def _():
-        half_pair(own_a, own_b, recv, sk_own, sk_recv, lhs, wts, sk, gate, y, m, sems, is_left)
+        half_pair(own_a, own_b, recv, gate, y, m, is_left)
 
         @pl.when(is_left)
         def _():
@@ -364,18 +365,18 @@
 
         @pl.when(jnp.logical_not(is_left))
         def _():
-            s0[...] = dot(m[...], sk[:ROWS, :]).astype(BF16)
+            s0[...] = dot(m[...], sk[...]).astype(BF16)
 
 
 def last_kernel(
-    own_a, own_b, recv, sk_own, sk_recv, acc, s0, m0, out, lhs, wts, sk, sh, gate, y, m, s, st, wide, q, ab, sems
+    own_a, own_b, recv, sk, gate, acc, s0, m0, out, sh, y, m, s, st, wide, q, ab
 ):
     is_left, busy = role()
     owns = (own_a, own_b)
 
     @pl.when(busy)
     def _():
-        half_pair(own_a, own_b, recv, sk_own, sk_recv, lhs, wts, sk, gate, y, m, sems, is_left)
+        half_pair(own_a, own_b, recv, gate, y, m, is_left)
 
         @pl.when(is_left)
         def _():
@@ -387,7 +388,7 @@
         @pl.when(jnp.logical_not(is_left))
         def _():
             s[:HALF, :] = s0[...]
-            s[HALF:, :] = dot(m[...], sk[:ROWS, :]).astype(BF16)
+            s[HALF:, :] = dot(m[...], sk[...]).astype(BF16)
 
         st[...] = dot(identity(BF16), s[...], ((1,), (1,))).astype(BF16)
         ab[:, :CHI] = dot(st[...], s[...])
@@ -414,109 +415,42 @@
 
     @pl.when(jnp.logical_not(busy))
     def _():
-        for x in range(2):
-            copy = pltpu.make_async_copy(owns[x], lhs.at[x], sems.at[x])
-            copy.start()
-            copy.wait()
-
         @pl.when(is_left)
         def _():
             for x in range(2):
-                out[x * HALF : (x + 1) * HALF, :] = lhs[x]
+                out[x * HALF : (x + 1) * HALF, :] = owns[x][...]
 
         @pl.when(jnp.logical_not(is_left))
         def _():
             for h in range(2):
                 for u in range(LEVELS // 2):
                     for e in range(2):
-                        slab = lhs[h, u * CHI : (u + 1) * CHI, e * 128 : (e + 1) * 128].astype(F32)
+                        slab = owns[h][u * CHI : (u + 1) * CHI, e * 128 : (e + 1) * 128].astype(F32)
                         wide[h, pl.ds(2 * u + e, CHI, stride=LEVELS), :] = slab
             for h in range(2):
                 out[:, h * 128 : (h + 1) * 128] = wide[h].astype(BF16)
 
 
 HALF_ARRAY = jax.ShapeDtypeStruct((HALF, CHI), BF16)
-HALVES = pltpu.VMEM((2, HALF, CHI), BF16)
 WHOLE = pltpu.VMEM((ROWS, CHI), BF16)
 TURNED = pltpu.VMEM((CHI, ROWS), BF16)
-SKETCH = pltpu.VMEM((ROWS + GATE, CHI), BF16)
-GATES = pltpu.VMEM((4 * GATE, 4 * GATE), BF16)
 WIDE = pltpu.VMEM((2, ROWS, 128), F32)
 GRAM = pltpu.VMEM((CHI, 2 * CHI), F32)
-
-
-def first_layer(own, recv, sk_own, sk_recv):
+FACTOR = [WHOLE, TURNED, WIDE, TURNED, GRAM]
+HALF_SCRATCH = [pltpu.VMEM((HALF, CHI), BF16), pltpu.VMEM((BONDS, GATE, CHI), BF16)]
+
+
+def call(kernel, name, out_shape, scratch, limit, *args):
+    single = not isinstance(out_shape, tuple)
     return pl.pallas_call(
-        first_kernel,
-        out_shape=(HALF_ARRAY, HALF_ARRAY),
-        in_specs=[ANY] * 4,
-        out_specs=(VMEM, VMEM),
-        scratch_shapes=[
-            HALVES,
-            WHOLE,
-            HALVES,
-            SKETCH,
-            GATES,
-            pltpu.VMEM((CHI, GATE, CHI), BF16),
-            pltpu.VMEM((ROWS, ROWS), BF16),
-            WHOLE,
-            TURNED,
-            WIDE,
-            TURNED,
-            GRAM,
-            pltpu.SemaphoreType.DMA((4,)),
-        ],
-        compiler_params=pltpu.CompilerParams(vmem_limit_bytes=32 << 20),
-        name="first",
-    )(own, recv, sk_own, sk_recv)
-
-
-HALF_SCRATCH = [
-    HALVES,
-    HALVES,
-    SKETCH,
-    pltpu.VMEM((HALF, CHI), BF16),
-    GATES,
-    pltpu.VMEM((BONDS, GATE, CHI), BF16),
-]
-
-
-def second_start(own_a, own_b, recv, sk_own, sk_recv):
-    return pl.pallas_call(
-        mid_kernel,
-        out_shape=(
-            jax.ShapeDtypeStruct((ROWS, CHI), F32),
-            HALF_ARRAY,
-            jax.ShapeDtypeStruct((HALF, ROWS), BF16),
-        ),
-        in_specs=[ANY] * 5,
-        out_specs=(VMEM, VMEM, VMEM),
-        scratch_shapes=[*HALF_SCRATCH, pltpu.SemaphoreType.DMA((5,))],
-        compiler_params=pltpu.CompilerParams(vmem_limit_bytes=24 << 20),
-        cost_estimate=pl.CostEstimate(flops=5 << 30, bytes_accessed=8 << 20, transcendentals=0),
-        name="mid",
-    )(own_a, own_b, recv, sk_own, sk_recv)
-
-
-def second_end(own_a, own_b, recv, sk_own, sk_recv, acc, s0, m0):
-    return pl.pallas_call(
-        last_kernel,
-        out_shape=jax.ShapeDtypeStruct((ROWS, CHI), BF16),
-        in_specs=[*[ANY] * 5, VMEM, VMEM, VMEM],
-        out_specs=VMEM,
-        scratch_shapes=[
-            *HALF_SCRATCH,
-            pltpu.VMEM((HALF, ROWS), BF16),
-            WHOLE,
-            TURNED,
-            WIDE,
-            TURNED,
-            GRAM,
-            pltpu.SemaphoreType.DMA((5,)),
-        ],
-        compiler_params=pltpu.CompilerParams(vmem_limit_bytes=32 << 20),
-        name="last",
-    )(own_a, own_b, recv, sk_own, sk_recv, acc, s0, m0)
+        kernel,
+        out_shape=out_shape,
+        in_specs=[VMEM] * len(args),
+        out_specs=VMEM if single else tuple(VMEM for _ in out_shape),
+        scratch_shapes=scratch,
+        compiler_params=pltpu.CompilerParams(vmem_limit_bytes=limit << 20),
+        name=name,
+    )(*args)
 
 
 def pack(sketch, gate):
@@ -529,15 +463,35 @@
     across = [(i, (i + 1) % devices if i % 2 else (i - 1) % devices) for i in range(devices)]
     own = site_tensors[0].reshape(ROWS, CHI)
     recv = lax.ppermute(own, "site", inside)
-    sk0 = pack(first_sketch[0], first_gates[0])
+    gate_recv = lax.ppermute(first_gates[0], "site", inside)
+    sk0 = first_sketch[0].astype(BF16)
     sk0_recv = lax.ppermute(sk0, "site", inside)
     sk1 = pack(second_sketch[0], second_gates[0])
+    sk1, gate_recv = lax.optimization_barrier((sk1, gate_recv))
     sk1_recv = lax.ppermute(sk1, "site", across)
-    own_a, own_b = first_layer(own, recv, sk0, sk0_recv)
+    product_scratch = [
+        pltpu.VMEM((2, HALF, CHI), BF16),
+        pltpu.VMEM((4 * GATE, 4 * GATE), BF16),
+        pltpu.VMEM((CHI, GATE, CHI), BF16),
+        WIDE,
+    ]
+    whole_matrix = jax.ShapeDtypeStruct((ROWS, ROWS), BF16)
+    half_matrix = jax.ShapeDtypeStruct((HALF, ROWS), BF16)
+    whole_array = jax.ShapeDtypeStruct((ROWS, CHI), BF16)
+    partial = jax.ShapeDtypeStruct((ROWS, CHI), F32)
+    gate_shape = jax.ShapeDtypeStruct((4 * GATE, 4 * GATE), BF16)
+    m = call(product_kernel, "product", whole_matrix, product_scratch, 24, own, recv, first_gates[0], gate_recv)
+    own_a, own_b = call(first_kernel, "first", (HALF_ARRAY, HALF_ARRAY), FACTOR, 24, m, sk0, sk0_recv)
     recv_a = lax.ppermute(own_a, "site", across)
     recv_b = lax.ppermute(own_b, "site", across)
-    acc, s0, m0 = second_start(own_a, own_b, recv_a, sk1, sk1_recv)
-    made = second_end(own_a, own_b, recv_b, sk1, sk1_recv, acc, s0, m0)
+    sk, gate = call(ready_kernel, "ready", (whole_array, gate_shape), [], 8, sk1, sk1_recv)
+    acc, s0, m0 = call(
+        mid_kernel, "mid", (partial, HALF_ARRAY, half_matrix), HALF_SCRATCH, 24, own_a, own_b, recv_a, sk, gate
+    )
+    last_scratch = [*HALF_SCRATCH, pltpu.VMEM((HALF, ROWS), BF16), *FACTOR]
+    made = call(
+        last_kernel, "last", whole_array, last_scratch, 32, own_a, own_b, recv_b, sk, gate, acc, s0, m0
+    )
     return made.reshape(1, CHI, LEVELS, CHI)
 
 

time: 58.5 us -> 57.5 us (0.983)
  Pallas kernels: 34.6 us -> 33.6 us
    convert_element_type x2 -> x1, other arithmetic: 2.12 us -> 0.17 us  [pack(): sketch.astype(BF16)]
    convert_element_type x0 -> x1, other arithmetic: none -> 1.87 us  [per_device(): sk0 = first_sketch[0].astype(BF16)]
    ppermute x1, starting transfers between devices: 1.9 us -> 0.21 us  [per_device(): recv_a = lax.ppermute(own_a, 'site', across)]
    ppermute x1, starting transfers between devices: 4.14 us -> 5.83 us  [per_device(): recv_b = lax.ppermute(own_b, 'site', across)]
    pallas_call x3 -> x5, Pallas kernels: 34.6 us -> 33.6 us  [call(): pl.pallas_call(kernel, out_shape=out_shape, in_specs=[VMEM] * len(args),...]
  transfers between devices with their start and end apart: 5 -> 6, of which waited for: 2 -> 2; matrix products, arithmetic and copies ran while one was open for 4% -> 4% of each run, Pallas kernels for 37% -> 37%
where the time goes in v5:
time: 57.5 us; the launch traced here: 57.4 us
  Pallas kernels  33.6 us (58%)
  starting transfers between devices  13.2 us (23%)
  waiting for transfers between devices  7.91 us (14%)
  other arithmetic  2.16 us (4%)
    pallas_call x5, Pallas kernels, call(): pl.pallas_call(kernel, out_shape=out_shape, in_specs=[VMEM] * len(args),...  33.6 us
    ppermute x1, starting transfers between devices, per_device(): sk1_recv = lax.ppermute(sk1, 'site', across)  6.53 us
    ppermute x1, waiting for transfers between devices, per_device(): recv_a = lax.ppermute(own_a, 'site', across)  6.46 us
    ppermute x1, starting transfers between devices, per_device(): recv_b = lax.ppermute(own_b, 'site', across)  5.83 us
    convert_element_type x1, other arithmetic, per_device(): sk0 = first_sketch[0].astype(BF16)  1.87 us
    ppermute x1, waiting for transfers between devices, per_device(): recv_b = lax.ppermute(own_b, 'site', across)  1.44 us
  transfers between devices with their start and end apart: 6, of which 2 were waited for; matrix products, arithmetic and copies ran while one was open for 4% of the time, Pallas kernels for 37%

profile of v5, /device:TPU:6, one launch (start us, length us, event | category | flops | bytes accessed | tf_op | source)
XLA Modules:
  0.0 57.4 jit_solution(6438125143977736690)
XLA Ops:
  0.0 0.0 copy-start.2
  0.0 0.0 collective-permute-start.1
  0.0 0.5 collective-permute-start
  0.5 1.9 %convert_bitcast_fusion.sk_own = bf16[2048,256]{1,0:T(8,128)(2,1)S(1)} fusion(s32[1,2048,256]{2,1,0:T(8,128)} %param.8), kind=kLoop, calls=%fused_computation.1 | loop fusion | flops 524288 | bytes 3145728 | tf_op jit(solution)/shard_map/convert_element_type | solution.py:467
  2.4 0.0 copy-start.3
  2.4 0.0 copy-start
  2.4 0.0 copy-start.1
  2.4 0.1 collective-permute-start.2
  2.5 0.0 copy-done.2
  2.5 0.2 convert_bitcast_fusion.1
  2.7 0.4 copy-done.3
  3.1 0.1 maximum_maximum_fusion.sk_own
  3.2 0.0 collective-permute-done.1.gate_recv
  3.2 6.5 %collective-permute-start.4 = (bf16[2112,256]{1,0:T(8,128)(2,1)S(1)}, bf16[2112,256]{1,0:T(8,128)(2,1)S(1)}, u32[]{:S(2)}, u32[]{:S(2)}) collective-permute-start(bf16[2112,256]{1,0:T(8,128)(2,1)S(1)} %maximum_maximum_fusion.sk_own), channel_id=1, source_target_pairs={{0,127},{1,2},{2,1},{3,4},{4,3},{5,6},{6,5},{7,8},{8,7},{9,10},{10... | collective-permute-start | bytes 3244040 | tf_op jit(solution)/shard_map/ppermute | solution.py:471
  9.8 0.0 collective-permute-done.recv
  9.8 0.0 copy-done
  9.8 0.0 copy-done.1
  9.8 6.2 %product.1.m = bf16[2048,2048]{1,0:T(8,128)(2,1)S(1)} custom-call(bf16[2048,256]{1,0:T(8,128)(2,1)S(1)} %bitcast.9, bf16[2048,256]{1,0:T(8,128)(2,1)S(1)} %collective-permute-done.recv, bf16[64,64]{1,0:T(8,128)(2,1)S(1)} %bitcast.11, bf16[64,64]{1,0:T(8,128)(2,1)S(1)} %collective-permute-done.1.gate_recv), custom_call_target="tpu_custom_call" | custom-call | tf_op jit(solution)/shard_map/product/pallas_call | solution.py:445
  16.0 0.0 collective-permute-done.2.sk_recv
  16.0 10.3 %first.1 = (bf16[1024,256]{1,0:T(8,128)(2,1)S(1)}, bf16[1024,256]{1,0:T(8,128)(2,1)S(1)}) custom-call(bf16[2048,2048]{1,0:T(8,128)(2,1)S(1)} %product.1.m, bf16[2048,256]{1,0:T(8,128)(2,1)S(1)} %convert_bitcast_fusion.sk_own, bf16[2048,256]{1,0:T(8,128)(2,1)S(1)} %collective-permute-done.2.sk_recv), custom_call_target="tpu_custom_call" | custom-call | tf_op jit(solution)/shard_map/first/pallas_call | solution.py:445
  26.3 0.2 collective-permute-start.5
  26.5 5.8 %collective-permute-start.3 = (bf16[1024,256]{1,0:T(8,128)(2,1)S(1)}, bf16[1024,256]{1,0:T(8,128)(2,1)S(1)}, u32[]{:S(2)}, u32[]{:S(2)}) collective-permute-start(bf16[1024,256]{1,0:T(8,128)(2,1)S(1)} %get-tuple-element.16.own_b), channel_id=1, source_target_pairs={{0,127},{1,2},{2,1},{3,4},{4,3},{5,6},{6,5},{7,8},{8,7},{9,10},{10... | collective-permute-start | bytes 1572872 | tf_op jit(solution)/shard_map/ppermute | solution.py:486
  32.3 0.0 collective-permute-done.4.sk_recv
  32.3 0.4 ready.1
  32.7 6.5 %collective-permute-done.5.recv = bf16[1024,256]{1,0:T(8,128)(2,1)S(1)} collective-permute-done((bf16[1024,256]{1,0:T(8,128)(2,1)S(1)}, bf16[1024,256]{1,0:T(8,128)(2,1)S(1)}, u32[]{:S(2)}, u32[]{:S(2)}) %collective-permute-start.5) | collective-permute-done | bytes 524320 | tf_op jit(solution)/shard_map/ppermute | solution.py:485
  39.2 4.2 %mid.1 = (f32[2048,256]{1,0:T(8,128)S(1)}, bf16[1024,256]{1,0:T(8,128)(2,1)S(1)}, bf16[1024,2048]{1,0:T(8,128)(2,1)S(1)}) custom-call(bf16[1024,256]{1,0:T(8,128)(2,1)S(1)} %get-tuple-element.15.own_a, bf16[1024,256]{1,0:T(8,128)(2,1)S(1)} %get-tuple-element.16.own_b, bf16[1024,256]{1,0:T(8,128)(2,1)S(1)} %collective-permute-done.5.recv, ...), custom_call_target="tpu_custom_call" | custom-call | tf_op jit(solution)/shard_map/mid/pallas_call | solution.py:445
  43.4 1.4 %collective-permute-done.3.recv = bf16[1024,256]{1,0:T(8,128)(2,1)S(1)} collective-permute-done((bf16[1024,256]{1,0:T(8,128)(2,1)S(1)}, bf16[1024,256]{1,0:T(8,128)(2,1)S(1)}, u32[]{:S(2)}, u32[]{:S(2)}) %collective-permute-start.3) | collective-permute-done | bytes 524320 | tf_op jit(solution)/shard_map/ppermute | solution.py:486
  44.8 12.5 %last.1 = bf16[2048,256]{1,0:T(8,128)(2,1)} custom-call(bf16[1024,256]{1,0:T(8,128)(2,1)S(1)} %get-tuple-element.15.own_a, bf16[1024,256]{1,0:T(8,128)(2,1)S(1)} %get-tuple-element.16.own_b, bf16[1024,256]{1,0:T(8,128)(2,1)S(1)} %collective-permute-done.3.recv, bf16[2048,256]{1,0:T(8,128)(2,1)S(1)} %get-tuple-element.18.sk, ...), custom_call_target="tpu_custom_call" | custom-call | tf_op jit(solution)/shard_map/last/pallas_call | solution.py:445
Async XLA Ops:
  0.0 2.5 %copy-start.2 = (s32[1,2048,256]{2,1,0:T(8,128)S(1)}, s32[1,2048,256]{2,1,0:T(8,128)}, u32[]{:S(2)}) copy-start(s32[1,2048,256]{2,1,0:T(8,128)} %param.9) | copy-start | bytes 6291460
  0.0 3.2 %collective-permute-start.1 = (bf16[64,64]{1,0:T(8,128)(2,1)}, bf16[64,64]{1,0:T(8,128)(2,1)S(1)}, u32[]{:S(2)}, u32[]{:S(2)}) collective-permute-start(bf16[64,64]{1,0:T(8,128)(2,1)} %bitcast.10), channel_id=1, source_target_pairs={{0,1},{1,0},{2,3},{3,2},{4,5},{5,4},{6,7},{7,6},{8,9},{9,8},{10,11... | collective-permute-start | bytes 24584 | tf_op jit(solution)/shard_map/ppermute | solution.py:466
  0.0 9.8 %collective-permute-start = (bf16[2048,256]{1,0:T(8,128)(2,1)}, bf16[2048,256]{1,0:T(8,128)(2,1)S(1)}, u32[]{:S(2)}, u32[]{:S(2)}) collective-permute-start(bf16[2048,256]{1,0:T(8,128)(2,1)} %bitcast.8), channel_id=1, source_target_pairs={{0,1},{1,0},{2,3},{3,2},{4,5},{5,4},{6,7},{7,6},{8,9},{9,8},{10,11... | collective-permute-start | bytes 3145736 | tf_op jit(solution)/shard_map/ppermute | solution.py:465
  2.4 0.7 %copy-start.3 = (bf16[1,64,64]{2,1,0:T(8,128)(2,1)S(1)}, bf16[1,64,64]{2,1,0:T(8,128)(2,1)}, u32[]{:S(2)}) copy-start(bf16[1,64,64]{2,1,0:T(8,128)(2,1)} %param.7) | copy-start | bytes 24580
  2.4 7.4 %copy-start = (bf16[1,256,8,256]{3,2,1,0:T(8,128)(2,1)S(1)}, bf16[1,256,8,256]{3,2,1,0:T(8,128)(2,1)}, u32[]{:S(2)}) copy-start(bf16[1,256,8,256]{3,2,1,0:T(8,128)(2,1)} %param.5) | copy-start | bytes 3145732
  2.4 7.4 %copy-start.1 = (bf16[1,64,64]{2,1,0:T(8,128)(2,1)S(1)}, bf16[1,64,64]{2,1,0:T(8,128)(2,1)}, u32[]{:S(2)}) copy-start(bf16[1,64,64]{2,1,0:T(8,128)(2,1)} %param.6) | copy-start | bytes 24580
  2.4 13.5 %collective-permute-start.2 = (bf16[2048,256]{1,0:T(8,128)(2,1)S(1)}, bf16[2048,256]{1,0:T(8,128)(2,1)S(1)}, u32[]{:S(2)}, u32[]{:S(2)}) collective-permute-start(bf16[2048,256]{1,0:T(8,128)(2,1)S(1)} %convert_bitcast_fusion.sk_own), channel_id=1, source_target_pairs={{0,1},{1,0},{2,3},{3,2},{4,5},{5,4},{6,7},{7,6},{8,9},{9,8},{10,11... | collective-permute-start | bytes 3145736 | tf_op jit(solution)/shard_map/ppermute | solution.py:468
  3.2 29.1 %collective-permute-start.4 = (bf16[2112,256]{1,0:T(8,128)(2,1)S(1)}, bf16[2112,256]{1,0:T(8,128)(2,1)S(1)}, u32[]{:S(2)}, u32[]{:S(2)}) collective-permute-start(bf16[2112,256]{1,0:T(8,128)(2,1)S(1)} %maximum_maximum_fusion.sk_own), channel_id=1, source_target_pairs={{0,127},{1,2},{2,1},{3,4},{4,3},{5,6},{6,5},{7,8},{8,7},{9,10},{10... | collective-permute-start | bytes 3244040 | tf_op jit(solution)/shard_map/ppermute | solution.py:471
  26.3 12.9 %collective-permute-start.5 = (bf16[1024,256]{1,0:T(8,128)(2,1)S(1)}, bf16[1024,256]{1,0:T(8,128)(2,1)S(1)}, u32[]{:S(2)}, u32[]{:S(2)}) collective-permute-start(bf16[1024,256]{1,0:T(8,128)(2,1)S(1)} %get-tuple-element.15.own_a), channel_id=1, source_target_pairs={{0,127},{1,2},{2,1},{3,4},{4,3},{5,6},{6,5},{7,8},{8,7},{9,10},{10... | collective-permute-start | bytes 1572872 | tf_op jit(solution)/shard_map/ppermute | solution.py:485
  26.5 18.3 %collective-permute-start.3 = (bf16[1024,256]{1,0:T(8,128)(2,1)S(1)}, bf16[1024,256]{1,0:T(8,128)(2,1)S(1)}, u32[]{:S(2)}, u32[]{:S(2)}) collective-permute-start(bf16[1024,256]{1,0:T(8,128)(2,1)S(1)} %get-tuple-element.16.own_b), channel_id=1, source_target_pairs={{0,127},{1,2},{2,1},{3,4},{4,3},{5,6},{6,5},{7,8},{8,7},{9,10},{10... | collective-permute-start | bytes 1572872 | tf_op jit(solution)/shard_map/ppermute | solution.py:486

commit v6 on v5

--- a/solution.py
+++ b/solution.py
@@ -136,6 +136,7 @@
 
 
 HALF = ROWS // 2
+ROW_SITES = 8
 BONDS = CHI // 2
 STEP = 512
 
@@ -221,35 +222,51 @@
 RIGHT_SCALE = LEFT_SCALE * ROWS**-0.5
 
 
-def product_kernel(own, recv, gate_own, gate_recv, m, wts, gate, y, wide):
+def waits_long():
+    return lax.rem(lax.axis_index("site"), ROW_SITES) == 0
+
+
+def product(left, right, small, m, wts, gate, y, wide):
+    gate[...] = gate_matrix(small[...])
+    for h in range(2):
+        wide[h] = right[:, h * 128 : (h + 1) * 128].astype(F32)
+
+    def put(h, u, value):
+        wts[h, u * CHI : (u + 1) * CHI, :] = value
+
+    take_slabs(wide, put)
+
+    def some(x, _):
+        block = left[pl.ds(pl.multiple_of(x * HALF, HALF), HALF), :]
+        two_site(lambda p: block, lambda p: wts.at[p], y, pl.multiple_of(x * BONDS, BONDS))
+        return 0
+
+    lax.fori_loop(0, 2, some, 0)
+
+
+def early_kernel(own, recv, gate_own, gate_recv, gate_next, m, gate_rows, wts, gate, y, wide):
+    gate_rows[...] = jnp.concatenate([gate_next[...]] * 4, axis=1)
+
+    @pl.when(waits_long())
+    def _():
+        product(own, recv, gate_own, m, wts, gate, y, wide)
+        gated(y, gate, m, ROWS)
+
+
+def late_kernel(m_in, own, recv, gate_own, gate_recv, m, wts, gate, y, wide):
     is_left = lax.rem(lax.axis_index("site"), 2) == 0
 
-    def product(left, right, small):
-        gate[...] = gate_matrix(small[...])
-        for h in range(2):
-            wide[h] = right[:, h * 128 : (h + 1) * 128].astype(F32)
-
-        def put(h, u, value):
-            wts[h, u * CHI : (u + 1) * CHI, :] = value
-
-        take_slabs(wide, put)
-
-        def some(x, _):
-            block = left[pl.ds(pl.multiple_of(x * HALF, HALF), HALF), :]
-            two_site(lambda p: block, lambda p: wts.at[p], y, pl.multiple_of(x * BONDS, BONDS))
-            return 0
-
-        lax.fori_loop(0, 2, some, 0)
-
-    @pl.when(is_left)
-    def _():
-        product(own, recv, gate_own)
-
-    @pl.when(jnp.logical_not(is_left))
-    def _():
-        product(recv, own, gate_recv)
-
-    gated(y, gate, m, ROWS)
+    @pl.when(jnp.logical_not(waits_long()))
+    def _():
+        @pl.when(is_left)
+        def _():
+            product(own, recv, gate_own, m, wts, gate, y, wide)
+
+        @pl.when(jnp.logical_not(is_left))
+        def _():
+            product(recv, own, gate_recv, m, wts, gate, y, wide)
+
+        gated(y, gate, m, ROWS)
 
 
 def first_kernel(m, sk_own, sk_recv, out_a, out_b, s, st, wide, q, ab):
@@ -440,7 +457,7 @@
 HALF_SCRATCH = [pltpu.VMEM((HALF, CHI), BF16), pltpu.VMEM((BONDS, GATE, CHI), BF16)]
 
 
-def call(kernel, name, out_shape, scratch, limit, *args):
+def call(kernel, name, out_shape, scratch, limit, *args, aliases={}):
     single = not isinstance(out_shape, tuple)
     return pl.pallas_call(
         kernel,
@@ -448,27 +465,16 @@
         in_specs=[VMEM] * len(args),
         out_specs=VMEM if single else tuple(VMEM for _ in out_shape),
         scratch_shapes=scratch,
+        input_output_aliases=aliases,
         compiler_params=pltpu.CompilerParams(vmem_limit_bytes=limit << 20),
         name=name,
     )(*args)
-
-
-def pack(sketch, gate):
-    return jnp.concatenate([sketch.astype(BF16), jnp.concatenate([gate] * 4, axis=1)], axis=0)
 
 
 def per_device(site_tensors, first_gates, second_gates, first_sketch, second_sketch):
     devices = lax.axis_size("site")
     inside = [(i, i ^ 1) for i in range(devices)]
     across = [(i, (i + 1) % devices if i % 2 else (i - 1) % devices) for i in range(devices)]
-    own = site_tensors[0].reshape(ROWS, CHI)
-    recv = lax.ppermute(own, "site", inside)
-    gate_recv = lax.ppermute(first_gates[0], "site", inside)
-    sk0 = first_sketch[0].astype(BF16)
-    sk0_recv = lax.ppermute(sk0, "site", inside)
-    sk1 = pack(second_sketch[0], second_gates[0])
-    sk1, gate_recv = lax.optimization_barrier((sk1, gate_recv))
-    sk1_recv = lax.ppermute(sk1, "site", across)
     product_scratch = [
         pltpu.VMEM((2, HALF, CHI), BF16),
         pltpu.VMEM((4 * GATE, 4 * GATE), BF16),
@@ -480,7 +486,39 @@
     whole_array = jax.ShapeDtypeStruct((ROWS, CHI), BF16)
     partial = jax.ShapeDtypeStruct((ROWS, CHI), F32)
     gate_shape = jax.ShapeDtypeStruct((4 * GATE, 4 * GATE), BF16)
-    m = call(product_kernel, "product", whole_matrix, product_scratch, 24, own, recv, first_gates[0], gate_recv)
+    gate_rows_shape = jax.ShapeDtypeStruct((GATE, CHI), BF16)
+    own = site_tensors[0].reshape(ROWS, CHI)
+    recv = lax.ppermute(own, "site", inside)
+    gate_recv = lax.ppermute(first_gates[0], "site", inside)
+    sk0 = first_sketch[0].astype(BF16)
+    sk0_recv = lax.ppermute(sk0, "site", inside)
+    m, gate_rows = call(
+        early_kernel,
+        "early",
+        (whole_matrix, gate_rows_shape),
+        product_scratch,
+        24,
+        own,
+        recv,
+        first_gates[0],
+        gate_recv,
+        second_gates[0],
+    )
+    sk1 = jnp.concatenate([second_sketch[0].astype(BF16), gate_rows], axis=0)
+    sk1_recv = lax.ppermute(sk1, "site", across)
+    m = call(
+        late_kernel,
+        "late",
+        whole_matrix,
+        product_scratch,
+        24,
+        m,
+        own,
+        recv,
+        first_gates[0],
+        gate_recv,
+        aliases={0: 0},
+    )
     own_a, own_b = call(first_kernel, "first", (HALF_ARRAY, HALF_ARRAY), FACTOR, 24, m, sk0, sk0_recv)
     recv_a = lax.ppermute(own_a, "site", across)
     recv_b = lax.ppermute(own_b, "site", across)

time: 57.5 us -> 58 us (level)
    ppermute x1, starting transfers between devices: 0.21 us -> 12 us  [per_device(): recv_a = lax.ppermute(own_a, 'site', across)]
    ppermute x1, starting transfers between devices: 6.53 us -> 0.24 us  [per_device(): sk1_recv = lax.ppermute(sk1, 'site', across)]
    ppermute x1, starting transfers between devices: 5.83 us -> 0.09 us  [per_device(): recv_b = lax.ppermute(own_b, 'site', across)]
    pallas_call x5 -> x6, Pallas kernels: 33.6 us -> 33.6 us  [call(): pl.pallas_call(kernel, out_shape=out_shape, in_specs=[VMEM] * len(args),...]
  transfers between devices with their start and end apart: 6 -> 6, of which waited for: 2 -> 3; matrix products, arithmetic and copies ran while one was open for 4% -> 4% of each run, Pallas kernels for 37% -> 36%
where the time goes in v6:
time: 58 us; the launch traced here: 57.9 us
  Pallas kernels  33.6 us (58%)
  starting transfers between devices  13 us (22%)
  waiting for transfers between devices  8.35 us (14%)
  other arithmetic  2.12 us (4%)
  local copies, waits for them, and re-layouts  0.74 us (1%)
    pallas_call x6, Pallas kernels, call(): pl.pallas_call(kernel, out_shape=out_shape, in_specs=[VMEM] * len(args),...  33.6 us
    ppermute x1, starting transfers between devices, per_device(): recv_a = lax.ppermute(own_a, 'site', across)  12 us
    ppermute x1, waiting for transfers between devices, per_device(): recv_a = lax.ppermute(own_a, 'site', across)  6.37 us
    convert_element_type x1, other arithmetic, per_device(): sk0 = first_sketch[0].astype(BF16)  1.87 us
    ppermute x1, waiting for transfers between devices, per_device(): recv_b = lax.ppermute(own_b, 'site', across)  1.78 us
  transfers between devices with their start and end apart: 6, of which 3 were waited for; matrix products, arithmetic and copies ran while one was open for 4% of the time, Pallas kernels for 36%

profile of v6, /device:TPU:6, one launch (start us, length us, event | category | flops | bytes accessed | tf_op | source)
XLA Modules:
  0.0 57.9 jit_solution(10539815775950295682)
XLA Ops:
  0.0 0.0 copy-start.3
  0.0 0.0 collective-permute-start
  0.0 0.5 collective-permute-start.1
  0.5 1.9 %convert_bitcast_fusion.1.sk_own = bf16[2048,256]{1,0:T(8,128)(2,1)S(1)} fusion(s32[1,2048,256]{2,1,0:T(8,128)} %param.8), kind=kLoop, calls=%fused_computation.2 | loop fusion | flops 524288 | bytes 3145728 | tf_op jit(solution)/shard_map/convert_element_type | solution.py:493
  2.4 0.0 copy-start
  2.4 0.0 copy-start.1
  2.4 0.0 copy-start.2
  2.4 0.1 collective-permute-start.2
  2.5 0.0 copy-done.3
  2.5 0.2 convert_bitcast_fusion
  2.7 0.2 collective-permute-done.1.gate_recv
  2.9 0.0 collective-permute-done.recv
  2.9 0.7 %copy-done = bf16[1,256,8,256]{3,2,1,0:T(8,128)(2,1)S(1)} copy-done((bf16[1,256,8,256]{3,2,1,0:T(8,128)(2,1)S(1)}, bf16[1,256,8,256]{3,2,1,0:T(8,128)(2,1)}, u32[]{:S(2)}) %copy-start) | copy-done | bytes 1048600
  3.6 0.0 copy-done.1
  3.6 0.0 copy-done.2
  3.6 6.2 %early.1 = (bf16[2048,2048]{1,0:T(8,128)(2,1)S(1)}, bf16[64,256]{1,0:T(8,128)(2,1)S(1)}) custom-call(bf16[2048,256]{1,0:T(8,128)(2,1)S(1)} %bitcast.9, bf16[2048,256]{1,0:T(8,128)(2,1)S(1)} %collective-permute-done.recv, bf16[64,64]{1,0:T(8,128)(2,1)S(1)} %bitcast.12, bf16[64,64]{1,0:T(8,128)(2,1)S(1)} %collective-permute-done.1.gate_recv, ...), custom_call_target="tpu_custom_call" | custom-call | tf_op jit(solution)/shard_map/early/pallas_call | solution.py:462
  9.9 0.1 pad_maximum_fusion.sk_own
  9.9 0.2 collective-permute-start.4
  10.2 0.0 collective-permute-done.2.sk_recv
  10.2 10.3 %first.1 = (bf16[1024,256]{1,0:T(8,128)(2,1)S(1)}, bf16[1024,256]{1,0:T(8,128)(2,1)S(1)}) custom-call(bf16[2048,2048]{1,0:T(8,128)(2,1)S(1)} %late.1.m, bf16[2048,256]{1,0:T(8,128)(2,1)S(1)} %convert_bitcast_fusion.1.sk_own, bf16[2048,256]{1,0:T(8,128)(2,1)S(1)} %collective-permute-done.2.sk_recv), custom_call_target="tpu_custom_call" | custom-call | tf_op jit(solution)/shard_map/first/pallas_call | solution.py:462
  20.5 12.0 %collective-permute-start.5 = (bf16[1024,256]{1,0:T(8,128)(2,1)S(1)}, bf16[1024,256]{1,0:T(8,128)(2,1)S(1)}, u32[]{:S(2)}, u32[]{:S(2)}) collective-permute-start(bf16[1024,256]{1,0:T(8,128)(2,1)S(1)} %get-tuple-element.15.own_a), channel_id=1, source_target_pairs={{0,127},{1,2},{2,1},{3,4},{4,3},{5,6},{6,5},{7,8},{8,7},{9,10},{10... | collective-permute-start | bytes 1572872 | tf_op jit(solution)/shard_map/ppermute | solution.py:523
  32.5 0.1 collective-permute-start.3
  32.6 0.0 collective-permute-done.4.sk_recv
  32.6 0.4 ready.1
  33.0 6.4 %collective-permute-done.5.recv = bf16[1024,256]{1,0:T(8,128)(2,1)S(1)} collective-permute-done((bf16[1024,256]{1,0:T(8,128)(2,1)S(1)}, bf16[1024,256]{1,0:T(8,128)(2,1)S(1)}, u32[]{:S(2)}, u32[]{:S(2)}) %collective-permute-start.5) | collective-permute-done | bytes 524320 | tf_op jit(solution)/shard_map/ppermute | solution.py:523
  39.4 4.2 %mid.1 = (f32[2048,256]{1,0:T(8,128)S(1)}, bf16[1024,256]{1,0:T(8,128)(2,1)S(1)}, bf16[1024,2048]{1,0:T(8,128)(2,1)S(1)}) custom-call(bf16[1024,256]{1,0:T(8,128)(2,1)S(1)} %get-tuple-element.15.own_a, bf16[1024,256]{1,0:T(8,128)(2,1)S(1)} %get-tuple-element.16.own_b, bf16[1024,256]{1,0:T(8,128)(2,1)S(1)} %collective-permute-done.5.recv, ...), custom_call_target="tpu_custom_call" | custom-call | tf_op jit(solution)/shard_map/mid/pallas_call | solution.py:462
  43.6 1.8 %collective-permute-done.3.recv = bf16[1024,256]{1,0:T(8,128)(2,1)S(1)} collective-permute-done((bf16[1024,256]{1,0:T(8,128)(2,1)S(1)}, bf16[1024,256]{1,0:T(8,128)(2,1)S(1)}, u32[]{:S(2)}, u32[]{:S(2)}) %collective-permute-start.3) | collective-permute-done | bytes 524320 | tf_op jit(solution)/shard_map/ppermute | solution.py:524
  45.3 12.5 %last.1 = bf16[2048,256]{1,0:T(8,128)(2,1)} custom-call(bf16[1024,256]{1,0:T(8,128)(2,1)S(1)} %get-tuple-element.15.own_a, bf16[1024,256]{1,0:T(8,128)(2,1)S(1)} %get-tuple-element.16.own_b, bf16[1024,256]{1,0:T(8,128)(2,1)S(1)} %collective-permute-done.3.recv, bf16[2048,256]{1,0:T(8,128)(2,1)S(1)} %get-tuple-element.18.sk, ...), custom_call_target="tpu_custom_call" | custom-call | tf_op jit(solution)/shard_map/last/pallas_call | solution.py:462
  (1 shorter events, 0.0 us)
Async XLA Ops:
  0.0 2.5 %copy-start.3 = (s32[1,2048,256]{2,1,0:T(8,128)S(1)}, s32[1,2048,256]{2,1,0:T(8,128)}, u32[]{:S(2)}) copy-start(s32[1,2048,256]{2,1,0:T(8,128)} %param.9) | copy-start | bytes 6291460
  0.0 2.9 %collective-permute-start = (bf16[2048,256]{1,0:T(8,128)(2,1)}, bf16[2048,256]{1,0:T(8,128)(2,1)S(1)}, u32[]{:S(2)}, u32[]{:S(2)}) collective-permute-start(bf16[2048,256]{1,0:T(8,128)(2,1)} %bitcast.8), channel_id=1, source_target_pairs={{0,1},{1,0},{2,3},{3,2},{4,5},{5,4},{6,7},{7,6},{8,9},{9,8},{10,11... | collective-permute-start | bytes 3145736 | tf_op jit(solution)/shard_map/ppermute | solution.py:491
  0.0 2.9 %collective-permute-start.1 = (bf16[64,64]{1,0:T(8,128)(2,1)}, bf16[64,64]{1,0:T(8,128)(2,1)S(1)}, u32[]{:S(2)}, u32[]{:S(2)}) collective-permute-start(bf16[64,64]{1,0:T(8,128)(2,1)} %bitcast.11), channel_id=1, source_target_pairs={{0,1},{1,0},{2,3},{3,2},{4,5},{5,4},{6,7},{7,6},{8,9},{9,8},{10,11... | collective-permute-start | bytes 24584 | tf_op jit(solution)/shard_map/ppermute | solution.py:492
  2.4 1.2 %copy-start = (bf16[1,256,8,256]{3,2,1,0:T(8,128)(2,1)S(1)}, bf16[1,256,8,256]{3,2,1,0:T(8,128)(2,1)}, u32[]{:S(2)}) copy-start(bf16[1,256,8,256]{3,2,1,0:T(8,128)(2,1)} %param.5) | copy-start | bytes 3145732
  2.4 1.2 %copy-start.1 = (bf16[1,64,64]{2,1,0:T(8,128)(2,1)S(1)}, bf16[1,64,64]{2,1,0:T(8,128)(2,1)}, u32[]{:S(2)}) copy-start(bf16[1,64,64]{2,1,0:T(8,128)(2,1)} %param.6) | copy-start | bytes 24580
  2.4 1.2 %copy-start.2 = (bf16[1,64,64]{2,1,0:T(8,128)(2,1)S(1)}, bf16[1,64,64]{2,1,0:T(8,128)(2,1)}, u32[]{:S(2)}) copy-start(bf16[1,64,64]{2,1,0:T(8,128)(2,1)} %param.7) | copy-start | bytes 24580
  2.4 7.7 %collective-permute-start.2 = (bf16[2048,256]{1,0:T(8,128)(2,1)S(1)}, bf16[2048,256]{1,0:T(8,128)(2,1)S(1)}, u32[]{:S(2)}, u32[]{:S(2)}) collective-permute-start(bf16[2048,256]{1,0:T(8,128)(2,1)S(1)} %convert_bitcast_fusion.1.sk_own), channel_id=1, source_target_pairs={{0,1},{1,0},{2,3},{3,2},{4,5},{5,4},{6,7},{7,6},{8,9},{9,8},{10,11... | collective-permute-start | bytes 3145736 | tf_op jit(solution)/shard_map/ppermute | solution.py:494
  9.9 22.7 %collective-permute-start.4 = (bf16[2112,256]{1,0:T(8,128)(2,1)S(1)}, bf16[2112,256]{1,0:T(8,128)(2,1)S(1)}, u32[]{:S(2)}, u32[]{:S(2)}) collective-permute-start(bf16[2112,256]{1,0:T(8,128)(2,1)S(1)} %pad_maximum_fusion.sk_own), channel_id=1, source_target_pairs={{0,127},{1,2},{2,1},{3,4},{4,3},{5,6},{6,5},{7,8},{8,7},{9,10},{10... | collective-permute-start | bytes 3244040 | tf_op jit(solution)/shard_map/ppermute | solution.py:508
  20.5 18.9 %collective-permute-start.5 = (bf16[1024,256]{1,0:T(8,128)(2,1)S(1)}, bf16[1024,256]{1,0:T(8,128)(2,1)S(1)}, u32[]{:S(2)}, u32[]{:S(2)}) collective-permute-start(bf16[1024,256]{1,0:T(8,128)(2,1)S(1)} %get-tuple-element.15.own_a), channel_id=1, source_target_pairs={{0,127},{1,2},{2,1},{3,4},{4,3},{5,6},{6,5},{7,8},{8,7},{9,10},{10... | collective-permute-start | bytes 1572872 | tf_op jit(solution)/shard_map/ppermute | solution.py:523
  32.5 12.8 %collective-permute-start.3 = (bf16[1024,256]{1,0:T(8,128)(2,1)S(1)}, bf16[1024,256]{1,0:T(8,128)(2,1)S(1)}, u32[]{:S(2)}, u32[]{:S(2)}) collective-permute-start(bf16[1024,256]{1,0:T(8,128)(2,1)S(1)} %get-tuple-element.16.own_b), channel_id=1, source_target_pairs={{0,127},{1,2},{2,1},{3,4},{4,3},{5,6},{6,5},{7,8},{8,7},{9,10},{10... | collective-permute-start | bytes 1572872 | tf_op jit(solution)/shard_map/ppermute | solution.py:524

commit v7 on v6

--- a/solution.py
+++ b/solution.py
@@ -226,8 +226,7 @@
     return lax.rem(lax.axis_index("site"), ROW_SITES) == 0
 
 
-def product(left, right, small, m, wts, gate, y, wide):
-    gate[...] = gate_matrix(small[...])
+def product(left, right, y, wts, wide):
     for h in range(2):
         wide[h] = right[:, h * 128 : (h + 1) * 128].astype(F32)
 
@@ -244,29 +243,31 @@
     lax.fori_loop(0, 2, some, 0)
 
 
-def early_kernel(own, recv, gate_own, gate_recv, gate_next, m, gate_rows, wts, gate, y, wide):
+def early_kernel(own, recv, gate_own, gate_recv, gate_next, y, gate, gate_rows, wts, wide):
     gate_rows[...] = jnp.concatenate([gate_next[...]] * 4, axis=1)
 
     @pl.when(waits_long())
     def _():
-        product(own, recv, gate_own, m, wts, gate, y, wide)
-        gated(y, gate, m, ROWS)
-
-
-def late_kernel(m_in, own, recv, gate_own, gate_recv, m, wts, gate, y, wide):
+        gate[...] = gate_matrix(gate_own[...])
+        product(own, recv, y, wts, wide)
+
+
+def late_kernel(y_in, gate_in, own, recv, gate_own, gate_recv, y, gate, m, wts, wide):
     is_left = lax.rem(lax.axis_index("site"), 2) == 0
 
     @pl.when(jnp.logical_not(waits_long()))
     def _():
         @pl.when(is_left)
         def _():
-            product(own, recv, gate_own, m, wts, gate, y, wide)
+            gate[...] = gate_matrix(gate_own[...])
+            product(own, recv, y, wts, wide)
 
         @pl.when(jnp.logical_not(is_left))
         def _():
-            product(recv, own, gate_recv, m, wts, gate, y, wide)
-
-        gated(y, gate, m, ROWS)
+            gate[...] = gate_matrix(gate_recv[...])
+            product(recv, own, y, wts, wide)
+
+    gated(y, gate, m, ROWS)
 
 
 def first_kernel(m, sk_own, sk_recv, out_a, out_b, s, st, wide, q, ab):
@@ -475,27 +476,23 @@
     devices = lax.axis_size("site")
     inside = [(i, i ^ 1) for i in range(devices)]
     across = [(i, (i + 1) % devices if i % 2 else (i - 1) % devices) for i in range(devices)]
-    product_scratch = [
-        pltpu.VMEM((2, HALF, CHI), BF16),
-        pltpu.VMEM((4 * GATE, 4 * GATE), BF16),
-        pltpu.VMEM((CHI, GATE, CHI), BF16),
-        WIDE,
-    ]
+    product_scratch = [pltpu.VMEM((2, HALF, CHI), BF16), WIDE]
     whole_matrix = jax.ShapeDtypeStruct((ROWS, ROWS), BF16)
     half_matrix = jax.ShapeDtypeStruct((HALF, ROWS), BF16)
     whole_array = jax.ShapeDtypeStruct((ROWS, CHI), BF16)
     partial = jax.ShapeDtypeStruct((ROWS, CHI), F32)
     gate_shape = jax.ShapeDtypeStruct((4 * GATE, 4 * GATE), BF16)
     gate_rows_shape = jax.ShapeDtypeStruct((GATE, CHI), BF16)
+    product_shape = jax.ShapeDtypeStruct((CHI, GATE, CHI), BF16)
     own = site_tensors[0].reshape(ROWS, CHI)
     recv = lax.ppermute(own, "site", inside)
     gate_recv = lax.ppermute(first_gates[0], "site", inside)
     sk0 = first_sketch[0].astype(BF16)
     sk0_recv = lax.ppermute(sk0, "site", inside)
-    m, gate_rows = call(
+    y, gate, gate_rows = call(
         early_kernel,
         "early",
-        (whole_matrix, gate_rows_shape),
+        (product_shape, gate_shape, gate_rows_shape),
         product_scratch,
         24,
         own,
@@ -506,18 +503,19 @@
     )
     sk1 = jnp.concatenate([second_sketch[0].astype(BF16), gate_rows], axis=0)
     sk1_recv = lax.ppermute(sk1, "site", across)
-    m = call(
+    _, _, m = call(
         late_kernel,
         "late",
-        whole_matrix,
+        (product_shape, gate_shape, whole_matrix),
         product_scratch,
         24,
-        m,
+        y,
+        gate,
         own,
         recv,
         first_gates[0],
         gate_recv,
-        aliases={0: 0},
+        aliases={0: 0, 1: 1},
     )
     own_a, own_b = call(first_kernel, "first", (HALF_ARRAY, HALF_ARRAY), FACTOR, 24, m, sk0, sk0_recv)
     recv_a = lax.ppermute(own_a, "site", across)

time: 58 us -> 55.1 us (0.950)
  starting transfers between devices: 13 us -> 10 us
    ppermute x1, starting transfers between devices: 12 us -> 6.19 us  [per_device(): recv_a = lax.ppermute(own_a, 'site', across)]
    ppermute x1, starting transfers between devices: 0.24 us -> 3.14 us  [per_device(): sk1_recv = lax.ppermute(sk1, 'site', across)]
  transfers between devices with their start and end apart: 6 -> 6, of which waited for: 3 -> 3; matrix products, arithmetic and copies ran while one was open for 4% -> 4% of each run, Pallas kernels for 36% -> 38%
where the time goes in v7:
time: 55.1 us; the launch traced here: 55 us
  Pallas kernels  33.6 us (61%)
  starting transfers between devices  10 us (18%)
  waiting for transfers between devices  8.35 us (15%)
  other arithmetic  2.12 us (4%)
  local copies, waits for them, and re-layouts  0.74 us (1%)
    pallas_call x6, Pallas kernels, call(): pl.pallas_call(kernel, out_shape=out_shape, in_specs=[VMEM] * len(args),...  33.6 us
    ppermute x1, waiting for transfers between devices, per_device(): recv_a = lax.ppermute(own_a, 'site', across)  6.37 us
    ppermute x1, starting transfers between devices, per_device(): recv_a = lax.ppermute(own_a, 'site', across)  6.19 us
    ppermute x1, starting transfers between devices, per_device(): sk1_recv = lax.ppermute(sk1, 'site', across)  3.14 us
    convert_element_type x1, other arithmetic, per_device(): sk0 = first_sketch[0].astype(BF16)  1.87 us
    ppermute x1, waiting for transfers between devices, per_device(): recv_b = lax.ppermute(own_b, 'site', across)  1.78 us
  transfers between devices with their start and end apart: 6, of which 3 were waited for; matrix products, arithmetic and copies ran while one was open for 4% of the time, Pallas kernels for 38%

profile of v7, /device:TPU:6, one launch (start us, length us, event | category | flops | bytes accessed | tf_op | source)
XLA Modules:
  0.0 55.0 jit_solution(15032257199724871346)
XLA Ops:
  0.0 0.0 copy-start.3
  0.0 0.0 collective-permute-start
  0.0 0.5 collective-permute-start.1
  0.5 1.9 %convert_bitcast_fusion.1.sk_own = bf16[2048,256]{1,0:T(8,128)(2,1)S(1)} fusion(s32[1,2048,256]{2,1,0:T(8,128)} %param.8), kind=kLoop, calls=%fused_computation.2 | loop fusion | flops 524288 | bytes 3145728 | tf_op jit(solution)/shard_map/convert_element_type | solution.py:490
  2.4 0.0 copy-start
  2.4 0.0 copy-start.1
  2.4 0.0 copy-start.2
  2.4 0.1 collective-permute-start.2
  2.5 0.0 copy-done.3
  2.5 0.2 convert_bitcast_fusion
  2.7 0.2 collective-permute-done.1.gate_recv
  2.9 0.0 collective-permute-done.recv
  2.9 0.7 %copy-done = bf16[1,256,8,256]{3,2,1,0:T(8,128)(2,1)S(1)} copy-done((bf16[1,256,8,256]{3,2,1,0:T(8,128)(2,1)S(1)}, bf16[1,256,8,256]{3,2,1,0:T(8,128)(2,1)}, u32[]{:S(2)}) %copy-start) | copy-done | bytes 1048600
  3.6 0.0 copy-done.1
  3.6 0.0 copy-done.2
  3.6 3.3 %early.1 = (bf16[256,64,256]{2,1,0:T(8,128)(2,1)S(1)}, bf16[256,256]{1,0:T(8,128)(2,1)S(1)}, bf16[64,256]{1,0:T(8,128)(2,1)S(1)}) custom-call(bf16[2048,256]{1,0:T(8,128)(2,1)S(1)} %bitcast.9, bf16[2048,256]{1,0:T(8,128)(2,1)S(1)} %collective-permute-done.recv, bf16[64,64]{1,0:T(8,128)(2,1)S(1)} %bitcast.12, ...), custom_call_target="tpu_custom_call" | custom-call | tf_op jit(solution)/shard_map/early/pallas_call | solution.py:463
  6.9 0.1 pad_maximum_fusion.sk_own
  7.0 3.1 %collective-permute-start.4 = (bf16[2112,256]{1,0:T(8,128)(2,1)S(1)}, bf16[2112,256]{1,0:T(8,128)(2,1)S(1)}, u32[]{:S(2)}, u32[]{:S(2)}) collective-permute-start(bf16[2112,256]{1,0:T(8,128)(2,1)S(1)} %pad_maximum_fusion.sk_own), channel_id=1, source_target_pairs={{0,127},{1,2},{2,1},{3,4},{4,3},{5,6},{6,5},{7,8},{8,7},{9,10},{10... | collective-permute-start | bytes 3244040 | tf_op jit(solution)/shard_map/ppermute | solution.py:505
  10.2 2.9 %late.1 = (bf16[256,64,256]{2,1,0:T(8,128)(2,1)S(1)}, bf16[256,256]{1,0:T(8,128)(2,1)S(1)}, bf16[2048,2048]{1,0:T(8,128)(2,1)S(1)}) custom-call(bf16[256,64,256]{2,1,0:T(8,128)(2,1)S(1)} %get-tuple-element.16.y_in, bf16[256,256]{1,0:T(8,128)(2,1)S(1)} %get-tuple-element.17.gate_in, ...), custom_call_target="tpu_custom_call", output_to_operand_aliasing={{0}: (0, {}), {1}: (1, {})} | custom-call | tf_op jit(solution)/shard_map/late/pallas_call | solution.py:463
  13.1 0.0 collective-permute-done.2.sk_recv
  13.1 10.3 %first.1 = (bf16[1024,256]{1,0:T(8,128)(2,1)S(1)}, bf16[1024,256]{1,0:T(8,128)(2,1)S(1)}) custom-call(bf16[2048,2048]{1,0:T(8,128)(2,1)S(1)} %get-tuple-element.18.m, bf16[2048,256]{1,0:T(8,128)(2,1)S(1)} %convert_bitcast_fusion.1.sk_own, bf16[2048,256]{1,0:T(8,128)(2,1)S(1)} %collective-permute-done.2.sk_recv), custom_call_target="tpu_custom_call" | custom-call | tf_op jit(solution)/shard_map/first/pallas_call | solution.py:463
  23.4 6.2 %collective-permute-start.5 = (bf16[1024,256]{1,0:T(8,128)(2,1)S(1)}, bf16[1024,256]{1,0:T(8,128)(2,1)S(1)}, u32[]{:S(2)}, u32[]{:S(2)}) collective-permute-start(bf16[1024,256]{1,0:T(8,128)(2,1)S(1)} %get-tuple-element.19.own_a), channel_id=1, source_target_pairs={{0,127},{1,2},{2,1},{3,4},{4,3},{5,6},{6,5},{7,8},{8,7},{9,10},{10... | collective-permute-start | bytes 1572872 | tf_op jit(solution)/shard_map/ppermute | solution.py:521
  29.6 0.1 collective-permute-start.3
  29.7 0.0 collective-permute-done.4.sk_recv
  29.7 0.4 ready.1
  30.1 6.4 %collective-permute-done.5.recv = bf16[1024,256]{1,0:T(8,128)(2,1)S(1)} collective-permute-done((bf16[1024,256]{1,0:T(8,128)(2,1)S(1)}, bf16[1024,256]{1,0:T(8,128)(2,1)S(1)}, u32[]{:S(2)}, u32[]{:S(2)}) %collective-permute-start.5) | collective-permute-done | bytes 524320 | tf_op jit(solution)/shard_map/ppermute | solution.py:521
  36.5 4.2 %mid.1 = (f32[2048,256]{1,0:T(8,128)S(1)}, bf16[1024,256]{1,0:T(8,128)(2,1)S(1)}, bf16[1024,2048]{1,0:T(8,128)(2,1)S(1)}) custom-call(bf16[1024,256]{1,0:T(8,128)(2,1)S(1)} %get-tuple-element.19.own_a, bf16[1024,256]{1,0:T(8,128)(2,1)S(1)} %get-tuple-element.20.own_b, bf16[1024,256]{1,0:T(8,128)(2,1)S(1)} %collective-permute-done.5.recv, ...), custom_call_target="tpu_custom_call" | custom-call | tf_op jit(solution)/shard_map/mid/pallas_call | solution.py:463
  40.6 1.8 %collective-permute-done.3.recv = bf16[1024,256]{1,0:T(8,128)(2,1)S(1)} collective-permute-done((bf16[1024,256]{1,0:T(8,128)(2,1)S(1)}, bf16[1024,256]{1,0:T(8,128)(2,1)S(1)}, u32[]{:S(2)}, u32[]{:S(2)}) %collective-permute-start.3) | collective-permute-done | bytes 524320 | tf_op jit(solution)/shard_map/ppermute | solution.py:522
  42.4 12.5 %last.1 = bf16[2048,256]{1,0:T(8,128)(2,1)} custom-call(bf16[1024,256]{1,0:T(8,128)(2,1)S(1)} %get-tuple-element.19.own_a, bf16[1024,256]{1,0:T(8,128)(2,1)S(1)} %get-tuple-element.20.own_b, bf16[1024,256]{1,0:T(8,128)(2,1)S(1)} %collective-permute-done.3.recv, bf16[2048,256]{1,0:T(8,128)(2,1)S(1)} %get-tuple-element.22.sk, ...), custom_call_target="tpu_custom_call" | custom-call | tf_op jit(solution)/shard_map/last/pallas_call | solution.py:463
Async XLA Ops:
  0.0 2.5 %copy-start.3 = (s32[1,2048,256]{2,1,0:T(8,128)S(1)}, s32[1,2048,256]{2,1,0:T(8,128)}, u32[]{:S(2)}) copy-start(s32[1,2048,256]{2,1,0:T(8,128)} %param.9) | copy-start | bytes 6291460
  0.0 2.9 %collective-permute-start = (bf16[2048,256]{1,0:T(8,128)(2,1)}, bf16[2048,256]{1,0:T(8,128)(2,1)S(1)}, u32[]{:S(2)}, u32[]{:S(2)}) collective-permute-start(bf16[2048,256]{1,0:T(8,128)(2,1)} %bitcast.8), channel_id=1, source_target_pairs={{0,1},{1,0},{2,3},{3,2},{4,5},{5,4},{6,7},{7,6},{8,9},{9,8},{10,11... | collective-permute-start | bytes 3145736 | tf_op jit(solution)/shard_map/ppermute | solution.py:488
  0.0 2.9 %collective-permute-start.1 = (bf16[64,64]{1,0:T(8,128)(2,1)}, bf16[64,64]{1,0:T(8,128)(2,1)S(1)}, u32[]{:S(2)}, u32[]{:S(2)}) collective-permute-start(bf16[64,64]{1,0:T(8,128)(2,1)} %bitcast.11), channel_id=1, source_target_pairs={{0,1},{1,0},{2,3},{3,2},{4,5},{5,4},{6,7},{7,6},{8,9},{9,8},{10,11... | collective-permute-start | bytes 24584 | tf_op jit(solution)/shard_map/ppermute | solution.py:489
  2.4 1.2 %copy-start = (bf16[1,256,8,256]{3,2,1,0:T(8,128)(2,1)S(1)}, bf16[1,256,8,256]{3,2,1,0:T(8,128)(2,1)}, u32[]{:S(2)}) copy-start(bf16[1,256,8,256]{3,2,1,0:T(8,128)(2,1)} %param.5) | copy-start | bytes 3145732
  2.4 1.2 %copy-start.1 = (bf16[1,64,64]{2,1,0:T(8,128)(2,1)S(1)}, bf16[1,64,64]{2,1,0:T(8,128)(2,1)}, u32[]{:S(2)}) copy-start(bf16[1,64,64]{2,1,0:T(8,128)(2,1)} %param.6) | copy-start | bytes 24580
  2.4 1.2 %copy-start.2 = (bf16[1,64,64]{2,1,0:T(8,128)(2,1)S(1)}, bf16[1,64,64]{2,1,0:T(8,128)(2,1)}, u32[]{:S(2)}) copy-start(bf16[1,64,64]{2,1,0:T(8,128)(2,1)} %param.7) | copy-start | bytes 24580
  2.4 10.6 %collective-permute-start.2 = (bf16[2048,256]{1,0:T(8,128)(2,1)S(1)}, bf16[2048,256]{1,0:T(8,128)(2,1)S(1)}, u32[]{:S(2)}, u32[]{:S(2)}) collective-permute-start(bf16[2048,256]{1,0:T(8,128)(2,1)S(1)} %convert_bitcast_fusion.1.sk_own), channel_id=1, source_target_pairs={{0,1},{1,0},{2,3},{3,2},{4,5},{5,4},{6,7},{7,6},{8,9},{9,8},{10,11... | collective-permute-start | bytes 3145736 | tf_op jit(solution)/shard_map/ppermute | solution.py:491
  7.0 22.7 %collective-permute-start.4 = (bf16[2112,256]{1,0:T(8,128)(2,1)S(1)}, bf16[2112,256]{1,0:T(8,128)(2,1)S(1)}, u32[]{:S(2)}, u32[]{:S(2)}) collective-permute-start(bf16[2112,256]{1,0:T(8,128)(2,1)S(1)} %pad_maximum_fusion.sk_own), channel_id=1, source_target_pairs={{0,127},{1,2},{2,1},{3,4},{4,3},{5,6},{6,5},{7,8},{8,7},{9,10},{10... | collective-permute-start | bytes 3244040 | tf_op jit(solution)/shard_map/ppermute | solution.py:505
  23.4 13.1 %collective-permute-start.5 = (bf16[1024,256]{1,0:T(8,128)(2,1)S(1)}, bf16[1024,256]{1,0:T(8,128)(2,1)S(1)}, u32[]{:S(2)}, u32[]{:S(2)}) collective-permute-start(bf16[1024,256]{1,0:T(8,128)(2,1)S(1)} %get-tuple-element.19.own_a), channel_id=1, source_target_pairs={{0,127},{1,2},{2,1},{3,4},{4,3},{5,6},{6,5},{7,8},{8,7},{9,10},{10... | collective-permute-start | bytes 1572872 | tf_op jit(solution)/shard_map/ppermute | solution.py:521
  29.6 12.8 %collective-permute-start.3 = (bf16[1024,256]{1,0:T(8,128)(2,1)S(1)}, bf16[1024,256]{1,0:T(8,128)(2,1)S(1)}, u32[]{:S(2)}, u32[]{:S(2)}) collective-permute-start(bf16[1024,256]{1,0:T(8,128)(2,1)S(1)} %get-tuple-element.20.own_b), channel_id=1, source_target_pairs={{0,127},{1,2},{2,1},{3,4},{4,3},{5,6},{6,5},{7,8},{8,7},{9,10},{10... | collective-permute-start | bytes 1572872 | tf_op jit(solution)/shard_map/ppermute | solution.py:522

commit v8 on v7

--- a/solution.py
+++ b/solution.py
@@ -136,7 +136,7 @@
 
 
 HALF = ROWS // 2
-ROW_SITES = 8
+ROW_SITES = 32
 BONDS = CHI // 2
 STEP = 512
 
@@ -270,26 +270,24 @@
     gated(y, gate, m, ROWS)
 
 
-def first_kernel(m, sk_own, sk_recv, out_a, out_b, s, st, wide, q, ab):
+def first_kernel(m, sk_own, sk_recv, out_a, out_b, sk, s, st, wide, q, ab):
     is_left = lax.rem(lax.axis_index("site"), 2) == 0
     outs = (out_a, out_b)
 
-    def sample(sketch):
-        def some(i, _):
-            rows = pl.ds(pl.multiple_of(i * HALF, HALF), HALF)
-            s[rows, :] = dot(m[rows, :], sketch[:ROWS, :]).astype(BF16)
-            return 0
-
-        lax.fori_loop(0, 2, some, 0)
-
     @pl.when(is_left)
     def _():
-        sample(sk_own)
+        sk[...] = sk_own[...].astype(F32).astype(BF16)
 
     @pl.when(jnp.logical_not(is_left))
     def _():
-        sample(sk_recv)
-
+        sk[...] = sk_recv[...].astype(F32).astype(BF16)
+
+    def sample(i, _):
+        rows = pl.ds(pl.multiple_of(i * HALF, HALF), HALF)
+        s[rows, :] = dot(m[rows, :], sk[...]).astype(BF16)
+        return 0
+
+    lax.fori_loop(0, 2, sample, 0)
     st[...] = dot(identity(BF16), s[...], ((1,), (1,))).astype(BF16)
     ab[:, :CHI] = dot(st[...], s[...])
 
@@ -487,7 +485,8 @@
     own = site_tensors[0].reshape(ROWS, CHI)
     recv = lax.ppermute(own, "site", inside)
     gate_recv = lax.ppermute(first_gates[0], "site", inside)
-    sk0 = first_sketch[0].astype(BF16)
+    sk1 = second_sketch[0].astype(BF16)
+    sk0, recv, gate_recv, sk1 = lax.optimization_barrier((first_sketch[0], recv, gate_recv, sk1))
     sk0_recv = lax.ppermute(sk0, "site", inside)
     y, gate, gate_rows = call(
         early_kernel,
@@ -501,7 +500,7 @@
         gate_recv,
         second_gates[0],
     )
-    sk1 = jnp.concatenate([second_sketch[0].astype(BF16), gate_rows], axis=0)
+    sk1 = jnp.concatenate([sk1, gate_rows], axis=0)
     sk1_recv = lax.ppermute(sk1, "site", across)
     _, _, m = call(
         late_kernel,
@@ -517,7 +516,7 @@
         gate_recv,
         aliases={0: 0, 1: 1},
     )
-    own_a, own_b = call(first_kernel, "first", (HALF_ARRAY, HALF_ARRAY), FACTOR, 24, m, sk0, sk0_recv)
+    own_a, own_b = call(first_kernel, "first", (HALF_ARRAY, HALF_ARRAY), [WHOLE, *FACTOR], 24, m, sk0, sk0_recv)
     recv_a = lax.ppermute(own_a, "site", across)
     recv_b = lax.ppermute(own_b, "site", across)
     sk, gate = call(ready_kernel, "ready", (whole_array, gate_shape), [], 8, sk1, sk1_recv)

time: 55.1 us -> 56.2 us (1.020)
  local copies, waits for them, and re-layouts: 0.74 us -> 1.52 us
    unnamed x8 -> x9, local copies, waits for them, and re-layouts: 0.74 us -> 1.51 us
    convert_element_type x2 -> x1, other arithmetic: 2.04 us -> 1.96 us  [per_device(): sk1 = second_sketch[0].astype(BF16)]
where the time goes in v8:
time: 56.2 us; the launch traced here: 56 us
  Pallas kernels  33.8 us (60%)
  starting transfers between devices  10.2 us (18%)
  waiting for transfers between devices  8.4 us (15%)
  other arithmetic  1.96 us (3%)
  local copies, waits for them, and re-layouts  1.52 us (3%)
    pallas_call x6, Pallas kernels, call(): pl.pallas_call(kernel, out_shape=out_shape, in_specs=[VMEM] * len(args),...  33.8 us
    ppermute x1, waiting for transfers between devices, per_device(): recv_a = lax.ppermute(own_a, 'site', across)  6.46 us
    ppermute x1, starting transfers between devices, per_device(): recv_a = lax.ppermute(own_a, 'site', across)  5.77 us
    ppermute x1, starting transfers between devices, per_device(): sk1_recv = lax.ppermute(sk1, 'site', across)  3.56 us
    convert_element_type x1, other arithmetic, per_device(): sk1 = second_sketch[0].astype(BF16)  1.96 us
    ppermute x1, waiting for transfers between devices, per_device(): recv_b = lax.ppermute(own_b, 'site', across)  1.51 us
    unnamed x9, local copies, waits for them, and re-layouts  1.51 us
  transfers between devices with their start and end apart: 6, of which 3 were waited for; matrix products, arithmetic and copies ran while one was open for 4% of the time, Pallas kernels for 38%

profile of v8, /device:TPU:6, one launch (start us, length us, event | category | flops | bytes accessed | tf_op | source)
XLA Modules:
  0.0 56.0 jit_solution(7622619005287624602)
XLA Ops:
  0.0 0.0 copy-start
  0.0 0.0 copy-start.1
  0.0 0.0 collective-permute-start
  0.0 0.5 collective-permute-start.1
  0.5 2.0 %convert_bitcast_fusion = bf16[2048,256]{1,0:T(8,128)(2,1)S(1)} fusion(s32[1,2048,256]{2,1,0:T(8,128)} %param.9), kind=kLoop, calls=%fused_computation | loop fusion | flops 524288 | bytes 3145728 | tf_op jit(solution)/shard_map/convert_element_type | solution.py:488
  2.5 0.4 collective-permute-done.1.gate_recv
  2.9 0.0 collective-permute-done.recv
  2.9 0.0 copy-done.1
  2.9 0.1 collective-permute-start.2
  3.0 0.0 copy-done
  3.0 0.0 copy-start.2
  3.0 0.7 %copy-done.2 = bf16[1,64,64]{2,1,0:T(8,128)(2,1)S(1)} copy-done((bf16[1,64,64]{2,1,0:T(8,128)(2,1)S(1)}, bf16[1,64,64]{2,1,0:T(8,128)(2,1)}, u32[]{:S(2)}) %copy-start.2) | copy-done | bytes 8216
  3.8 0.0 copy-start.3
  3.8 0.7 %copy-done.3 = bf16[1,64,64]{2,1,0:T(8,128)(2,1)S(1)} copy-done((bf16[1,64,64]{2,1,0:T(8,128)(2,1)S(1)}, bf16[1,64,64]{2,1,0:T(8,128)(2,1)}, u32[]{:S(2)}) %copy-start.3) | copy-done | bytes 8216
  4.5 3.3 %early.1 = (bf16[256,64,256]{2,1,0:T(8,128)(2,1)S(1)}, bf16[256,256]{1,0:T(8,128)(2,1)S(1)}, bf16[64,256]{1,0:T(8,128)(2,1)S(1)}) custom-call(bf16[2048,256]{1,0:T(8,128)(2,1)S(1)} %bitcast.8, bf16[2048,256]{1,0:T(8,128)(2,1)S(1)} %collective-permute-done.recv, bf16[64,64]{1,0:T(8,128)(2,1)S(1)} %bitcast.13, ...), custom_call_target="tpu_custom_call" | custom-call | tf_op jit(solution)/shard_map/early/pallas_call | solution.py:461
  7.8 0.1 constant_dynamic-update-slice_fusion.1
  7.9 3.6 %collective-permute-start.4 = (bf16[2112,256]{1,0:T(8,128)(2,1)S(1)}, bf16[2112,256]{1,0:T(8,128)(2,1)S(1)}, u32[]{:S(2)}, u32[]{:S(2)}) collective-permute-start(bf16[2112,256]{1,0:T(8,128)(2,1)S(1)} %constant_dynamic-update-slice_fusion.sk_own), channel_id=1, source_target_pairs={{0,127},{1,2},{2,1},{3,4},{4,3},{5,6},{6,5},{7,8},{8,7},{9,10},{10... | collective-permute-start | bytes 3244040 | tf_op jit(solution)/shard_map/ppermute | solution.py:504
  11.5 2.9 %late.1 = (bf16[256,64,256]{2,1,0:T(8,128)(2,1)S(1)}, bf16[256,256]{1,0:T(8,128)(2,1)S(1)}, bf16[2048,2048]{1,0:T(8,128)(2,1)S(1)}) custom-call(bf16[256,64,256]{2,1,0:T(8,128)(2,1)S(1)} %get-tuple-element.22.y_in, bf16[256,256]{1,0:T(8,128)(2,1)S(1)} %get-tuple-element.23.gate_in, ...), custom_call_target="tpu_custom_call", output_to_operand_aliasing={{0}: (0, {}), {1}: (1, {})} | custom-call | tf_op jit(solution)/shard_map/late/pallas_call | solution.py:461
  14.4 0.0 collective-permute-done.2.sk_recv
  14.4 10.4 %first.1 = (bf16[1024,256]{1,0:T(8,128)(2,1)S(1)}, bf16[1024,256]{1,0:T(8,128)(2,1)S(1)}) custom-call(bf16[2048,2048]{1,0:T(8,128)(2,1)S(1)} %get-tuple-element.24.m, s32[2048,256]{1,0:T(8,128)S(1)} %bitcast.11, s32[2048,256]{1,0:T(8,128)S(1)} %collective-permute-done.2.sk_recv), custom_call_target="tpu_custom_call" | custom-call | tf_op jit(solution)/shard_map/first/pallas_call | solution.py:461
  24.8 5.8 %collective-permute-start.5 = (bf16[1024,256]{1,0:T(8,128)(2,1)S(1)}, bf16[1024,256]{1,0:T(8,128)(2,1)S(1)}, u32[]{:S(2)}, u32[]{:S(2)}) collective-permute-start(bf16[1024,256]{1,0:T(8,128)(2,1)S(1)} %get-tuple-element.26.own_a), channel_id=1, source_target_pairs={{0,127},{1,2},{2,1},{3,4},{4,3},{5,6},{6,5},{7,8},{8,7},{9,10},{10... | collective-permute-start | bytes 1572872 | tf_op jit(solution)/shard_map/ppermute | solution.py:520
  30.6 0.3 collective-permute-start.3
  30.9 0.0 collective-permute-done.4.sk_recv
  30.9 0.4 ready.1
  31.3 6.5 %collective-permute-done.5.recv = bf16[1024,256]{1,0:T(8,128)(2,1)S(1)} collective-permute-done((bf16[1024,256]{1,0:T(8,128)(2,1)S(1)}, bf16[1024,256]{1,0:T(8,128)(2,1)S(1)}, u32[]{:S(2)}, u32[]{:S(2)}) %collective-permute-start.5) | collective-permute-done | bytes 524320 | tf_op jit(solution)/shard_map/ppermute | solution.py:520
  37.7 4.2 %mid.1 = (f32[2048,256]{1,0:T(8,128)S(1)}, bf16[1024,256]{1,0:T(8,128)(2,1)S(1)}, bf16[1024,2048]{1,0:T(8,128)(2,1)S(1)}) custom-call(bf16[1024,256]{1,0:T(8,128)(2,1)S(1)} %get-tuple-element.26.own_a, bf16[1024,256]{1,0:T(8,128)(2,1)S(1)} %get-tuple-element.27.own_b, bf16[1024,256]{1,0:T(8,128)(2,1)S(1)} %collective-permute-done.5.recv, ...), custom_call_target="tpu_custom_call" | custom-call | tf_op jit(solution)/shard_map/mid/pallas_call | solution.py:461
  41.9 1.5 %collective-permute-done.3.recv = bf16[1024,256]{1,0:T(8,128)(2,1)S(1)} collective-permute-done((bf16[1024,256]{1,0:T(8,128)(2,1)S(1)}, bf16[1024,256]{1,0:T(8,128)(2,1)S(1)}, u32[]{:S(2)}, u32[]{:S(2)}) %collective-permute-start.3) | collective-permute-done | bytes 524320 | tf_op jit(solution)/shard_map/ppermute | solution.py:521
  43.4 12.5 %last.1 = bf16[2048,256]{1,0:T(8,128)(2,1)} custom-call(bf16[1024,256]{1,0:T(8,128)(2,1)S(1)} %get-tuple-element.26.own_a, bf16[1024,256]{1,0:T(8,128)(2,1)S(1)} %get-tuple-element.27.own_b, bf16[1024,256]{1,0:T(8,128)(2,1)S(1)} %collective-permute-done.3.recv, bf16[2048,256]{1,0:T(8,128)(2,1)S(1)} %get-tuple-element.30.sk, ...), custom_call_target="tpu_custom_call" | custom-call | tf_op jit(solution)/shard_map/last/pallas_call | solution.py:461
  (1 shorter events, 0.0 us)
Async XLA Ops:
  0.0 3.0 %copy-start = (bf16[1,256,8,256]{3,2,1,0:T(8,128)(2,1)S(1)}, bf16[1,256,8,256]{3,2,1,0:T(8,128)(2,1)}, u32[]{:S(2)}) copy-start(bf16[1,256,8,256]{3,2,1,0:T(8,128)(2,1)} %param.5) | copy-start | bytes 3145732
  0.0 2.9 %copy-start.1 = (s32[1,2048,256]{2,1,0:T(8,128)S(1)}, s32[1,2048,256]{2,1,0:T(8,128)}, u32[]{:S(2)}) copy-start(s32[1,2048,256]{2,1,0:T(8,128)} %param.8) | copy-start | bytes 6291460
  0.0 2.9 %collective-permute-start = (bf16[2048,256]{1,0:T(8,128)(2,1)}, bf16[2048,256]{1,0:T(8,128)(2,1)S(1)}, u32[]{:S(2)}, u32[]{:S(2)}) collective-permute-start(bf16[2048,256]{1,0:T(8,128)(2,1)} %bitcast.7), channel_id=1, source_target_pairs={{0,1},{1,0},{2,3},{3,2},{4,5},{5,4},{6,7},{7,6},{8,9},{9,8},{10,11... | collective-permute-start | bytes 3145736 | tf_op jit(solution)/shard_map/ppermute | solution.py:486
  0.0 2.9 %collective-permute-start.1 = (bf16[64,64]{1,0:T(8,128)(2,1)}, bf16[64,64]{1,0:T(8,128)(2,1)S(1)}, u32[]{:S(2)}, u32[]{:S(2)}) collective-permute-start(bf16[64,64]{1,0:T(8,128)(2,1)} %bitcast.12), channel_id=1, source_target_pairs={{0,1},{1,0},{2,3},{3,2},{4,5},{5,4},{6,7},{7,6},{8,9},{9,8},{10,11... | collective-permute-start | bytes 24584 | tf_op jit(solution)/shard_map/ppermute | solution.py:487
  2.9 11.4 %collective-permute-start.2 = (s32[2048,256]{1,0:T(8,128)S(1)}, s32[2048,256]{1,0:T(8,128)S(1)}, u32[]{:S(2)}, u32[]{:S(2)}) collective-permute-start(s32[2048,256]{1,0:T(8,128)S(1)} %bitcast.10), channel_id=1, source_target_pairs={{0,1},{1,0},{2,3},{3,2},{4,5},{5,4},{6,7},{7,6},{8,9},{9,8},{10,11... | collective-permute-start | bytes 6291464 | tf_op jit(solution)/shard_map/ppermute | solution.py:490
  3.0 0.7 %copy-start.2 = (bf16[1,64,64]{2,1,0:T(8,128)(2,1)S(1)}, bf16[1,64,64]{2,1,0:T(8,128)(2,1)}, u32[]{:S(2)}) copy-start(bf16[1,64,64]{2,1,0:T(8,128)(2,1)} %param.6) | copy-start | bytes 24580
  3.8 0.7 %copy-start.3 = (bf16[1,64,64]{2,1,0:T(8,128)(2,1)S(1)}, bf16[1,64,64]{2,1,0:T(8,128)(2,1)}, u32[]{:S(2)}) copy-start(bf16[1,64,64]{2,1,0:T(8,128)(2,1)} %param.7) | copy-start | bytes 24580
  7.9 23.0 %collective-permute-start.4 = (bf16[2112,256]{1,0:T(8,128)(2,1)S(1)}, bf16[2112,256]{1,0:T(8,128)(2,1)S(1)}, u32[]{:S(2)}, u32[]{:S(2)}) collective-permute-start(bf16[2112,256]{1,0:T(8,128)(2,1)S(1)} %constant_dynamic-update-slice_fusion.sk_own), channel_id=1, source_target_pairs={{0,127},{1,2},{2,1},{3,4},{4,3},{5,6},{6,5},{7,8},{8,7},{9,10},{10... | collective-permute-start | bytes 3244040 | tf_op jit(solution)/shard_map/ppermute | solution.py:504
  24.8 12.9 %collective-permute-start.5 = (bf16[1024,256]{1,0:T(8,128)(2,1)S(1)}, bf16[1024,256]{1,0:T(8,128)(2,1)S(1)}, u32[]{:S(2)}, u32[]{:S(2)}) collective-permute-start(bf16[1024,256]{1,0:T(8,128)(2,1)S(1)} %get-tuple-element.26.own_a), channel_id=1, source_target_pairs={{0,127},{1,2},{2,1},{3,4},{4,3},{5,6},{6,5},{7,8},{8,7},{9,10},{10... | collective-permute-start | bytes 1572872 | tf_op jit(solution)/shard_map/ppermute | solution.py:520
  30.6 12.8 %collective-permute-start.3 = (bf16[1024,256]{1,0:T(8,128)(2,1)S(1)}, bf16[1024,256]{1,0:T(8,128)(2,1)S(1)}, u32[]{:S(2)}, u32[]{:S(2)}) collective-permute-start(bf16[1024,256]{1,0:T(8,128)(2,1)S(1)} %get-tuple-element.27.own_b), channel_id=1, source_target_pairs={{0,127},{1,2},{2,1},{3,4},{4,3},{5,6},{6,5},{7,8},{8,7},{9,10},{10... | collective-permute-start | bytes 1572872 | tf_op jit(solution)/shard_map/ppermute | solution.py:521

commit v9 on v7

--- a/solution.py
+++ b/solution.py
@@ -136,7 +136,7 @@
 
 
 HALF = ROWS // 2
-ROW_SITES = 8
+ROW_SITES = 32
 BONDS = CHI // 2
 STEP = 512
 
@@ -243,16 +243,15 @@
     lax.fori_loop(0, 2, some, 0)
 
 
-def early_kernel(own, recv, gate_own, gate_recv, gate_next, y, gate, gate_rows, wts, wide):
+def early_kernel(own, recv, gate_recv, gate_next, y, gate_rows, wts, wide):
     gate_rows[...] = jnp.concatenate([gate_next[...]] * 4, axis=1)
 
     @pl.when(waits_long())
     def _():
-        gate[...] = gate_matrix(gate_own[...])
         product(own, recv, y, wts, wide)
 
 
-def late_kernel(y_in, gate_in, own, recv, gate_own, gate_recv, y, gate, m, wts, wide):
+def late_kernel(y_in, own, recv, gate_own, gate_recv, y, m, gate, wts, wide):
     is_left = lax.rem(lax.axis_index("site"), 2) == 0
 
     @pl.when(jnp.logical_not(waits_long()))
@@ -266,6 +265,10 @@
         def _():
             gate[...] = gate_matrix(gate_recv[...])
             product(recv, own, y, wts, wide)
+
+    @pl.when(waits_long())
+    def _():
+        gate[...] = gate_matrix(gate_own[...])
 
     gated(y, gate, m, ROWS)
 
@@ -489,33 +492,31 @@
     gate_recv = lax.ppermute(first_gates[0], "site", inside)
     sk0 = first_sketch[0].astype(BF16)
     sk0_recv = lax.ppermute(sk0, "site", inside)
-    y, gate, gate_rows = call(
+    y, gate_rows = call(
         early_kernel,
         "early",
-        (product_shape, gate_shape, gate_rows_shape),
+        (product_shape, gate_rows_shape),
         product_scratch,
         24,
         own,
         recv,
-        first_gates[0],
         gate_recv,
         second_gates[0],
     )
     sk1 = jnp.concatenate([second_sketch[0].astype(BF16), gate_rows], axis=0)
     sk1_recv = lax.ppermute(sk1, "site", across)
-    _, _, m = call(
+    _, m = call(
         late_kernel,
         "late",
-        (product_shape, gate_shape, whole_matrix),
-        product_scratch,
+        (product_shape, whole_matrix),
+        [pltpu.VMEM((4 * GATE, 4 * GATE), BF16), *product_scratch],
         24,
         y,
-        gate,
         own,
         recv,
         first_gates[0],
         gate_recv,
-        aliases={0: 0, 1: 1},
+        aliases={0: 0},
     )
     own_a, own_b = call(first_kernel, "first", (HALF_ARRAY, HALF_ARRAY), FACTOR, 24, m, sk0, sk0_recv)
     recv_a = lax.ppermute(own_a, "site", across)

time: 55.1 us -> 55 us (level)
    ppermute x1, starting transfers between devices: 6.19 us -> 5.62 us  [per_device(): recv_a = lax.ppermute(own_a, 'site', across)]
  transfers between devices with their start and end apart: 6 -> 6, of which waited for: 3 -> 3; matrix products, arithmetic and copies ran while one was open for 4% -> 4% of each run, Pallas kernels for 38% -> 39%
where the time goes in v9:
time: 55 us; the launch traced here: 54.8 us
  Pallas kernels  33.7 us (61%)
  starting transfers between devices  10 us (18%)
  waiting for transfers between devices  8.08 us (15%)
  other arithmetic  2.15 us (4%)
  local copies, waits for them, and re-layouts  0.74 us (1%)
    pallas_call x6, Pallas kernels, call(): pl.pallas_call(kernel, out_shape=out_shape, in_specs=[VMEM] * len(args),...  33.7 us
    ppermute x1, waiting for transfers between devices, per_device(): recv_a = lax.ppermute(own_a, 'site', across)  6.46 us
    ppermute x1, starting transfers between devices, per_device(): recv_a = lax.ppermute(own_a, 'site', across)  5.62 us
    ppermute x1, starting transfers between devices, per_device(): sk1_recv = lax.ppermute(sk1, 'site', across)  3.4 us
    convert_element_type x1, other arithmetic, per_device(): sk0 = first_sketch[0].astype(BF16)  1.87 us
    ppermute x1, waiting for transfers between devices, per_device(): recv_b = lax.ppermute(own_b, 'site', across)  1.44 us
  transfers between devices with their start and end apart: 6, of which 3 were waited for; matrix products, arithmetic and copies ran while one was open for 4% of the time, Pallas kernels for 39%

profile of v9, /device:TPU:6, one launch (start us, length us, event | category | flops | bytes accessed | tf_op | source)
XLA Modules:
  0.0 54.8 jit_solution(15610936181654734129)
XLA Ops:
  0.0 0.0 copy-start.3
  0.0 0.0 collective-permute-start
  0.0 0.5 collective-permute-start.1
  0.5 1.9 %convert_bitcast_fusion.1.sk_own = bf16[2048,256]{1,0:T(8,128)(2,1)S(1)} fusion(s32[1,2048,256]{2,1,0:T(8,128)} %param.8), kind=kLoop, calls=%fused_computation.2 | loop fusion | flops 524288 | bytes 3145728 | tf_op jit(solution)/shard_map/convert_element_type | solution.py:493
  2.4 0.0 copy-start
  2.4 0.0 copy-start.1
  2.4 0.1 collective-permute-start.2
  2.5 0.0 copy-done.3
  2.5 0.2 convert_bitcast_fusion
  2.7 0.2 collective-permute-done.1.gate_recv
  2.9 0.0 collective-permute-done.recv
  2.9 0.7 %copy-done = bf16[1,256,8,256]{3,2,1,0:T(8,128)(2,1)S(1)} copy-done((bf16[1,256,8,256]{3,2,1,0:T(8,128)(2,1)S(1)}, bf16[1,256,8,256]{3,2,1,0:T(8,128)(2,1)}, u32[]{:S(2)}) %copy-start) | copy-done | bytes 1048600
  3.6 0.0 copy-done.1
  3.6 0.0 copy-start.2
  3.6 3.1 %early.1 = (bf16[256,64,256]{2,1,0:T(8,128)(2,1)S(1)}, bf16[64,256]{1,0:T(8,128)(2,1)S(1)}) custom-call(bf16[2048,256]{1,0:T(8,128)(2,1)S(1)} %bitcast.9, bf16[2048,256]{1,0:T(8,128)(2,1)S(1)} %collective-permute-done.recv, bf16[64,64]{1,0:T(8,128)(2,1)S(1)} %collective-permute-done.1.gate_recv, bf16[64,64]{1,0:T(8,128)(2,1)S(1)} %bitcast.11), custom_call_target="tpu_custom_call" | custom-call | tf_op jit(solution)/shard_map/early/pallas_call | solution.py:466
  6.7 0.1 pad_maximum_fusion.sk_own
  6.8 3.4 %collective-permute-start.4 = (bf16[2112,256]{1,0:T(8,128)(2,1)S(1)}, bf16[2112,256]{1,0:T(8,128)(2,1)S(1)}, u32[]{:S(2)}, u32[]{:S(2)}) collective-permute-start(bf16[2112,256]{1,0:T(8,128)(2,1)S(1)} %pad_maximum_fusion.sk_own), channel_id=1, source_target_pairs={{0,127},{1,2},{2,1},{3,4},{4,3},{5,6},{6,5},{7,8},{8,7},{9,10},{10... | collective-permute-start | bytes 3244040 | tf_op jit(solution)/shard_map/ppermute | solution.py:507
  10.2 0.0 copy-done.2
  10.2 3.2 %late.1 = (bf16[256,64,256]{2,1,0:T(8,128)(2,1)S(1)}, bf16[2048,2048]{1,0:T(8,128)(2,1)S(1)}) custom-call(bf16[256,64,256]{2,1,0:T(8,128)(2,1)S(1)} %get-tuple-element.15.y_in, bf16[2048,256]{1,0:T(8,128)(2,1)S(1)} %bitcast.10, bf16[2048,256]{1,0:T(8,128)(2,1)S(1)} %collective-permute-done.recv, ...), custom_call_target="tpu_custom_call", output_to_operand_aliasing={{0}: (0, {})} | custom-call | tf_op jit(solution)/shard_map/late/pallas_call | solution.py:466
  13.4 0.0 collective-permute-done.2.sk_recv
  13.4 10.3 %first.1 = (bf16[1024,256]{1,0:T(8,128)(2,1)S(1)}, bf16[1024,256]{1,0:T(8,128)(2,1)S(1)}) custom-call(bf16[2048,2048]{1,0:T(8,128)(2,1)S(1)} %get-tuple-element.16.m, bf16[2048,256]{1,0:T(8,128)(2,1)S(1)} %convert_bitcast_fusion.1.sk_own, bf16[2048,256]{1,0:T(8,128)(2,1)S(1)} %collective-permute-done.2.sk_recv), custom_call_target="tpu_custom_call" | custom-call | tf_op jit(solution)/shard_map/first/pallas_call | solution.py:466
  23.7 5.6 %collective-permute-start.5 = (bf16[1024,256]{1,0:T(8,128)(2,1)S(1)}, bf16[1024,256]{1,0:T(8,128)(2,1)S(1)}, u32[]{:S(2)}, u32[]{:S(2)}) collective-permute-start(bf16[1024,256]{1,0:T(8,128)(2,1)S(1)} %get-tuple-element.17.own_a), channel_id=1, source_target_pairs={{0,127},{1,2},{2,1},{3,4},{4,3},{5,6},{6,5},{7,8},{8,7},{9,10},{10... | collective-permute-start | bytes 1572872 | tf_op jit(solution)/shard_map/ppermute | solution.py:522
  29.4 0.4 collective-permute-start.3
  29.8 0.0 collective-permute-done.4.sk_recv
  29.8 0.4 ready.1
  30.2 6.5 %collective-permute-done.5.recv = bf16[1024,256]{1,0:T(8,128)(2,1)S(1)} collective-permute-done((bf16[1024,256]{1,0:T(8,128)(2,1)S(1)}, bf16[1024,256]{1,0:T(8,128)(2,1)S(1)}, u32[]{:S(2)}, u32[]{:S(2)}) %collective-permute-start.5) | collective-permute-done | bytes 524320 | tf_op jit(solution)/shard_map/ppermute | solution.py:522
  36.6 4.2 %mid.1 = (f32[2048,256]{1,0:T(8,128)S(1)}, bf16[1024,256]{1,0:T(8,128)(2,1)S(1)}, bf16[1024,2048]{1,0:T(8,128)(2,1)S(1)}) custom-call(bf16[1024,256]{1,0:T(8,128)(2,1)S(1)} %get-tuple-element.17.own_a, bf16[1024,256]{1,0:T(8,128)(2,1)S(1)} %get-tuple-element.18.own_b, bf16[1024,256]{1,0:T(8,128)(2,1)S(1)} %collective-permute-done.5.recv, ...), custom_call_target="tpu_custom_call" | custom-call | tf_op jit(solution)/shard_map/mid/pallas_call | solution.py:466
  40.8 1.4 %collective-permute-done.3.recv = bf16[1024,256]{1,0:T(8,128)(2,1)S(1)} collective-permute-done((bf16[1024,256]{1,0:T(8,128)(2,1)S(1)}, bf16[1024,256]{1,0:T(8,128)(2,1)S(1)}, u32[]{:S(2)}, u32[]{:S(2)}) %collective-permute-start.3) | collective-permute-done | bytes 524320 | tf_op jit(solution)/shard_map/ppermute | solution.py:523
  42.3 12.5 %last.1 = bf16[2048,256]{1,0:T(8,128)(2,1)} custom-call(bf16[1024,256]{1,0:T(8,128)(2,1)S(1)} %get-tuple-element.17.own_a, bf16[1024,256]{1,0:T(8,128)(2,1)S(1)} %get-tuple-element.18.own_b, bf16[1024,256]{1,0:T(8,128)(2,1)S(1)} %collective-permute-done.3.recv, bf16[2048,256]{1,0:T(8,128)(2,1)S(1)} %get-tuple-element.20.sk, ...), custom_call_target="tpu_custom_call" | custom-call | tf_op jit(solution)/shard_map/last/pallas_call | solution.py:466
Async XLA Ops:
  0.0 2.5 %copy-start.3 = (s32[1,2048,256]{2,1,0:T(8,128)S(1)}, s32[1,2048,256]{2,1,0:T(8,128)}, u32[]{:S(2)}) copy-start(s32[1,2048,256]{2,1,0:T(8,128)} %param.9) | copy-start | bytes 6291460
  0.0 2.9 %collective-permute-start = (bf16[2048,256]{1,0:T(8,128)(2,1)}, bf16[2048,256]{1,0:T(8,128)(2,1)S(1)}, u32[]{:S(2)}, u32[]{:S(2)}) collective-permute-start(bf16[2048,256]{1,0:T(8,128)(2,1)} %bitcast.8), channel_id=1, source_target_pairs={{0,1},{1,0},{2,3},{3,2},{4,5},{5,4},{6,7},{7,6},{8,9},{9,8},{10,11... | collective-permute-start | bytes 3145736 | tf_op jit(solution)/shard_map/ppermute | solution.py:491
  0.0 2.9 %collective-permute-start.1 = (bf16[64,64]{1,0:T(8,128)(2,1)}, bf16[64,64]{1,0:T(8,128)(2,1)S(1)}, u32[]{:S(2)}, u32[]{:S(2)}) collective-permute-start(bf16[64,64]{1,0:T(8,128)(2,1)} %bitcast.12), channel_id=1, source_target_pairs={{0,1},{1,0},{2,3},{3,2},{4,5},{5,4},{6,7},{7,6},{8,9},{9,8},{10,11... | collective-permute-start | bytes 24584 | tf_op jit(solution)/shard_map/ppermute | solution.py:492
  2.4 1.2 %copy-start = (bf16[1,256,8,256]{3,2,1,0:T(8,128)(2,1)S(1)}, bf16[1,256,8,256]{3,2,1,0:T(8,128)(2,1)}, u32[]{:S(2)}) copy-start(bf16[1,256,8,256]{3,2,1,0:T(8,128)(2,1)} %param.5) | copy-start | bytes 3145732
  2.4 1.2 %copy-start.1 = (bf16[1,64,64]{2,1,0:T(8,128)(2,1)S(1)}, bf16[1,64,64]{2,1,0:T(8,128)(2,1)}, u32[]{:S(2)}) copy-start(bf16[1,64,64]{2,1,0:T(8,128)(2,1)} %param.7) | copy-start | bytes 24580
  2.4 11.0 %collective-permute-start.2 = (bf16[2048,256]{1,0:T(8,128)(2,1)S(1)}, bf16[2048,256]{1,0:T(8,128)(2,1)S(1)}, u32[]{:S(2)}, u32[]{:S(2)}) collective-permute-start(bf16[2048,256]{1,0:T(8,128)(2,1)S(1)} %convert_bitcast_fusion.1.sk_own), channel_id=1, source_target_pairs={{0,1},{1,0},{2,3},{3,2},{4,5},{5,4},{6,7},{7,6},{8,9},{9,8},{10,11... | collective-permute-start | bytes 3145736 | tf_op jit(solution)/shard_map/ppermute | solution.py:494
  3.6 6.6 %copy-start.2 = (bf16[1,64,64]{2,1,0:T(8,128)(2,1)S(1)}, bf16[1,64,64]{2,1,0:T(8,128)(2,1)}, u32[]{:S(2)}) copy-start(bf16[1,64,64]{2,1,0:T(8,128)(2,1)} %param.6) | copy-start | bytes 24580
  6.8 23.0 %collective-permute-start.4 = (bf16[2112,256]{1,0:T(8,128)(2,1)S(1)}, bf16[2112,256]{1,0:T(8,128)(2,1)S(1)}, u32[]{:S(2)}, u32[]{:S(2)}) collective-permute-start(bf16[2112,256]{1,0:T(8,128)(2,1)S(1)} %pad_maximum_fusion.sk_own), channel_id=1, source_target_pairs={{0,127},{1,2},{2,1},{3,4},{4,3},{5,6},{6,5},{7,8},{8,7},{9,10},{10... | collective-permute-start | bytes 3244040 | tf_op jit(solution)/shard_map/ppermute | solution.py:507
  23.7 12.9 %collective-permute-start.5 = (bf16[1024,256]{1,0:T(8,128)(2,1)S(1)}, bf16[1024,256]{1,0:T(8,128)(2,1)S(1)}, u32[]{:S(2)}, u32[]{:S(2)}) collective-permute-start(bf16[1024,256]{1,0:T(8,128)(2,1)S(1)} %get-tuple-element.17.own_a), channel_id=1, source_target_pairs={{0,127},{1,2},{2,1},{3,4},{4,3},{5,6},{6,5},{7,8},{8,7},{9,10},{10... | collective-permute-start | bytes 1572872 | tf_op jit(solution)/shard_map/ppermute | solution.py:522
  29.4 12.9 %collective-permute-start.3 = (bf16[1024,256]{1,0:T(8,128)(2,1)S(1)}, bf16[1024,256]{1,0:T(8,128)(2,1)S(1)}, u32[]{:S(2)}, u32[]{:S(2)}) collective-permute-start(bf16[1024,256]{1,0:T(8,128)(2,1)S(1)} %get-tuple-element.18.own_b), channel_id=1, source_target_pairs={{0,127},{1,2},{2,1},{3,4},{4,3},{5,6},{6,5},{7,8},{8,7},{9,10},{10... | collective-permute-start | bytes 1572872 | tf_op jit(solution)/shard_map/ppermute | solution.py:523
